TPU v7x, 256 devices: a whole 4x4x8 slice. The times are simulated.
256 devices in a mesh: ctx: 64 (over z, y, core), tp: 4 (over x).
Axes of the slice: x: 4, y: 4, z: 8, core: 2. Of those that a mesh axis runs over, the one named last changes fastest.
Arguments:
- queries: bfloat16 [8192, 8192], P('ctx', 'tp'), may hold values from -6 to 6
- rotated_keys: bfloat16 [8192, 1024], P('ctx', 'tp'), may hold values from -6 to 6
- value_vectors: bfloat16 [8192, 1024], P('ctx', 'tp'), may hold values from -6 to 6
- doc_lengths: int32 [64], replicated, may hold values from 1 to 1024, 8192 in all
- owner_lists: int32 [64, 64], replicated, may hold values from 0 to 63, as said below
- out_weight: bfloat16 [4096, 8192], P('ctx', 'tp'), may hold values from -0.0625 to 0.0625
Outputs:
- layer_out: bfloat16 [8192, 4096], P('ctx', 'tp')
Inputs may be any that keep to these rules, and one draw needn't show every extreme that they name: `doc_lengths`: the lengths add up to 8192; the longest is exactly 1024. Each row and each column of owner_lists names every owner index once.
All inputs are finite; a program needn't handle non-finite values.
Results may differ from a plain program's by a relative error of at most 0.015.
Values may be sent and summed in bfloat16 or wider, within the bound.
No kernel may reach another device: no remote copies, remote signals or barrier semaphores. Data moves between devices by JAX's collectives and lax.ppermute only.
A program may use at most 128 MiB of HBM per device.

v0:
```python
import math

import jax
import jax.numpy as jnp
from jax import lax
from jax.sharding import PartitionSpec as P

HEAD_SIZE = 128
DOCCAP = 1024


negative_fill = -1e30


def shifted(value, axis, steps):
    count = lax.axis_size(axis)
    first, last = (max(0, -steps), min(count, count - steps))
    return lax.ppermute(value, axis, [(source, source + steps) for source in range(first, last)])


def doc_index(doc_ends, positions):
    return jnp.sum((doc_ends[None, :] <= positions[:, None]).astype(jnp.int32), axis=1)


def fresh_state(row_count, kv_heads, group_width):
    return (
        jnp.full((kv_heads, group_width, row_count), negative_fill, jnp.float32),
        jnp.zeros((kv_heads, group_width, row_count), jnp.float32),
        jnp.zeros((row_count, kv_heads, group_width, HEAD_SIZE), jnp.float32),
    )


def attend(carry_state, query_rows, query_pos, query_doc, key_rows, value_rows, key_pos, key_doc):
    row_ceiling, row_total, weighted = carry_state
    kv_heads = key_rows.shape[1] // HEAD_SIZE
    group_width = query_rows.shape[1] // HEAD_SIZE // kv_heads
    query_head_rows = query_rows.reshape(query_rows.shape[0], kv_heads, group_width, HEAD_SIZE)
    key_head_rows = key_rows.reshape(key_rows.shape[0], kv_heads, HEAD_SIZE)
    value_head_rows = value_rows.reshape(value_rows.shape[0], kv_heads, HEAD_SIZE)
    scores = jnp.einsum(
        "rkgd,ckd->kgrc", query_head_rows, key_head_rows, preferred_element_type=jnp.float32
    ) * (1.0 / math.sqrt(HEAD_SIZE))
    admitted = (
        (query_doc[:, None] == key_doc[None, :])
        & (key_pos[None, :] <= query_pos[:, None])
        & (key_pos[None, :] >= 0)
    )
    new_top = jnp.maximum(row_ceiling, jnp.max(jnp.where(admitted, scores, negative_fill), axis=3))
    weights = jnp.where(admitted, jnp.exp(scores - new_top[..., None]), 0.0)
    factor = jnp.exp(row_ceiling - new_top)
    row_total = row_total * factor + jnp.sum(weights, axis=3)
    addition = jnp.einsum(
        "kgrc,ckd->rkgd",
        weights.astype(jnp.bfloat16),
        value_head_rows,
        preferred_element_type=jnp.float32,
    )
    weighted = weighted * jnp.transpose(factor, (2, 0, 1))[..., None] + addition
    return (new_top, row_total, weighted)


def finish_rows(carry_state):
    row_ceiling, row_total, weighted = carry_state
    attended = weighted / jnp.transpose(row_total, (2, 0, 1))[..., None]
    return attended.astype(jnp.bfloat16).reshape(weighted.shape[0], -1)


def on_device(queries, rotated_keys, value_vectors, doc_lengths, owner_lists, out_weight):
    ctx_count = lax.axis_size("ctx")
    own_index = lax.axis_index("ctx")
    tok_dev = queries.shape[0]
    row_width = queries.shape[1]
    granule = tok_dev // ctx_count
    kv_heads = rotated_keys.shape[1] // HEAD_SIZE
    group_width = row_width // HEAD_SIZE // kv_heads
    doc_ends = jnp.cumsum(doc_lengths)
    longest = min(DOCCAP, tok_dev * ctx_count // 2)
    reach_count = min(ctx_count - 1, (longest + tok_dev - 2) // tok_dev)
    own_homes = lax.dynamic_index_in_dim(owner_lists, own_index, 0, keepdims=False)
    granule_order = jnp.argsort(own_homes)
    own_pos = own_index * tok_dev + jnp.arange(tok_dev, dtype=jnp.int32)
    own_doc = doc_index(doc_ends, own_pos)
    carry_state = attend(
        fresh_state(tok_dev, kv_heads, group_width),
        queries,
        own_pos,
        own_doc,
        rotated_keys,
        value_vectors,
        own_pos,
        own_doc,
    )
    for step_back in range(1, reach_count + 1):
        earlier_key, earlier_value = shifted((rotated_keys, value_vectors), "ctx", step_back)
        key_pos = own_pos - step_back * tok_dev
        key_doc = doc_index(doc_ends, key_pos)
        reaches = (key_pos[-1] >= 0) & (key_doc[-1] == own_doc[0])
        carry_state = lax.cond(
            reaches,
            lambda carried: attend(
                carried, queries, own_pos, own_doc, earlier_key, earlier_value, key_pos, key_doc
            ),
            lambda carried: carried,
            carry_state,
        )
    local_rows = finish_rows(carry_state)
    grouped = jnp.take(local_rows.reshape(ctx_count, granule, row_width), granule_order, axis=0)
    attended = lax.all_to_all(grouped, "ctx", split_axis=0, concat_axis=0, tiled=True).reshape(
        tok_dev, row_width
    )
    terms = lax.dot_general(
        attended,
        lax.all_gather(out_weight, "ctx", axis=0, tiled=True),
        (((1,), (1,)), ((), ())),
        preferred_element_type=jnp.float32,
    )
    return lax.psum_scatter(terms.astype(jnp.bfloat16), "tp", scatter_dimension=1, tiled=True)


def solution(mesh):
    placed = (P("ctx", "tp"), P("ctx", "tp"), P("ctx", "tp"), P(), P(), P("ctx", "tp"))
    return jax.shard_map(
        on_device, mesh=mesh, in_specs=placed, out_specs=P("ctx", "tp"), check_vma=False
    )
```

profile of v0, /device:TPU:8, one launch (start us, length us, event | category | flops | bytes accessed | tf_op | source)
XLA Modules:
  0.0 185.6 jit_solution(11338475588924673400)
XLA Ops:
  6.5 0.7 all-gather.2.cloned.1.call-update
  7.3 1.9 %collective-permute-start = (bf16[128,256]{1,0:T(8,128)(2,1)}, bf16[128,256]{1,0:T(8,128)(2,1)S(1)}, u32[]{:S(2)}, u32[]{:S(2)}) collective-permute-start(bf16[128,256]{1,0:T(8,128)(2,1)} %param.23), channel_id=1, source_target_pairs={{0,4},{4,8},{8,12},{12,16},{16,20},{20,24},{24,28},{28,32},{32,36}... | collective-permute-start | bytes 196616 | tf_op jit(solution)/shard_map/ppermute | solution.py:18
  9.2 3.5 %collective-permute-start.2 = (bf16[128,256]{1,0:T(8,128)(2,1)}, bf16[128,256]{1,0:T(8,128)(2,1)S(1)}, u32[]{:S(2)}, u32[]{:S(2)}) collective-permute-start(bf16[128,256]{1,0:T(8,128)(2,1)} %param.23), channel_id=1, source_target_pairs={{0,8},{4,12},{8,16},{12,20},{16,24},{20,28},{24,32},{28,36},{32,40... | collective-permute-start | bytes 196616 | tf_op jit(solution)/shard_map/ppermute | solution.py:18
  12.7 3.0 %collective-permute-start.1 = (bf16[128,256]{1,0:T(8,128)(2,1)}, bf16[128,256]{1,0:T(8,128)(2,1)}, u32[]{:S(2)}, u32[]{:S(2)}) collective-permute-start(bf16[128,256]{1,0:T(8,128)(2,1)} %param.24), channel_id=1, source_target_pairs={{0,4},{4,8},{8,12},{12,16},{16,20},{20,24},{24,28},{28,32},{32,36}... | collective-permute-start | bytes 196616 | tf_op jit(solution)/shard_map/ppermute | solution.py:18
  15.8 3.5 %collective-permute-start.3 = (bf16[128,256]{1,0:T(8,128)(2,1)}, bf16[128,256]{1,0:T(8,128)(2,1)S(1)}, u32[]{:S(2)}, u32[]{:S(2)}) collective-permute-start(bf16[128,256]{1,0:T(8,128)(2,1)} %param.24), channel_id=1, source_target_pairs={{0,8},{4,12},{8,16},{12,20},{16,24},{20,28},{24,32},{28,36},{32,40... | collective-permute-start | bytes 196616 | tf_op jit(solution)/shard_map/ppermute | solution.py:18
  19.2 3.1 %collective-permute-start.4 = (bf16[128,256]{1,0:T(8,128)(2,1)}, bf16[128,256]{1,0:T(8,128)(2,1)S(1)}, u32[]{:S(2)}, u32[]{:S(2)}) collective-permute-start(bf16[128,256]{1,0:T(8,128)(2,1)} %param.23), channel_id=1, source_target_pairs={{0,12},{4,16},{8,20},{12,24},{16,28},{20,32},{24,36},{28,40},{32,4... | collective-permute-start | bytes 196616 | tf_op jit(solution)/shard_map/ppermute | solution.py:18
  22.4 0.9 reshape.270
  23.2 0.9 reshape.272
  24.1 0.7 copy.114
  25.1 1.2 copy.191
  27.9 2.0 %sort.17 = (s32[64]{0:T(128)}, s32[64]{0:T(128)S(1)}) sort(s32[64]{0:T(128)S(1)} %dynamic-slice_bitcast_fusion, s32[64]{0:T(128)S(1)} %iota.29), dimensions={0}, to_apply=%region_0.0 | sort | flops 384 | bytes 1024 | tf_op jit(solution)/shard_map/jit(argsort)/sort | solution.py:80
  29.9 3.7 %collective-permute-start.5 = (bf16[128,256]{1,0:T(8,128)(2,1)}, bf16[128,256]{1,0:T(8,128)(2,1)S(1)}, u32[]{:S(2)}, u32[]{:S(2)}) collective-permute-start(bf16[128,256]{1,0:T(8,128)(2,1)} %param.24), channel_id=1, source_target_pairs={{0,12},{4,16},{8,20},{12,24},{16,28},{20,32},{24,36},{28,40},{32,4... | collective-permute-start | bytes 196616 | tf_op jit(solution)/shard_map/ppermute | solution.py:18
  33.6 5.7 %collective-permute-start.6 = (bf16[128,256]{1,0:T(8,128)(2,1)}, bf16[128,256]{1,0:T(8,128)(2,1)S(1)}, u32[]{:S(2)}, u32[]{:S(2)}) collective-permute-start(bf16[128,256]{1,0:T(8,128)(2,1)} %param.23), channel_id=1, source_target_pairs={{0,16},{4,20},{8,24},{12,28},{16,32},{20,36},{24,40},{28,44},{32,4... | collective-permute-start | bytes 196616 | tf_op jit(solution)/shard_map/ppermute | solution.py:18
  39.3 3.0 %collective-permute-start.7 = (bf16[128,256]{1,0:T(8,128)(2,1)}, bf16[128,256]{1,0:T(8,128)(2,1)S(1)}, u32[]{:S(2)}, u32[]{:S(2)}) collective-permute-start(bf16[128,256]{1,0:T(8,128)(2,1)} %param.24), channel_id=1, source_target_pairs={{0,16},{4,20},{8,24},{12,28},{16,32},{20,36},{24,40},{28,44},{32,4... | collective-permute-start | bytes 196616 | tf_op jit(solution)/shard_map/ppermute | solution.py:18
  42.4 4.1 %collective-permute-start.8 = (bf16[128,256]{1,0:T(8,128)(2,1)}, bf16[128,256]{1,0:T(8,128)(2,1)S(1)}, u32[]{:S(2)}, u32[]{:S(2)}) collective-permute-start(bf16[128,256]{1,0:T(8,128)(2,1)} %param.23), channel_id=1, source_target_pairs={{0,20},{4,24},{8,28},{12,32},{16,36},{20,40},{24,44},{28,48},{32,5... | collective-permute-start | bytes 196616 | tf_op jit(solution)/shard_map/ppermute | solution.py:18
  46.6 5.6 %collective-permute-start.9 = (bf16[128,256]{1,0:T(8,128)(2,1)}, bf16[128,256]{1,0:T(8,128)(2,1)S(1)}, u32[]{:S(2)}, u32[]{:S(2)}) collective-permute-start(bf16[128,256]{1,0:T(8,128)(2,1)} %param.24), channel_id=1, source_target_pairs={{0,20},{4,24},{8,28},{12,32},{16,36},{20,40},{24,44},{28,48},{32,5... | collective-permute-start | bytes 196616 | tf_op jit(solution)/shard_map/ppermute | solution.py:18
  52.2 3.7 %collective-permute-start.10 = (bf16[128,256]{1,0:T(8,128)(2,1)}, bf16[128,256]{1,0:T(8,128)(2,1)S(1)}, u32[]{:S(2)}, u32[]{:S(2)}) collective-permute-start(bf16[128,256]{1,0:T(8,128)(2,1)} %param.23), channel_id=1, source_target_pairs={{0,24},{4,28},{8,32},{12,36},{16,40},{20,44},{24,48},{28,52},{32,5... | collective-permute-start | bytes 196616 | tf_op jit(solution)/shard_map/ppermute | solution.py:18
  55.9 0.6 compare_and_fusion
  56.5 0.6 slice.73
  57.1 0.6 slice.71
  57.7 0.6 slice.69
  58.3 0.6 slice.67
  58.9 0.6 slice.65
  59.5 0.7 slice.63
  60.1 0.6 slice.61
  60.7 0.6 slice.58
  61.3 0.6 slice.74
  63.1 0.6 slice.72
  64.9 0.6 slice.70
  66.7 0.6 slice.68
  68.5 0.6 slice.66
  70.3 0.6 slice.64
  72.1 0.7 slice.62
  74.1 0.6 slice.59
  76.0 4.9 %collective-permute-start.11 = (bf16[128,256]{1,0:T(8,128)(2,1)}, bf16[128,256]{1,0:T(8,128)(2,1)}, u32[]{:S(2)}, u32[]{:S(2)}) collective-permute-start(bf16[128,256]{1,0:T(8,128)(2,1)} %param.24), channel_id=1, source_target_pairs={{0,24},{4,28},{8,32},{12,36},{16,40},{20,44},{24,48},{28,52},{32,5... | collective-permute-start | bytes 196616 | tf_op jit(solution)/shard_map/ppermute | solution.py:18
  80.9 1.3 collective-permute-start.12
  82.2 4.8 %collective-permute-start.13 = (bf16[128,256]{1,0:T(8,128)(2,1)}, bf16[128,256]{1,0:T(8,128)(2,1)S(1)}, u32[]{:S(2)}, u32[]{:S(2)}) collective-permute-start(bf16[128,256]{1,0:T(8,128)(2,1)} %param.24), channel_id=1, source_target_pairs={{0,28},{4,32},{8,36},{12,40},{16,44},{20,48},{24,52},{28,56},{32,6... | collective-permute-start | bytes 196616 | tf_op jit(solution)/shard_map/ppermute | solution.py:18
  87.1 1.3 collective-permute-start.14
  88.4 1.7 collective-permute-start.15
  90.2 3.6 %conditional.8 = ((f32[2,8,128]{2,1,0:T(8,128)S(1)}, f32[2,8,128]{2,1,0:T(8,128)S(1)}, f32[128,2,8,128]{3,0,2,1:T(8,128)S(1)})) conditional(s32[]{:T(128)} %bitcast.49, (f32[2,8,128]{2,1,0:T(8,128)S(1)}, f32[2,8,128]{2,1,0:T(8,128)S(1)}, f32[128,2,8,128]{3,0,2,1:T(8,128)S(1)}) %tuple.55, (s32[128]{0:T(128)S(1)}, s32[128]{0:T(128)S(1)}, ...), branch_computations={%region_13.14_spmd, %region_14.17_spmd} | conditional | flops 137173120 | bytes 7408416 | solution.py:98
  90.4 1.2 copy.183
  92.2 0.9 reshape.240
  93.1 0.7 fusion
  94.5 1.5 collective-permute-done.15
  96.8 1.6 gather_fusion
  99.0 44.3 %all_to_all.5 = bf16[64,2,2048]{2,1,0:T(2,128)(2,1)S(1)} all-to-all(bf16[64,2,2048]{2,1,0:T(2,128)(2,1)S(1)} %broadcast_select_fusion), channel_id=1, replica_groups=mesh['ctx'=64,'tp'=4] {'ctx'}, dimensions={0} | all-to-all | bytes 1048576 | tf_op jit(solution)/shard_map/all_to_all | solution.py:108
  143.5 12.4 %convolution_convert_fusion = bf16[128,4096]{1,0:T(8,128)(2,1)} fusion(bf16[128,2048]{1,0:T(8,128)(2,1)S(1)} %reshape.273, bf16[4096,2048]{1,0:T(8,128)(2,1)} %all-gather.2.cloned.1.call-done), kind=kOutput, calls=%fused_computation.161 | convolution fusion | flops 2148007936 | bytes 18350080 | tf_op jit(solution)/shard_map/dot_general | solution.py:111
  156.0 22.8 %reduce-scatter.2.cloned.1.call-done = bf16[128,1024]{1,0:T(8,128)(2,1)} async-done(((bf16[128,4096]{1,0:T(8,128)(2,1)}), bf16[128,1024]{1,0:T(8,128)(2,1)}) %reduce-scatter.2.cloned.1.call-update) | async-done | bytes 262160 | tf_op jit(solution)/shard_map/reduce_scatter | solution.py:117
  (100 shorter events, 4.6 us)
Async XLA Ops:
  6.5 21.3 %copy-start = (s32[64,64]{1,0:T(8,128)S(1)}, s32[64,64]{1,0:T(8,128)}, u32[]{:S(2)}) copy-start(s32[64,64]{1,0:T(8,128)} %param.26) | copy-start | bytes 49156
  6.5 137.0 %all-gather.2.cloned.1.call-start = ((), (), s32[]{:S(2)}) async-start(), calls=%async_computation.2 | async-start | bytes 17039360 | tf_op jit(solution)/shard_map/all_gather | solution.py:113
  7.3 171.5 %reduce-scatter.2.cloned.1.call-start = ((), (), s32[]{:S(2)}) async-start(), calls=%async_computation.3 | async-start | bytes 1310720 | tf_op jit(solution)/shard_map/reduce_scatter | solution.py:117
  7.3 22.6 %collective-permute-start = (bf16[128,256]{1,0:T(8,128)(2,1)}, bf16[128,256]{1,0:T(8,128)(2,1)S(1)}, u32[]{:S(2)}, u32[]{:S(2)}) collective-permute-start(bf16[128,256]{1,0:T(8,128)(2,1)} %param.23), channel_id=1, source_target_pairs={{0,4},{4,8},{8,12},{12,16},{16,20},{20,24},{24,28},{28,32},{32,36}... | collective-permute-start | bytes 196616 | tf_op jit(solution)/shard_map/ppermute | solution.py:18
  9.2 30.1 %collective-permute-start.2 = (bf16[128,256]{1,0:T(8,128)(2,1)}, bf16[128,256]{1,0:T(8,128)(2,1)S(1)}, u32[]{:S(2)}, u32[]{:S(2)}) collective-permute-start(bf16[128,256]{1,0:T(8,128)(2,1)} %param.23), channel_id=1, source_target_pairs={{0,8},{4,12},{8,16},{12,20},{16,24},{20,28},{24,32},{28,36},{32,40... | collective-permute-start | bytes 196616 | tf_op jit(solution)/shard_map/ppermute | solution.py:18
  12.7 20.9 %collective-permute-start.1 = (bf16[128,256]{1,0:T(8,128)(2,1)}, bf16[128,256]{1,0:T(8,128)(2,1)}, u32[]{:S(2)}, u32[]{:S(2)}) collective-permute-start(bf16[128,256]{1,0:T(8,128)(2,1)} %param.24), channel_id=1, source_target_pairs={{0,4},{4,8},{8,12},{12,16},{16,20},{20,24},{24,28},{28,32},{32,36}... | collective-permute-start | bytes 196616 | tf_op jit(solution)/shard_map/ppermute | solution.py:18
  15.8 26.6 %collective-permute-start.3 = (bf16[128,256]{1,0:T(8,128)(2,1)}, bf16[128,256]{1,0:T(8,128)(2,1)S(1)}, u32[]{:S(2)}, u32[]{:S(2)}) collective-permute-start(bf16[128,256]{1,0:T(8,128)(2,1)} %param.24), channel_id=1, source_target_pairs={{0,8},{4,12},{8,16},{12,20},{16,24},{20,28},{24,32},{28,36},{32,40... | collective-permute-start | bytes 196616 | tf_op jit(solution)/shard_map/ppermute | solution.py:18
  19.2 27.3 %collective-permute-start.4 = (bf16[128,256]{1,0:T(8,128)(2,1)}, bf16[128,256]{1,0:T(8,128)(2,1)S(1)}, u32[]{:S(2)}, u32[]{:S(2)}) collective-permute-start(bf16[128,256]{1,0:T(8,128)(2,1)} %param.23), channel_id=1, source_target_pairs={{0,12},{4,16},{8,20},{12,24},{16,28},{20,32},{24,36},{28,40},{32,4... | collective-permute-start | bytes 196616 | tf_op jit(solution)/shard_map/ppermute | solution.py:18
  26.3 60.7 %copy-start.16 = (s32[128]{0:T(128)}, s32[128]{0:T(128)S(1)}, u32[]{:S(2)}) copy-start(s32[128]{0:T(128)S(1)} %broadcast_add_fusion.1) | copy-start | bytes 1540
  26.3 60.7 %copy-start.14 = (s32[128]{0:T(128)}, s32[128]{0:T(128)S(1)}, u32[]{:S(2)}) copy-start(s32[128]{0:T(128)S(1)} %broadcast_add_fusion.2) | copy-start | bytes 1540
  26.3 60.7 %copy-start.12 = (s32[128]{0:T(128)}, s32[128]{0:T(128)S(1)}, u32[]{:S(2)}) copy-start(s32[128]{0:T(128)S(1)} %broadcast_add_fusion.3) | copy-start | bytes 1540
  26.3 60.7 %copy-start.10 = (s32[128]{0:T(128)}, s32[128]{0:T(128)S(1)}, u32[]{:S(2)}) copy-start(s32[128]{0:T(128)S(1)} %broadcast_add_fusion.4) | copy-start | bytes 1540
  26.4 60.7 %copy-start.8 = (s32[128]{0:T(128)}, s32[128]{0:T(128)S(1)}, u32[]{:S(2)}) copy-start(s32[128]{0:T(128)S(1)} %broadcast_add_fusion.5) | copy-start | bytes 1540
  26.4 60.6 %copy-start.4 = (s32[128]{0:T(128)}, s32[128]{0:T(128)S(1)}, u32[]{:S(2)}) copy-start(s32[128]{0:T(128)S(1)} %broadcast_add_fusion.6) | copy-start | bytes 1540
  26.5 60.5 %copy-start.6 = (s32[128]{0:T(128)}, s32[128]{0:T(128)S(1)}, u32[]{:S(2)}) copy-start(s32[128]{0:T(128)S(1)} %get-tuple-element.341) | copy-start | bytes 1540
  26.5 60.5 %copy-start.9 = (s32[128]{0:T(128)}, s32[128]{0:T(128)S(1)}, u32[]{:S(2)}) copy-start(s32[128]{0:T(128)S(1)} %get-tuple-element.342) | copy-start | bytes 1540
  26.6 60.5 %copy-start.11 = (s32[128]{0:T(128)}, s32[128]{0:T(128)S(1)}, u32[]{:S(2)}) copy-start(s32[128]{0:T(128)S(1)} %get-tuple-element.343) | copy-start | bytes 1540
  26.6 60.5 %copy-start.13 = (s32[128]{0:T(128)}, s32[128]{0:T(128)S(1)}, u32[]{:S(2)}) copy-start(s32[128]{0:T(128)S(1)} %get-tuple-element.344) | copy-start | bytes 1540
  26.6 60.5 %copy-start.15 = (s32[128]{0:T(128)}, s32[128]{0:T(128)S(1)}, u32[]{:S(2)}) copy-start(s32[128]{0:T(128)S(1)} %get-tuple-element.345) | copy-start | bytes 1540
  26.6 60.5 %copy-start.17 = (s32[128]{0:T(128)}, s32[128]{0:T(128)S(1)}, u32[]{:S(2)}) copy-start(s32[128]{0:T(128)S(1)} %get-tuple-element.346) | copy-start | bytes 1540
  26.6 61.8 %copy-start.2 = (s32[128]{0:T(128)}, s32[128]{0:T(128)S(1)}, u32[]{:S(2)}) copy-start(s32[128]{0:T(128)S(1)} %get-tuple-element.347) | copy-start | bytes 1540
  29.9 22.2 %collective-permute-start.5 = (bf16[128,256]{1,0:T(8,128)(2,1)}, bf16[128,256]{1,0:T(8,128)(2,1)S(1)}, u32[]{:S(2)}, u32[]{:S(2)}) collective-permute-start(bf16[128,256]{1,0:T(8,128)(2,1)} %param.24), channel_id=1, source_target_pairs={{0,12},{4,16},{8,20},{12,24},{16,28},{20,32},{24,36},{28,40},{32,4... | collective-permute-start | bytes 196616 | tf_op jit(solution)/shard_map/ppermute | solution.py:18
  33.6 42.3 %collective-permute-start.6 = (bf16[128,256]{1,0:T(8,128)(2,1)}, bf16[128,256]{1,0:T(8,128)(2,1)S(1)}, u32[]{:S(2)}, u32[]{:S(2)}) collective-permute-start(bf16[128,256]{1,0:T(8,128)(2,1)} %param.23), channel_id=1, source_target_pairs={{0,16},{4,20},{8,24},{12,28},{16,32},{20,36},{24,40},{28,44},{32,4... | collective-permute-start | bytes 196616 | tf_op jit(solution)/shard_map/ppermute | solution.py:18
  39.3 41.6 %collective-permute-start.7 = (bf16[128,256]{1,0:T(8,128)(2,1)}, bf16[128,256]{1,0:T(8,128)(2,1)S(1)}, u32[]{:S(2)}, u32[]{:S(2)}) collective-permute-start(bf16[128,256]{1,0:T(8,128)(2,1)} %param.24), channel_id=1, source_target_pairs={{0,16},{4,20},{8,24},{12,28},{16,32},{20,36},{24,40},{28,44},{32,4... | collective-permute-start | bytes 196616 | tf_op jit(solution)/shard_map/ppermute | solution.py:18
  42.4 39.8 %collective-permute-start.8 = (bf16[128,256]{1,0:T(8,128)(2,1)}, bf16[128,256]{1,0:T(8,128)(2,1)S(1)}, u32[]{:S(2)}, u32[]{:S(2)}) collective-permute-start(bf16[128,256]{1,0:T(8,128)(2,1)} %param.23), channel_id=1, source_target_pairs={{0,20},{4,24},{8,28},{12,32},{16,36},{20,40},{24,44},{28,48},{32,5... | collective-permute-start | bytes 196616 | tf_op jit(solution)/shard_map/ppermute | solution.py:18
  46.6 40.5 %collective-permute-start.9 = (bf16[128,256]{1,0:T(8,128)(2,1)}, bf16[128,256]{1,0:T(8,128)(2,1)S(1)}, u32[]{:S(2)}, u32[]{:S(2)}) collective-permute-start(bf16[128,256]{1,0:T(8,128)(2,1)} %param.24), channel_id=1, source_target_pairs={{0,20},{4,24},{8,28},{12,32},{16,36},{20,40},{24,44},{28,48},{32,5... | collective-permute-start | bytes 196616 | tf_op jit(solution)/shard_map/ppermute | solution.py:18
  52.1 36.3 %copy-start.1 = (bf16[128,256]{1,0:T(8,128)(2,1)}, bf16[128,256]{1,0:T(8,128)(2,1)S(1)}, u32[]{:S(2)}) copy-start(bf16[128,256]{1,0:T(8,128)(2,1)S(1)} %collective-permute-done.5) | copy-start | bytes 196612
  52.2 36.3 %collective-permute-start.10 = (bf16[128,256]{1,0:T(8,128)(2,1)}, bf16[128,256]{1,0:T(8,128)(2,1)S(1)}, u32[]{:S(2)}, u32[]{:S(2)}) collective-permute-start(bf16[128,256]{1,0:T(8,128)(2,1)} %param.23), channel_id=1, source_target_pairs={{0,24},{4,28},{8,32},{12,36},{16,40},{20,44},{24,48},{28,52},{32,5... | collective-permute-start | bytes 196616 | tf_op jit(solution)/shard_map/ppermute | solution.py:18
  76.0 17.9 %collective-permute-start.11 = (bf16[128,256]{1,0:T(8,128)(2,1)}, bf16[128,256]{1,0:T(8,128)(2,1)}, u32[]{:S(2)}, u32[]{:S(2)}) collective-permute-start(bf16[128,256]{1,0:T(8,128)(2,1)} %param.24), channel_id=1, source_target_pairs={{0,24},{4,28},{8,32},{12,36},{16,40},{20,44},{24,48},{28,52},{32,5... | collective-permute-start | bytes 196616 | tf_op jit(solution)/shard_map/ppermute | solution.py:18
  80.9 13.0 %collective-permute-start.12 = (bf16[128,256]{1,0:T(8,128)(2,1)}, bf16[128,256]{1,0:T(8,128)(2,1)S(1)}, u32[]{:S(2)}, u32[]{:S(2)}) collective-permute-start(bf16[128,256]{1,0:T(8,128)(2,1)} %param.23), channel_id=1, source_target_pairs={{0,28},{4,32},{8,36},{12,40},{16,44},{20,48},{24,52},{28,56},{32,6... | collective-permute-start | bytes 196616 | tf_op jit(solution)/shard_map/ppermute | solution.py:18
  82.2 11.7 %collective-permute-start.13 = (bf16[128,256]{1,0:T(8,128)(2,1)}, bf16[128,256]{1,0:T(8,128)(2,1)S(1)}, u32[]{:S(2)}, u32[]{:S(2)}) collective-permute-start(bf16[128,256]{1,0:T(8,128)(2,1)} %param.24), channel_id=1, source_target_pairs={{0,28},{4,32},{8,36},{12,40},{16,44},{20,48},{24,52},{28,56},{32,6... | collective-permute-start | bytes 196616 | tf_op jit(solution)/shard_map/ppermute | solution.py:18
  87.1 7.4 %collective-permute-start.14 = (bf16[128,256]{1,0:T(8,128)(2,1)}, bf16[128,256]{1,0:T(8,128)(2,1)S(1)}, u32[]{:S(2)}, u32[]{:S(2)}) collective-permute-start(bf16[128,256]{1,0:T(8,128)(2,1)} %param.23), channel_id=1, source_target_pairs={{0,32},{4,36},{8,40},{12,44},{16,48},{20,52},{24,56},{28,60},{32,6... | collective-permute-start | bytes 196616 | tf_op jit(solution)/shard_map/ppermute | solution.py:18
  88.4 7.6 %collective-permute-start.15 = (bf16[128,256]{1,0:T(8,128)(2,1)}, bf16[128,256]{1,0:T(8,128)(2,1)S(1)}, u32[]{:S(2)}, u32[]{:S(2)}) collective-permute-start(bf16[128,256]{1,0:T(8,128)(2,1)} %param.24), channel_id=1, source_target_pairs={{0,32},{4,36},{8,40},{12,44},{16,48},{20,52},{24,56},{28,60},{32,6... | collective-permute-start | bytes 196616 | tf_op jit(solution)/shard_map/ppermute | solution.py:18
  93.8 0.6 copy-start.5
  93.8 0.7 copy-start.7
  93.8 2.2 %copy-start.3 = (s32[128]{0:T(128)S(1)}, s32[128]{0:T(128)}, u32[]{:S(2)}) copy-start(s32[128]{0:T(128)} %copy-done.2) | copy-start | bytes 1540
  93.9 4.6 %copy-start.18 = (pred[64]{0:T(512)(128)(4,1)S(1)}, pred[64]{0:T(512)(128)(4,1)}, u32[]{:S(2)}) copy-start(pred[64]{0:T(512)(128)(4,1)} %compare_and_fusion) | copy-start | bytes 196
Sparse Core Ops, SparseCore 0:
  10.1 105.9 all-gather.1
  156.1 22.6 reduce-scatter.1
where the time goes:
time: 187 us; the launch traced here: 186 us
  starting transfers between devices  54.9 us (29%)
  blocking collectives  44.3 us (24%)
  waiting for transfers between devices  25.1 us (13%)
  between operations  23.9 us (13%)
  local copies, waits for them, and re-layouts  18.4 us (10%)
  matrix products  14.3 us (8%)
  other arithmetic  4.54 us (2%)
    ppermute x16, starting transfers between devices, shifted(): lax.ppermute(value, axis, [(source, source + steps) for source in range(f...  54.9 us
    all_to_all x1, blocking collectives, on_device(): lax.all_to_all(grouped, 'ctx', split_axis=0, concat_axis=0, tiled=True)  44.3 us
    reduce_scatter x1, waiting for transfers between devices, on_device(): lax.psum_scatter(terms.astype(jnp.bfloat16), 'tp', scatter_dimension=1, t...  22.8 us
    dot_general x1, matrix products, on_device(): lax.dot_general(attended, lax.all_gather(out_weight, 'ctx', axis=0, tiled...  12.4 us
    slice x16, local copies, waits for them, and re-layouts, on_device(): reaches = (key_pos[-1] >= 0) & (key_doc[-1] == own_doc[0])  9.67 us
  transfers between devices with their start and end apart: 18, of which 2 were waited for; matrix products, arithmetic and copies ran while one was open for 13% of the time, Pallas kernels for 0%

commit v1 on v0

v1 whole, which is shorter than its diff:
```python
import functools
import math

import jax
import jax.numpy as jnp
from jax import lax
from jax.experimental import pallas as pl
from jax.experimental.pallas import tpu as pltpu
from jax.sharding import Mesh
from jax.sharding import PartitionSpec as P

HEAD = 128
BLOCK = 128
NEG = -1e30
BF16 = jnp.bfloat16
F32 = jnp.float32
NZ, NY, NC = 8, 4, 2
ROW = NY * NC
CTX = NZ * ROW
CHIPS = NZ * NY
REACH = 4


def attend_kernel(place_ref, homes_ref, ends_ref, q_ref, *refs):
    mine, other, out_ref = refs[: REACH + 1], refs[REACH + 1 : 2 * REACH + 2], refs[-1]
    index, core = place_ref[0], place_ref[1]
    rows = lax.broadcasted_iota(jnp.int32, (BLOCK, BLOCK), 0)
    lanes = lax.broadcasted_iota(jnp.int32, (BLOCK, BLOCK), 1)
    chosen = (homes_ref[...] == rows % CTX) & (lanes % 2 == rows // CTX)
    query_pos = index * BLOCK + jnp.sum(jnp.where(chosen, lanes, 0), axis=1, keepdims=True)
    ends = ends_ref[...]
    doc_start = jnp.max(jnp.where(ends <= query_pos, ends, 0), axis=1, keepdims=True)
    queries = jnp.dot(
        jnp.where(chosen, 1.0, 0.0).astype(BF16), q_ref[...], preferred_element_type=F32
    ).astype(BF16)

    parts = [ref[...] for ref in mine]
    starts = [index - 2 * s for s in range(REACH + 1)]
    for s in range(REACH):
        parts.append(jnp.where(core == 0, other[s + 1][...], other[s][...]))
        starts.append(jnp.where(core == 0, index + 1 - 2 * (s + 1), index - 1 - 2 * s))
    lane_row = lax.broadcasted_iota(jnp.int32, (1, BLOCK), 1)
    key_pos = jnp.concatenate([start * BLOCK + lane_row for start in starts], axis=1)
    admitted = (key_pos <= query_pos) & (key_pos >= doc_start)
    bias = jnp.where(admitted, 0.0, NEG)

    kv_heads = parts[0].shape[1] // HEAD // 2
    heads = q_ref.shape[1] // HEAD
    group = heads // kv_heads
    scale = math.log2(math.e) / math.sqrt(HEAD)
    for k in range(kv_heads):
        keys = jnp.concatenate([p[:, k * HEAD : (k + 1) * HEAD] for p in parts], axis=0)
        first = (kv_heads + k) * HEAD
        values = jnp.concatenate([p[:, first : first + HEAD] for p in parts], axis=0)
        step = 2
        for g in range(0, group, step):
            columns = [(k * group + g + n) * HEAD for n in range(step)]
            stacked = jnp.concatenate([queries[:, c : c + HEAD] for c in columns], axis=0)
            scores = lax.dot_general(
                stacked, keys, (((1,), (1,)), ((), ())), preferred_element_type=F32
            )
            scores = scores + jnp.concatenate([bias] * step, axis=0)
            top = jnp.max(scores, axis=1, keepdims=True)
            weights = jnp.exp2((scores - top) * scale)
            total = jnp.sum(weights, axis=1, keepdims=True)
            summed = jnp.dot(weights.astype(BF16), values, preferred_element_type=F32)
            attended = (summed / total).astype(BF16)
            for n, c in enumerate(columns):
                out_ref[:, c : c + HEAD] = attended[n * BLOCK : (n + 1) * BLOCK]


def project_kernel(a_ref, w_ref, o_ref):
    product = lax.dot_general(
        a_ref[...], w_ref[...], (((1,), (1,)), ((), ())), preferred_element_type=F32
    ).astype(BF16)
    for part in range(o_ref.shape[0]):
        o_ref[part] = product[:, part * 128 : (part + 1) * 128]


def reduce_kernel(x_ref, o_ref, total):
    total[...] = functools.reduce(jnp.add, [x_ref[p].astype(F32) for p in range(x_ref.shape[0])])
    for owner in range(CTX):
        o_ref[owner] = total[pl.ds(owner, 16, stride=CTX), :].astype(BF16)


def place_kernel(x_ref, o_ref):
    for z in range(NZ):
        for y in range(NY):
            pair = [x_ref[(z * NY + y) * NC + c].astype(F32) for c in range(NC)]
            for half in range(2):
                joined = jnp.concatenate([p[:, half * 64 : half * 64 + 64] for p in pair], axis=1)
                o_ref[z * 16 : z * 16 + 16, half * 512 + y * 128 : half * 512 + y * 128 + 128] = (
                    joined.astype(BF16)
                )


def call(kernel, out_shape, flops, moved, **kwargs):
    return pl.pallas_call(
        kernel,
        out_shape=out_shape,
        cost_estimate=pl.CostEstimate(flops=flops, bytes_accessed=moved, transcendentals=0),
        compiler_params=pltpu.CompilerParams(vmem_limit_bytes=48 << 20),
        **kwargs,
    )


def chip_shift(value, steps):
    pairs = [
        (chip * NC + core, (chip + steps) * NC + core)
        for chip in range(CHIPS - steps)
        for core in range(NC)
    ]
    return lax.ppermute(value, ("z", "y", "core"), pairs)


def core_swap(value):
    return lax.ppermute(value, "core", [(0, 1), (1, 0)])


def on_device(queries, rotated_keys, value_vectors, doc_lengths, owner_lists, out_weight):
    index = lax.axis_index(("z", "y", "core")).astype(jnp.int32)
    core = lax.axis_index("core").astype(jnp.int32)
    tokens, row_width = queries.shape
    vmem = pl.BlockSpec(memory_space=pltpu.VMEM)
    smem = pl.BlockSpec(memory_space=pltpu.SMEM)

    weight = lax.all_gather(out_weight, "z", axis=0, tiled=True)

    own = jnp.concatenate([rotated_keys, value_vectors], axis=1)
    mine = [own] + [chip_shift(own, s) for s in range(1, REACH + 1)]
    other = [core_swap(v) for v in mine]

    order = jnp.arange(doc_lengths.shape[0])
    ends = jnp.sum(jnp.where(order[None, :] <= order[:, None], doc_lengths[None, :], 0), axis=1)
    ends = jnp.pad(ends, (0, BLOCK - ends.shape[0]), constant_values=1 << 30).reshape(1, BLOCK)
    homes = lax.dynamic_slice_in_dim(owner_lists, index, 1, axis=0)
    homes = jnp.broadcast_to(homes[:, :, None], (1, CTX, tokens // CTX)).reshape(1, tokens)
    place = jnp.stack([index, core])

    attended = call(
        attend_kernel,
        jax.ShapeDtypeStruct(queries.shape, BF16),
        4 * tokens * row_width * 9 * BLOCK,
        10 << 20,
        in_specs=[smem] + [vmem] * (3 + 2 * (REACH + 1)),
        out_specs=vmem,
    )(place, homes.astype(jnp.int32), ends.astype(jnp.int32), queries, *mine, *other)

    rows = lax.all_gather(attended, ("y", "core"), axis=0, tiled=True)
    step = 256
    features = weight.shape[0]
    shares = call(
        project_kernel,
        jax.ShapeDtypeStruct((features // 128, rows.shape[0], 128), BF16),
        2 * rows.shape[0] * features * row_width,
        7 << 20,
        grid=(rows.shape[0] // step,),
        in_specs=[
            pl.BlockSpec((step, row_width), lambda m: (m, 0)),
            pl.BlockSpec((features, row_width), lambda m: (0, 0)),
        ],
        out_specs=pl.BlockSpec((features // 128, step, 128), lambda m: (0, m, 0)),
    )(rows, weight)

    shares = lax.all_to_all(shares, "tp", 0, 0, tiled=True)
    sent = call(
        reduce_kernel,
        jax.ShapeDtypeStruct((CTX, 16, 128), BF16),
        4 << 20,
        2 << 20,
        in_specs=[vmem],
        out_specs=vmem,
        scratch_shapes=[pltpu.VMEM((rows.shape[0], 128), F32)],
    )(shares)
    received = lax.all_to_all(sent, ("z", "y", "core"), 0, 0, tiled=True)
    return call(
        place_kernel,
        jax.ShapeDtypeStruct((tokens, features * 2), BF16),
        1 << 20,
        1 << 19,
        in_specs=[vmem],
        out_specs=vmem,
    )(received)


def solution(mesh):
    split = Mesh(mesh.devices.reshape(NZ, NY, NC, -1), ("z", "y", "core", "tp"))
    ctx = ("z", "y", "core")
    placed = (P(ctx, "tp"), P(ctx, "tp"), P(ctx, "tp"), P(), P(), P(ctx, "tp"))
    return jax.shard_map(
        on_device, mesh=split, in_specs=placed, out_specs=P(ctx, "tp"), check_vma=False
    )
```

time: 187 us -> 148 us (0.79)
  starting transfers between devices: 54.9 us -> 16.6 us
  waiting for transfers between devices: 25.1 us -> 55.7 us
  matrix products: 14.3 us -> 0 us
  local copies, waits for them, and re-layouts: 18.4 us -> 4.55 us
  Pallas kernels: 0 us -> 12.7 us
  between operations: 23.9 us -> 13.5 us
  other arithmetic: 4.54 us -> 0.84 us
  blocking collectives: 44.3 us -> 41.8 us
    all_gather x1 -> x2, waiting for transfers between devices: 0.02 us -> 52.1 us  [the longest x1 36.1 us: on_device(): rows = lax.all_gather(attended, ('y', 'core'), axis=0, tiled=True)]
    ppermute x16 -> x9, starting transfers between devices: 54.9 us -> 16.5 us  [the longest x4 15.8 us: chip_shift(): return lax.ppermute(value, ('z', 'y', 'core'), pairs)]
    reduce_scatter x1 -> x0, waiting for transfers between devices: 22.8 us -> none  [on_device(): lax.psum_scatter(terms.astype(jnp.bfloat16), 'tp', scatter_dimension=1, t...]
    dot_general x5 -> x0, matrix products: 14.3 us -> none  [the longest x1 12.4 us: on_device(): lax.dot_general(attended, lax.all_gather(out_weight, 'ctx', axis=0, tiled...]
    pallas_call x0 -> x4, Pallas kernels: none -> 12.7 us  [the longest x1 6.5 us: on_device(): call(attend_kernel, jax.ShapeDtypeStruct(queries.shape, BF16), 4 * tokens...]
    slice x16 -> x0, local copies, waits for them, and re-layouts: 9.67 us -> none  [on_device(): reaches = (key_pos[-1] >= 0) & (key_doc[-1] == own_doc[0])]
    reshape x5 -> x1, local copies, waits for them, and re-layouts: 2.83 us -> 0.01 us  [on_device(): jnp.pad(ends, (0, BLOCK - ends.shape[0]), constant_values=1 << 30)]
    all_to_all x1 -> x2, blocking collectives: 44.3 us -> 41.8 us  [the longest x1 22.3 us: on_device(): received = lax.all_to_all(sent, ('z', 'y', 'core'), 0, 0, tiled=True)]
  transfers between devices with their start and end apart: 18 -> 11, of which waited for: 2 -> 4; matrix products, arithmetic and copies ran while one was open for 13% -> 2% of each run, Pallas kernels for 0% -> 4%
where the time goes in v1:
time: 148 us; the launch traced here: 146 us
  waiting for transfers between devices  55.7 us (38%)
  blocking collectives  41.8 us (28%)
  starting transfers between devices  16.6 us (11%)
  between operations  13.5 us (9%)
  Pallas kernels  12.7 us (9%)
  local copies, waits for them, and re-layouts  4.55 us (3%)
    all_gather x1, waiting for transfers between devices, on_device(): rows = lax.all_gather(attended, ('y', 'core'), axis=0, tiled=True)  36.1 us
    all_to_all x1, blocking collectives, on_device(): received = lax.all_to_all(sent, ('z', 'y', 'core'), 0, 0, tiled=True)  22.3 us
    all_to_all x1, blocking collectives, on_device(): shares = lax.all_to_all(shares, 'tp', 0, 0, tiled=True)  19.5 us
    all_gather x1, waiting for transfers between devices, on_device(): weight = lax.all_gather(out_weight, 'z', axis=0, tiled=True)  16 us
    ppermute x4, starting transfers between devices, chip_shift(): return lax.ppermute(value, ('z', 'y', 'core'), pairs)  15.8 us
    pallas_call x1, Pallas kernels, on_device(): call(attend_kernel, jax.ShapeDtypeStruct(queries.shape, BF16), 4 * tokens...  6.5 us
    pallas_call x1, Pallas kernels, on_device(): call(project_kernel, jax.ShapeDtypeStruct((features // 128, rows.shape[0]...  4.82 us
    unnamed x7, local copies, waits for them, and re-layouts  3.48 us
  transfers between devices with their start and end apart: 11, of which 4 were waited for; matrix products, arithmetic and copies ran while one was open for 2% of the time, Pallas kernels for 4%

profile of v1, /device:TPU:8, one launch (start us, length us, event | category | flops | bytes accessed | tf_op | source)
XLA Modules:
  0.0 145.7 jit_solution(1202189178548776117)
XLA Ops:
  6.5 0.0 copy-start
  6.5 0.0 all-gather.5.cloned.1.call-start
  6.5 0.7 all-gather.5.cloned.1.call-update
  7.3 0.0 all-gather.3.cloned.1.call-start
  7.3 0.8 constant_dynamic-update-slice_fusion.1
  8.2 0.8 constant_dynamic-update-slice_fusion.refs_0_
  9.0 0.0 collective-permute-start.4
  9.0 3.8 %collective-permute-start.3 = (bf16[128,512]{1,0:T(8,128)(2,1)S(1)}, bf16[128,512]{1,0:T(8,128)(2,1)S(1)}, u32[]{:S(2)}, u32[]{:S(2)}) collective-permute-start(bf16[128,512]{1,0:T(8,128)(2,1)S(1)} %constant_dynamic-update-slice_fusion.refs_0_), channel_id=1, source_target_pairs={{0,32},{4,36},{8,40},{12,44},{16,48},{20,52},{24,56},{28,60},{32,6... | collective-permute-start | bytes 393224 | tf_op jit(solution)/shard_map/ppermute | solution.py:113
  12.8 3.7 %collective-permute-start.2 = (bf16[128,512]{1,0:T(8,128)(2,1)S(1)}, bf16[128,512]{1,0:T(8,128)(2,1)S(1)}, u32[]{:S(2)}, u32[]{:S(2)}) collective-permute-start(bf16[128,512]{1,0:T(8,128)(2,1)S(1)} %constant_dynamic-update-slice_fusion.refs_0_), channel_id=1, source_target_pairs={{0,24},{4,28},{8,32},{12,36},{16,40},{20,44},{24,48},{28,52},{32,5... | collective-permute-start | bytes 393224 | tf_op jit(solution)/shard_map/ppermute | solution.py:113
  16.5 4.5 %collective-permute-start.1 = (bf16[128,512]{1,0:T(8,128)(2,1)S(1)}, bf16[128,512]{1,0:T(8,128)(2,1)S(1)}, u32[]{:S(2)}, u32[]{:S(2)}) collective-permute-start(bf16[128,512]{1,0:T(8,128)(2,1)S(1)} %constant_dynamic-update-slice_fusion.refs_0_), channel_id=1, source_target_pairs={{0,16},{4,20},{8,24},{12,28},{16,32},{20,36},{24,40},{28,44},{32,4... | collective-permute-start | bytes 393224 | tf_op jit(solution)/shard_map/ppermute | solution.py:113
  21.0 3.8 %collective-permute-start = (bf16[128,512]{1,0:T(8,128)(2,1)S(1)}, bf16[128,512]{1,0:T(8,128)(2,1)S(1)}, u32[]{:S(2)}, u32[]{:S(2)}) collective-permute-start(bf16[128,512]{1,0:T(8,128)(2,1)S(1)} %constant_dynamic-update-slice_fusion.refs_0_), channel_id=1, source_target_pairs={{0,8},{4,12},{8,16},{12,20},{16,24},{20,28},{24,32},{28,36},{32,40... | collective-permute-start | bytes 393224 | tf_op jit(solution)/shard_map/ppermute | solution.py:113
  24.8 0.8 select_reduce_fusion
  25.6 0.0 collective-permute-done.3.refs_4_
  25.6 0.1 collective-permute-start.8
  25.7 0.0 collective-permute-done.2.refs_3_
  25.8 0.5 collective-permute-start.7
  26.2 0.0 collective-permute-done.1.refs_2_
  26.3 0.1 collective-permute-start.6
  26.4 1.9 %collective-permute-done.refs_1_ = bf16[128,512]{1,0:T(8,128)(2,1)S(1)} collective-permute-done((bf16[128,512]{1,0:T(8,128)(2,1)S(1)}, bf16[128,512]{1,0:T(8,128)(2,1)S(1)}, u32[]{:S(2)}, u32[]{:S(2)}) %collective-permute-start) | collective-permute-done | bytes 131104 | tf_op jit(solution)/shard_map/ppermute | solution.py:113
  28.2 0.0 collective-permute-start.5
  28.2 0.0 copy-done
  28.2 0.1 broadcast_in_dim.26
  28.3 0.1 broadcast_in_dim.27.homes_ref
  28.4 0.1 pad_add_fusion.place_ref
  28.5 0.0 collective-permute-done.4.refs_5_
  28.5 0.0 collective-permute-done.8.refs_9_
  28.5 0.0 collective-permute-done.7.refs_8_
  28.5 0.0 collective-permute-done.6.refs_7_
  28.5 1.0 collective-permute-done.5.refs_6_
  29.6 0.0 copy-start.2
  29.6 1.0 copy-done.2
  30.6 6.5 %shard_map.64 = bf16[128,2048]{1,0:T(8,128)(2,1)} custom-call(s32[2]{0:T(128)S(1)} %pad_add_fusion.place_ref, s32[1,128]{1,0:T(1,128)S(1)} %broadcast_in_dim.27.homes_ref, s32[1,128]{1,0:T(1,128)S(1)} %pad_bitcast_fusion.ends_ref, bf16[128,2048]{1,0:T(8,128)(2,1)S(1)} %copy-done.2, bf16[128,512]{1,0:T(8,128)(2,1)S(1)} %constant_dynamic-update-slice_fusion.refs_0_, ...), custom_call_target="tpu_custom_call" | custom-call | flops 1207959552 | bytes 10485760 | tf_op jit(solution)/shard_map/pallas_call | solution.py:140
  37.1 0.0 all-gather.3.cloned.1.call-update
  37.1 16.0 %all-gather.5.cloned.1.call-done.w_ref = bf16[512,2048]{1,0:T(8,128)(2,1)} async-done(((bf16[64,2048]{1,0:T(8,128)(2,1)}), bf16[512,2048]{1,0:T(8,128)(2,1)}) %all-gather.5.cloned.1.call-update) | async-done | bytes 2097168 | tf_op jit(solution)/shard_map/all_gather | solution.py:127
  53.1 36.1 %all-gather.3.cloned.1.call-done.a_ref = bf16[1024,2048]{1,0:T(8,128)(2,1)} async-done(((bf16[128,2048]{1,0:T(8,128)(2,1)}), bf16[1024,2048]{1,0:T(8,128)(2,1)}) %all-gather.3.cloned.1.call-update) | async-done | bytes 4194320 | tf_op jit(solution)/shard_map/all_gather | solution.py:149
  89.3 0.0 copy-start.1
  89.3 1.6 %copy-done.1 = bf16[512,2048]{1,0:T(8,128)(2,1)S(1)} copy-done((bf16[512,2048]{1,0:T(8,128)(2,1)S(1)}, bf16[512,2048]{1,0:T(8,128)(2,1)}, u32[]{:S(2)}) %copy-start.1) | copy-done | bytes 2097176
  90.8 4.8 %shard_map.65 = bf16[4,1024,128]{2,1,0:T(8,128)(2,1)S(1)} custom-call(bf16[1024,2048]{1,0:T(8,128)(2,1)} %all-gather.3.cloned.1.call-done.a_ref, bf16[512,2048]{1,0:T(8,128)(2,1)S(1)} %copy-done.1), custom_call_target="tpu_custom_call" | custom-call | flops 2147483648 | bytes 7340032 | tf_op jit(solution)/shard_map/pallas_call | solution.py:152
  95.7 19.5 %all_to_all.10.x_ref = bf16[4,1024,128]{2,1,0:T(8,128)(2,1)S(1)} all-to-all(bf16[4,1024,128]{2,1,0:T(8,128)(2,1)S(1)} %shard_map.65), channel_id=1, replica_groups=mesh['z'=8,'y'=4,'core'=2,'tp'=4] {'tp'}, dimensions={0} | all-to-all | bytes 2097152 | tf_op jit(solution)/shard_map/all_to_all | solution.py:165
  115.2 0.5 shard_map.66
  115.7 22.3 %all_to_all.11.x_ref = bf16[64,16,128]{2,1,0:T(8,128)(2,1)S(1)} all-to-all(bf16[64,16,128]{2,1,0:T(8,128)(2,1)S(1)} %shard_map.66), channel_id=1, replica_groups=mesh['z'=8,'y'=4,'core'=2,'tp'=4] {'z','y','core'}, dimensions={0} | all-to-all | bytes 524288 | tf_op jit(solution)/shard_map/all_to_all | solution.py:175
  138.0 0.8 shard_map.67
  (2 shorter events, 0.0 us)
Async XLA Ops:
  6.5 21.7 %copy-start = (s32[64,64]{1,0:T(8,128)S(1)}, s32[64,64]{1,0:T(8,128)}, u32[]{:S(2)}) copy-start(s32[64,64]{1,0:T(8,128)} %param.10) | copy-start | bytes 49156
  6.5 46.6 %all-gather.5.cloned.1.call-start = ((), (), s32[]{:S(2)}) async-start(), calls=%async_computation.3 | async-start | bytes 2359296 | tf_op jit(solution)/shard_map/all_gather | solution.py:127
  7.3 82.0 %all-gather.3.cloned.1.call-start = ((), (), s32[]{:S(2)}) async-start(), calls=%async_computation.2 | async-start | bytes 4718592 | tf_op jit(solution)/shard_map/all_gather | solution.py:149
  9.0 19.5 %collective-permute-start.4 = (bf16[128,512]{1,0:T(8,128)(2,1)S(1)}, bf16[128,512]{1,0:T(8,128)(2,1)S(1)}, u32[]{:S(2)}, u32[]{:S(2)}) collective-permute-start(bf16[128,512]{1,0:T(8,128)(2,1)S(1)} %constant_dynamic-update-slice_fusion.refs_0_), channel_id=1, source_target_pairs={{0,4},{4,0},{1,5},{5,1},{2,6},{6,2},{3,7},{7,3},{8,12},{12,8},{9,1... | collective-permute-start | bytes 393224 | tf_op jit(solution)/shard_map/ppermute | solution.py:117
  9.0 16.6 %collective-permute-start.3 = (bf16[128,512]{1,0:T(8,128)(2,1)S(1)}, bf16[128,512]{1,0:T(8,128)(2,1)S(1)}, u32[]{:S(2)}, u32[]{:S(2)}) collective-permute-start(bf16[128,512]{1,0:T(8,128)(2,1)S(1)} %constant_dynamic-update-slice_fusion.refs_0_), channel_id=1, source_target_pairs={{0,32},{4,36},{8,40},{12,44},{16,48},{20,52},{24,56},{28,60},{32,6... | collective-permute-start | bytes 393224 | tf_op jit(solution)/shard_map/ppermute | solution.py:113
  12.8 12.9 %collective-permute-start.2 = (bf16[128,512]{1,0:T(8,128)(2,1)S(1)}, bf16[128,512]{1,0:T(8,128)(2,1)S(1)}, u32[]{:S(2)}, u32[]{:S(2)}) collective-permute-start(bf16[128,512]{1,0:T(8,128)(2,1)S(1)} %constant_dynamic-update-slice_fusion.refs_0_), channel_id=1, source_target_pairs={{0,24},{4,28},{8,32},{12,36},{16,40},{20,44},{24,48},{28,52},{32,5... | collective-permute-start | bytes 393224 | tf_op jit(solution)/shard_map/ppermute | solution.py:113
  16.5 9.7 %collective-permute-start.1 = (bf16[128,512]{1,0:T(8,128)(2,1)S(1)}, bf16[128,512]{1,0:T(8,128)(2,1)S(1)}, u32[]{:S(2)}, u32[]{:S(2)}) collective-permute-start(bf16[128,512]{1,0:T(8,128)(2,1)S(1)} %constant_dynamic-update-slice_fusion.refs_0_), channel_id=1, source_target_pairs={{0,16},{4,20},{8,24},{12,28},{16,32},{20,36},{24,40},{28,44},{32,4... | collective-permute-start | bytes 393224 | tf_op jit(solution)/shard_map/ppermute | solution.py:113
  21.0 7.2 %collective-permute-start = (bf16[128,512]{1,0:T(8,128)(2,1)S(1)}, bf16[128,512]{1,0:T(8,128)(2,1)S(1)}, u32[]{:S(2)}, u32[]{:S(2)}) collective-permute-start(bf16[128,512]{1,0:T(8,128)(2,1)S(1)} %constant_dynamic-update-slice_fusion.refs_0_), channel_id=1, source_target_pairs={{0,8},{4,12},{8,16},{12,20},{16,24},{20,28},{24,32},{28,36},{32,40... | collective-permute-start | bytes 393224 | tf_op jit(solution)/shard_map/ppermute | solution.py:113
  25.6 2.9 %collective-permute-start.8 = (bf16[128,512]{1,0:T(8,128)(2,1)S(1)}, bf16[128,512]{1,0:T(8,128)(2,1)S(1)}, u32[]{:S(2)}, u32[]{:S(2)}) collective-permute-start(bf16[128,512]{1,0:T(8,128)(2,1)S(1)} %collective-permute-done.3.refs_4_), channel_id=1, source_target_pairs={{0,4},{4,0},{1,5},{5,1},{2,6},{6,2},{3,7},{7,3},{8,12},{12,8},{9,1... | collective-permute-start | bytes 393224 | tf_op jit(solution)/shard_map/ppermute | solution.py:117
  25.8 2.8 %collective-permute-start.7 = (bf16[128,512]{1,0:T(8,128)(2,1)S(1)}, bf16[128,512]{1,0:T(8,128)(2,1)S(1)}, u32[]{:S(2)}, u32[]{:S(2)}) collective-permute-start(bf16[128,512]{1,0:T(8,128)(2,1)S(1)} %collective-permute-done.2.refs_3_), channel_id=1, source_target_pairs={{0,4},{4,0},{1,5},{5,1},{2,6},{6,2},{3,7},{7,3},{8,12},{12,8},{9,1... | collective-permute-start | bytes 393224 | tf_op jit(solution)/shard_map/ppermute | solution.py:117
  26.3 2.3 %collective-permute-start.6 = (bf16[128,512]{1,0:T(8,128)(2,1)S(1)}, bf16[128,512]{1,0:T(8,128)(2,1)S(1)}, u32[]{:S(2)}, u32[]{:S(2)}) collective-permute-start(bf16[128,512]{1,0:T(8,128)(2,1)S(1)} %collective-permute-done.1.refs_2_), channel_id=1, source_target_pairs={{0,4},{4,0},{1,5},{5,1},{2,6},{6,2},{3,7},{7,3},{8,12},{12,8},{9,1... | collective-permute-start | bytes 393224 | tf_op jit(solution)/shard_map/ppermute | solution.py:117
  28.2 1.3 collective-permute-start.5
  29.6 1.0 copy-start.2
  89.3 1.6 %copy-start.1 = (bf16[512,2048]{1,0:T(8,128)(2,1)S(1)}, bf16[512,2048]{1,0:T(8,128)(2,1)}, u32[]{:S(2)}) copy-start(bf16[512,2048]{1,0:T(8,128)(2,1)} %all-gather.5.cloned.1.call-done.w_ref) | copy-start | bytes 6291460
Sparse Core Ops, SparseCore 0:
  9.1 43.9 all-gather.4
  55.0 34.2 all-gather.2

commit v2 on v1

--- a/solution.py
+++ b/solution.py
@@ -69,16 +69,46 @@
                 out_ref[:, c : c + HEAD] = attended[n * BLOCK : (n + 1) * BLOCK]
 
 
-def project_kernel(a_ref, w_ref, o_ref):
-    product = lax.dot_general(
-        a_ref[...], w_ref[...], (((1,), (1,)), ((), ())), preferred_element_type=F32
-    ).astype(BF16)
-    for part in range(o_ref.shape[0]):
-        o_ref[part] = product[:, part * 128 : (part + 1) * 128]
-
-
-def reduce_kernel(x_ref, o_ref, total):
-    total[...] = functools.reduce(jnp.add, [x_ref[p].astype(F32) for p in range(x_ref.shape[0])])
+def join_kernel(k_ref, v_ref, o_ref):
+    width = k_ref.shape[1]
+    o_ref[:, :width] = k_ref[...]
+    o_ref[:, width:] = v_ref[...]
+
+
+def project_kernel(turn_ref, w_ref, *refs):
+    blocks, outs = refs[:-4], refs[-4:]
+    rows = jnp.concatenate([ref[...] for ref in blocks], axis=0)
+    for pair in range(2):
+        weight = jnp.concatenate(
+            [
+                w_ref[pl.ds(pl.multiple_of(((turn_ref[0] + d) % 4) * 128, 128), 128), :]
+                for d in (2 * pair, 2 * pair + 1)
+            ],
+            axis=0,
+        )
+        product = lax.dot_general(
+            rows, weight, (((1,), (1,)), ((), ())), preferred_element_type=F32
+        )
+        for n in range(2):
+            out = outs[2 * pair + n]
+            out[...] = product[:, n * 128 : (n + 1) * 128].astype(out.dtype)
+
+
+def reduce_kernel(place_ref, *refs):
+    shares, o_ref, total = refs[:-2], refs[-2], refs[-1]
+    y, core = place_ref[0], place_ref[1]
+    sources = [(0, 0), (0, 1), (3, 0), (3, 1), (1, 0), (1, 1), (2, 0), (2, 1)]
+    block = 0
+    for chunk in range(3):
+        own = shares[4 * chunk]
+        summed = own[...]
+        for n in range(1, 4):
+            summed = summed + shares[4 * chunk + n][...].astype(F32)
+        for first in range(0, own.shape[0], BLOCK):
+            dy, dc = sources[block]
+            row = (((y + dy) % NY) * NC + (core + dc) % NC) * BLOCK
+            total[pl.ds(pl.multiple_of(row, BLOCK), BLOCK), :] = summed[first : first + BLOCK]
+            block += 1
     for owner in range(CTX):
         o_ref[owner] = total[pl.ds(owner, 16, stride=CTX), :].astype(BF16)
 
@@ -106,11 +136,16 @@
 
 def chip_shift(value, steps):
     pairs = [
-        (chip * NC + core, (chip + steps) * NC + core)
-        for chip in range(CHIPS - steps)
+        (chip * NC + core, (chip + steps) % CHIPS * NC + core)
+        for chip in range(CHIPS)
         for core in range(NC)
     ]
     return lax.ppermute(value, ("z", "y", "core"), pairs)
+
+
+def ring_shift(value, axis, steps):
+    count = lax.axis_size(axis)
+    return lax.ppermute(value, axis, [(n, (n + steps) % count) for n in range(count)])
 
 
 def core_swap(value):
@@ -126,7 +161,14 @@
 
     weight = lax.all_gather(out_weight, "z", axis=0, tiled=True)
 
-    own = jnp.concatenate([rotated_keys, value_vectors], axis=1)
+    own = call(
+        join_kernel,
+        jax.ShapeDtypeStruct((tokens, 2 * rotated_keys.shape[1]), BF16),
+        0,
+        1 << 18,
+        in_specs=[vmem, vmem],
+        out_specs=vmem,
+    )(rotated_keys, value_vectors)
     mine = [own] + [chip_shift(own, s) for s in range(1, REACH + 1)]
     other = [core_swap(v) for v in mine]
 
@@ -146,32 +188,38 @@
         out_specs=vmem,
     )(place, homes.astype(jnp.int32), ends.astype(jnp.int32), queries, *mine, *other)
 
-    rows = lax.all_gather(attended, ("y", "core"), axis=0, tiled=True)
-    step = 256
+    turn = lax.axis_index("tp").astype(jnp.int32).reshape(1)
     features = weight.shape[0]
-    shares = call(
-        project_kernel,
-        jax.ShapeDtypeStruct((features // 128, rows.shape[0], 128), BF16),
-        2 * rows.shape[0] * features * row_width,
-        7 << 20,
-        grid=(rows.shape[0] // step,),
-        in_specs=[
-            pl.BlockSpec((step, row_width), lambda m: (m, 0)),
-            pl.BlockSpec((features, row_width), lambda m: (0, 0)),
-        ],
-        out_specs=pl.BlockSpec((features // 128, step, 128), lambda m: (0, m, 0)),
-    )(rows, weight)
-
-    shares = lax.all_to_all(shares, "tp", 0, 0, tiled=True)
+
+    def project(blocks):
+        rows = sum(block.shape[0] for block in blocks)
+        shape = (rows, 128)
+        shares = call(
+            project_kernel,
+            [jax.ShapeDtypeStruct(shape, F32)] + [jax.ShapeDtypeStruct(shape, BF16)] * 3,
+            2 * rows * features * row_width,
+            (2 << 20) + rows * (2 * row_width + 1280),
+            in_specs=[smem] + [vmem] * (1 + len(blocks)),
+            out_specs=[vmem] * 4,
+        )(turn, weight, *blocks)
+        return [shares[0]] + [ring_shift(shares[d], "tp", d) for d in (1, 3, 2)]
+
+    half = tokens // 2
+    below, above = ring_shift(attended, "y", 1), ring_shift(attended, "y", -1)
+    shares = project([attended, core_swap(attended)])
+    far = [ring_shift(below[:half], "y", 1), ring_shift(above[half:], "y", -1)]
+    shares += project([below, core_swap(below), above, core_swap(above)])
+    shares += project(far + [core_swap(v) for v in far])
+
     sent = call(
         reduce_kernel,
         jax.ShapeDtypeStruct((CTX, 16, 128), BF16),
         4 << 20,
         2 << 20,
-        in_specs=[vmem],
-        out_specs=vmem,
-        scratch_shapes=[pltpu.VMEM((rows.shape[0], 128), F32)],
-    )(shares)
+        in_specs=[smem] + [vmem] * 12,
+        out_specs=vmem,
+        scratch_shapes=[pltpu.VMEM((ROW * tokens, 128), F32)],
+    )(jnp.stack([lax.axis_index("y").astype(jnp.int32), core]), *shares)
     received = lax.all_to_all(sent, ("z", "y", "core"), 0, 0, tiled=True)
     return call(
         place_kernel,

time: 148 us -> 116 us (0.78)
  waiting for transfers between devices: 55.7 us -> 29.8 us
  blocking collectives: 41.8 us -> 24.7 us
  starting transfers between devices: 16.6 us -> 29.2 us
    all_gather x1 -> x0, waiting for transfers between devices: 36.1 us -> none  [on_device(): rows = lax.all_gather(attended, ('y', 'core'), axis=0, tiled=True)]
    ppermute x0 -> x13, waiting for transfers between devices: none -> 22 us  [ring_shift(): lax.ppermute(value, axis, [(n, (n + steps) % count) for n in range(count)])]
    all_to_all x1 -> x0, blocking collectives: 19.5 us -> none  [on_device(): shares = lax.all_to_all(shares, 'tp', 0, 0, tiled=True)]
    ppermute x0 -> x13, starting transfers between devices: none -> 19.2 us  [ring_shift(): lax.ppermute(value, axis, [(n, (n + steps) % count) for n in range(count)])]
    all_gather x1, waiting for transfers between devices: 16 us -> 0.01 us  [on_device(): weight = lax.all_gather(out_weight, 'z', axis=0, tiled=True)]
    ppermute x4, starting transfers between devices: 15.8 us -> 8.27 us  [chip_shift(): return lax.ppermute(value, ('z', 'y', 'core'), pairs)]
    ppermute x4, waiting for transfers between devices: 1.86 us -> 6.26 us  [chip_shift(): return lax.ppermute(value, ('z', 'y', 'core'), pairs)]
    all_to_all x1, blocking collectives: 22.3 us -> 24.7 us  [on_device(): received = lax.all_to_all(sent, ('z', 'y', 'core'), 0, 0, tiled=True)]
  transfers between devices with their start and end apart: 11 -> 28, of which waited for: 4 -> 10; matrix products, arithmetic and copies ran while one was open for 2% -> 1% of each run, Pallas kernels for 4% -> 8%
where the time goes in v2:
time: 116 us; the launch traced here: 114 us
  waiting for transfers between devices  29.8 us (26%)
  starting transfers between devices  29.2 us (25%)
  blocking collectives  24.7 us (21%)
  between operations  13.5 us (12%)
  Pallas kernels  11.4 us (10%)
  local copies, waits for them, and re-layouts  4.57 us (4%)
    all_to_all x1, blocking collectives, on_device(): received = lax.all_to_all(sent, ('z', 'y', 'core'), 0, 0, tiled=True)  24.7 us
    ppermute x13, waiting for transfers between devices, ring_shift(): lax.ppermute(value, axis, [(n, (n + steps) % count) for n in range(count)])  22 us
    ppermute x13, starting transfers between devices, ring_shift(): lax.ppermute(value, axis, [(n, (n + steps) % count) for n in range(count)])  19.2 us
    ppermute x4, starting transfers between devices, chip_shift(): return lax.ppermute(value, ('z', 'y', 'core'), pairs)  8.27 us
    ppermute x4, waiting for transfers between devices, chip_shift(): return lax.ppermute(value, ('z', 'y', 'core'), pairs)  6.26 us
    pallas_call x1, Pallas kernels, on_device(): call(attend_kernel, jax.ShapeDtypeStruct(queries.shape, BF16), 4 * tokens...  5.68 us
    unnamed x12, local copies, waits for them, and re-layouts  4.31 us
    pallas_call x3, Pallas kernels, project(): call(project_kernel, [jax.ShapeDtypeStruct(shape, F32)] + [jax.ShapeDtype...  3.87 us
  transfers between devices with their start and end apart: 28, of which 10 were waited for; matrix products, arithmetic and copies ran while one was open for 1% of the time, Pallas kernels for 8%

profile of v2, /device:TPU:8, one launch (start us, length us, event | category | flops | bytes accessed | tf_op | source)
XLA Modules:
  0.0 114.1 jit_solution(17153532498017418230)
XLA Ops:
  6.5 0.7 all-gather.2.cloned.1.call-update
  7.3 0.8 copy-done.3
  8.1 0.8 copy-done.4
  9.0 1.7 %collective-permute-start = (bf16[128,512]{1,0:T(8,128)(2,1)S(1)}, bf16[128,512]{1,0:T(8,128)(2,1)S(1)}, u32[]{:S(2)}, u32[]{:S(2)}) collective-permute-start(bf16[128,512]{1,0:T(8,128)(2,1)S(1)} %shard_map.64.refs_0_), channel_id=1, source_target_pairs={{0,8},{4,12},{8,16},{12,20},{16,24},{20,28},{24,32},{28,36},{32,40... | collective-permute-start | bytes 393224 | tf_op jit(solution)/shard_map/ppermute | solution.py:143
  10.6 2.3 %collective-permute-start.1 = (bf16[128,512]{1,0:T(8,128)(2,1)S(1)}, bf16[128,512]{1,0:T(8,128)(2,1)S(1)}, u32[]{:S(2)}, u32[]{:S(2)}) collective-permute-start(bf16[128,512]{1,0:T(8,128)(2,1)S(1)} %shard_map.64.refs_0_), channel_id=1, source_target_pairs={{0,16},{4,20},{8,24},{12,28},{16,32},{20,36},{24,40},{28,44},{32,4... | collective-permute-start | bytes 393224 | tf_op jit(solution)/shard_map/ppermute | solution.py:143
  12.9 2.4 %collective-permute-start.2 = (bf16[128,512]{1,0:T(8,128)(2,1)S(1)}, bf16[128,512]{1,0:T(8,128)(2,1)S(1)}, u32[]{:S(2)}, u32[]{:S(2)}) collective-permute-start(bf16[128,512]{1,0:T(8,128)(2,1)S(1)} %shard_map.64.refs_0_), channel_id=1, source_target_pairs={{0,24},{4,28},{8,32},{12,36},{16,40},{20,44},{24,48},{28,52},{32,5... | collective-permute-start | bytes 393224 | tf_op jit(solution)/shard_map/ppermute | solution.py:143
  15.3 1.9 %collective-permute-start.3 = (bf16[128,512]{1,0:T(8,128)(2,1)S(1)}, bf16[128,512]{1,0:T(8,128)(2,1)S(1)}, u32[]{:S(2)}, u32[]{:S(2)}) collective-permute-start(bf16[128,512]{1,0:T(8,128)(2,1)S(1)} %shard_map.64.refs_0_), channel_id=1, source_target_pairs={{0,32},{4,36},{8,40},{12,44},{16,48},{20,52},{24,56},{28,60},{32,6... | collective-permute-start | bytes 393224 | tf_op jit(solution)/shard_map/ppermute | solution.py:143
  17.2 0.8 select_reduce_fusion
  18.0 0.6 collective-permute-start.5
  18.6 6.0 %collective-permute-done.1.refs_2_ = bf16[128,512]{1,0:T(8,128)(2,1)S(1)} collective-permute-done((bf16[128,512]{1,0:T(8,128)(2,1)S(1)}, bf16[128,512]{1,0:T(8,128)(2,1)S(1)}, u32[]{:S(2)}, u32[]{:S(2)}) %collective-permute-start.1) | collective-permute-done | bytes 131104 | tf_op jit(solution)/shard_map/ppermute | solution.py:143
  24.6 0.3 collective-permute-done.2.refs_3_
  24.9 0.2 collective-permute-start.7
  25.1 0.3 collective-permute-start.8
  25.4 0.1 broadcast_in_dim.26
  25.5 0.1 broadcast_in_dim.27.homes_ref
  25.6 0.1 pad_add_fusion.1.place_ref
  25.7 0.2 collective-permute-done.6.refs_7_
  25.9 0.3 collective-permute-done.7.refs_8_
  26.2 0.2 collective-permute-done.8.refs_9_
  26.5 1.0 copy-done.5
  27.5 5.7 %shard_map.65.refs_0_ = bf16[128,2048]{1,0:T(8,128)(2,1)S(1)} custom-call(s32[2]{0:T(128)S(1)} %pad_add_fusion.1.place_ref, s32[1,128]{1,0:T(1,128)S(1)} %broadcast_in_dim.27.homes_ref, s32[1,128]{1,0:T(1,128)S(1)} %pad_bitcast_fusion.ends_ref, bf16[128,2048]{1,0:T(8,128)(2,1)S(1)} %copy-done.5, bf16[128,512]{1,0:T(8,128)(2,1)S(1)} %shard_map.64.refs_0_, ...), custom_call_target="tpu_custom_call" | custom-call | flops 1207959552 | bytes 10485760 | tf_op jit(solution)/shard_map/pallas_call | solution.py:182
  33.2 2.3 %collective-permute-start.13 = (bf16[128,2048]{1,0:T(8,128)(2,1)S(1)}, bf16[128,2048]{1,0:T(8,128)(2,1)S(1)}, u32[]{:S(2)}, u32[]{:S(2)}) collective-permute-start(bf16[128,2048]{1,0:T(8,128)(2,1)S(1)} %shard_map.65.refs_0_), channel_id=1, source_target_pairs={{0,8},{8,16},{16,24},{24,0},{1,9},{9,17},{17,25},{25,1},{2,10},{10... | collective-permute-start | bytes 1572872 | tf_op jit(solution)/shard_map/ppermute | solution.py:148
  35.5 0.1 collective-permute-start.9
  35.6 11.9 %collective-permute-done.13.refs_0_ = bf16[128,2048]{1,0:T(8,128)(2,1)S(1)} collective-permute-done((bf16[128,2048]{1,0:T(8,128)(2,1)S(1)}, bf16[128,2048]{1,0:T(8,128)(2,1)S(1)}, u32[]{:S(2)}, u32[]{:S(2)}) %collective-permute-start.13) | collective-permute-done | bytes 524320 | tf_op jit(solution)/shard_map/ppermute | solution.py:148
  47.4 2.3 %collective-permute-start.20 = (bf16[64,2048]{1,0:T(8,128)(2,1)S(1)}, bf16[64,2048]{1,0:T(8,128)(2,1)S(1)}, u32[]{:S(2)}, u32[]{:S(2)}) collective-permute-start(bf16[64,2048]{1,0:T(8,128)(2,1)S(1)} %slice.8), channel_id=1, source_target_pairs={{0,8},{8,16},{16,24},{24,0},{1,9},{9,17},{17,25},{25,1},{2,10},{10... | collective-permute-start | bytes 786440 | tf_op jit(solution)/shard_map/ppermute | solution.py:148
  49.8 1.1 collective-permute-start.21
  50.9 0.5 collective-permute-start.16
  51.4 5.6 %collective-permute-done.20.refs_0_ = bf16[64,2048]{1,0:T(8,128)(2,1)S(1)} collective-permute-done((bf16[64,2048]{1,0:T(8,128)(2,1)S(1)}, bf16[64,2048]{1,0:T(8,128)(2,1)S(1)}, u32[]{:S(2)}, u32[]{:S(2)}) %collective-permute-start.20) | collective-permute-done | bytes 262176 | tf_op jit(solution)/shard_map/ppermute | solution.py:148
  57.0 0.7 collective-permute-done.21.refs_1_
  57.8 1.6 %copy-done.1 = bf16[512,2048]{1,0:T(8,128)(2,1)S(1)} copy-done((bf16[512,2048]{1,0:T(8,128)(2,1)S(1)}, bf16[512,2048]{1,0:T(8,128)(2,1)}, u32[]{:S(2)}) %copy-start.1) | copy-done | bytes 2097176
  59.3 0.7 shard_map.66
  60.1 1.6 %collective-permute-start.10 = (bf16[256,128]{1,0:T(8,128)(2,1)S(1)}, bf16[256,128]{1,0:T(8,128)(2,1)S(1)}, u32[]{:S(2)}, u32[]{:S(2)}) collective-permute-start(bf16[256,128]{1,0:T(8,128)(2,1)S(1)} %get-tuple-element.18), channel_id=1, source_target_pairs={{0,1},{1,2},{2,3},{3,0},{4,5},{5,6},{6,7},{7,4},{8,9},{9,10},{10,1... | collective-permute-start | bytes 196616 | tf_op jit(solution)/shard_map/ppermute | solution.py:148
  61.7 1.7 %collective-permute-start.11 = (bf16[256,128]{1,0:T(8,128)(2,1)S(1)}, bf16[256,128]{1,0:T(8,128)(2,1)S(1)}, u32[]{:S(2)}, u32[]{:S(2)}) collective-permute-start(bf16[256,128]{1,0:T(8,128)(2,1)S(1)} %get-tuple-element.19), channel_id=1, source_target_pairs={{0,3},{1,0},{2,1},{3,2},{4,7},{5,4},{6,5},{7,6},{8,11},{9,8},{10,9... | collective-permute-start | bytes 196616 | tf_op jit(solution)/shard_map/ppermute | solution.py:148
  63.4 1.9 %collective-permute-start.12 = (bf16[256,128]{1,0:T(8,128)(2,1)S(1)}, bf16[256,128]{1,0:T(8,128)(2,1)S(1)}, u32[]{:S(2)}, u32[]{:S(2)}) collective-permute-start(bf16[256,128]{1,0:T(8,128)(2,1)S(1)} %get-tuple-element.20), channel_id=1, source_target_pairs={{0,2},{1,3},{2,0},{3,1},{4,6},{5,7},{6,4},{7,5},{8,10},{9,11},{10,... | collective-permute-start | bytes 196616 | tf_op jit(solution)/shard_map/ppermute | solution.py:148
  65.3 1.8 %shard_map.68 = (f32[256,128]{1,0:T(8,128)S(1)}, bf16[256,128]{1,0:T(8,128)(2,1)S(1)}, bf16[256,128]{1,0:T(8,128)(2,1)S(1)}, bf16[256,128]{1,0:T(8,128)(2,1)S(1)}) custom-call(s32[1]{0:T(128)} %bitcast.2.turn_ref, bf16[512,2048]{1,0:T(8,128)(2,1)S(1)} %copy-done.2, bf16[64,2048]{1,0:T(8,128)(2,1)S(1)} %collective-permute-done.20.refs_0_, ...), custom_call_target="tpu_custom_call" | custom-call | flops 536870912 | bytes 3473408 | tf_op jit(solution)/shard_map/pallas_call | solution.py:197
  67.2 0.7 collective-permute-start.24
  67.8 1.3 %shard_map.67 = (f32[512,128]{1,0:T(8,128)S(1)}, bf16[512,128]{1,0:T(8,128)(2,1)S(1)}, bf16[512,128]{1,0:T(8,128)(2,1)S(1)}, bf16[512,128]{1,0:T(8,128)(2,1)S(1)}) custom-call(s32[1]{0:T(128)} %bitcast.2.turn_ref, bf16[512,2048]{1,0:T(8,128)(2,1)S(1)} %copy-done.2, bf16[128,2048]{1,0:T(8,128)(2,1)S(1)} %collective-permute-done.13.refs_0_, ...), custom_call_target="tpu_custom_call" | custom-call | flops 1073741824 | bytes 4849664 | tf_op jit(solution)/shard_map/pallas_call | solution.py:197
  69.1 1.1 collective-permute-start.17
  70.2 2.2 %collective-permute-start.18 = (bf16[512,128]{1,0:T(8,128)(2,1)S(1)}, bf16[512,128]{1,0:T(8,128)(2,1)S(1)}, u32[]{:S(2)}, u32[]{:S(2)}) collective-permute-start(bf16[512,128]{1,0:T(8,128)(2,1)S(1)} %get-tuple-element.23), channel_id=1, source_target_pairs={{0,3},{1,0},{2,1},{3,2},{4,7},{5,4},{6,5},{7,6},{8,11},{9,8},{10,9... | collective-permute-start | bytes 393224 | tf_op jit(solution)/shard_map/ppermute | solution.py:148
  72.5 0.9 collective-permute-start.19
  73.4 1.5 %collective-permute-start.25 = (bf16[256,128]{1,0:T(8,128)(2,1)S(1)}, bf16[256,128]{1,0:T(8,128)(2,1)S(1)}, u32[]{:S(2)}, u32[]{:S(2)}) collective-permute-start(bf16[256,128]{1,0:T(8,128)(2,1)S(1)} %get-tuple-element.27), channel_id=1, source_target_pairs={{0,3},{1,0},{2,1},{3,2},{4,7},{5,4},{6,5},{7,6},{8,11},{9,8},{10,9... | collective-permute-start | bytes 196616 | tf_op jit(solution)/shard_map/ppermute | solution.py:148
  74.9 1.9 %collective-permute-start.26 = (bf16[256,128]{1,0:T(8,128)(2,1)S(1)}, bf16[256,128]{1,0:T(8,128)(2,1)S(1)}, u32[]{:S(2)}, u32[]{:S(2)}) collective-permute-start(bf16[256,128]{1,0:T(8,128)(2,1)S(1)} %get-tuple-element.28), channel_id=1, source_target_pairs={{0,2},{1,3},{2,0},{3,1},{4,6},{5,7},{6,4},{7,5},{8,10},{9,11},{10,... | collective-permute-start | bytes 196616 | tf_op jit(solution)/shard_map/ppermute | solution.py:148
  76.8 0.1 pad_add_fusion.place_ref
  76.9 3.5 %collective-permute-done.25.refs_10_ = bf16[256,128]{1,0:T(8,128)(2,1)S(1)} collective-permute-done((bf16[256,128]{1,0:T(8,128)(2,1)S(1)}, bf16[256,128]{1,0:T(8,128)(2,1)S(1)}, u32[]{:S(2)}, u32[]{:S(2)}) %collective-permute-start.25) | collective-permute-done | bytes 65568 | tf_op jit(solution)/shard_map/ppermute | solution.py:148
  80.4 0.3 collective-permute-done.26.refs_11_
  80.7 1.0 shard_map.69
  81.7 24.7 %all_to_all.5.x_ref = bf16[64,16,128]{2,1,0:T(8,128)(2,1)S(1)} all-to-all(bf16[64,16,128]{2,1,0:T(8,128)(2,1)S(1)} %shard_map.69), channel_id=1, replica_groups=mesh['z'=8,'y'=4,'core'=2,'tp'=4] {'z','y','core'}, dimensions={0} | all-to-all | bytes 524288 | tf_op jit(solution)/shard_map/all_to_all | solution.py:223
  106.4 0.8 shard_map.70
  (38 shorter events, 0.2 us)
Async XLA Ops:
  6.5 18.9 %copy-start = (s32[64,64]{1,0:T(8,128)S(1)}, s32[64,64]{1,0:T(8,128)}, u32[]{:S(2)}) copy-start(s32[64,64]{1,0:T(8,128)} %param.10) | copy-start | bytes 49156
  6.5 51.2 %all-gather.2.cloned.1.call-start = ((), (), s32[]{:S(2)}) async-start(), calls=%async_computation.1 | async-start | bytes 2359296 | tf_op jit(solution)/shard_map/all_gather | solution.py:162
  7.3 0.8 copy-start.3
  8.1 0.8 copy-start.4
  9.0 9.1 %collective-permute-start = (bf16[128,512]{1,0:T(8,128)(2,1)S(1)}, bf16[128,512]{1,0:T(8,128)(2,1)S(1)}, u32[]{:S(2)}, u32[]{:S(2)}) collective-permute-start(bf16[128,512]{1,0:T(8,128)(2,1)S(1)} %shard_map.64.refs_0_), channel_id=1, source_target_pairs={{0,8},{4,12},{8,16},{12,20},{16,24},{20,28},{24,32},{28,36},{32,40... | collective-permute-start | bytes 393224 | tf_op jit(solution)/shard_map/ppermute | solution.py:143
  10.6 14.0 %collective-permute-start.1 = (bf16[128,512]{1,0:T(8,128)(2,1)S(1)}, bf16[128,512]{1,0:T(8,128)(2,1)S(1)}, u32[]{:S(2)}, u32[]{:S(2)}) collective-permute-start(bf16[128,512]{1,0:T(8,128)(2,1)S(1)} %shard_map.64.refs_0_), channel_id=1, source_target_pairs={{0,16},{4,20},{8,24},{12,28},{16,32},{20,36},{24,40},{28,44},{32,4... | collective-permute-start | bytes 393224 | tf_op jit(solution)/shard_map/ppermute | solution.py:143
  12.9 12.0 %collective-permute-start.2 = (bf16[128,512]{1,0:T(8,128)(2,1)S(1)}, bf16[128,512]{1,0:T(8,128)(2,1)S(1)}, u32[]{:S(2)}, u32[]{:S(2)}) collective-permute-start(bf16[128,512]{1,0:T(8,128)(2,1)S(1)} %shard_map.64.refs_0_), channel_id=1, source_target_pairs={{0,24},{4,28},{8,32},{12,36},{16,40},{20,44},{24,48},{28,52},{32,5... | collective-permute-start | bytes 393224 | tf_op jit(solution)/shard_map/ppermute | solution.py:143
  15.3 9.8 %collective-permute-start.3 = (bf16[128,512]{1,0:T(8,128)(2,1)S(1)}, bf16[128,512]{1,0:T(8,128)(2,1)S(1)}, u32[]{:S(2)}, u32[]{:S(2)}) collective-permute-start(bf16[128,512]{1,0:T(8,128)(2,1)S(1)} %shard_map.64.refs_0_), channel_id=1, source_target_pairs={{0,32},{4,36},{8,40},{12,44},{16,48},{20,52},{24,56},{28,60},{32,6... | collective-permute-start | bytes 393224 | tf_op jit(solution)/shard_map/ppermute | solution.py:143
  17.2 8.5 %collective-permute-start.4 = (bf16[128,512]{1,0:T(8,128)(2,1)S(1)}, bf16[128,512]{1,0:T(8,128)(2,1)S(1)}, u32[]{:S(2)}, u32[]{:S(2)}) collective-permute-start(bf16[128,512]{1,0:T(8,128)(2,1)S(1)} %shard_map.64.refs_0_), channel_id=1, source_target_pairs={{0,4},{4,0},{1,5},{5,1},{2,6},{6,2},{3,7},{7,3},{8,12},{12,8},{9,1... | collective-permute-start | bytes 393224 | tf_op jit(solution)/shard_map/ppermute | solution.py:152
  18.0 7.7 %collective-permute-start.5 = (bf16[128,512]{1,0:T(8,128)(2,1)S(1)}, bf16[128,512]{1,0:T(8,128)(2,1)S(1)}, u32[]{:S(2)}, u32[]{:S(2)}) collective-permute-start(bf16[128,512]{1,0:T(8,128)(2,1)S(1)} %collective-permute-done.refs_1_), channel_id=1, source_target_pairs={{0,4},{4,0},{1,5},{5,1},{2,6},{6,2},{3,7},{7,3},{8,12},{12,8},{9,1... | collective-permute-start | bytes 393224 | tf_op jit(solution)/shard_map/ppermute | solution.py:152
  24.6 1.3 %collective-permute-start.6 = (bf16[128,512]{1,0:T(8,128)(2,1)S(1)}, bf16[128,512]{1,0:T(8,128)(2,1)S(1)}, u32[]{:S(2)}, u32[]{:S(2)}) collective-permute-start(bf16[128,512]{1,0:T(8,128)(2,1)S(1)} %collective-permute-done.1.refs_2_), channel_id=1, source_target_pairs={{0,4},{4,0},{1,5},{5,1},{2,6},{6,2},{3,7},{7,3},{8,12},{12,8},{9,1... | collective-permute-start | bytes 393224 | tf_op jit(solution)/shard_map/ppermute | solution.py:152
  24.9 1.3 %collective-permute-start.7 = (bf16[128,512]{1,0:T(8,128)(2,1)S(1)}, bf16[128,512]{1,0:T(8,128)(2,1)S(1)}, u32[]{:S(2)}, u32[]{:S(2)}) collective-permute-start(bf16[128,512]{1,0:T(8,128)(2,1)S(1)} %collective-permute-done.2.refs_3_), channel_id=1, source_target_pairs={{0,4},{4,0},{1,5},{5,1},{2,6},{6,2},{3,7},{7,3},{8,12},{12,8},{9,1... | collective-permute-start | bytes 393224 | tf_op jit(solution)/shard_map/ppermute | solution.py:152
  25.1 1.3 %collective-permute-start.8 = (bf16[128,512]{1,0:T(8,128)(2,1)S(1)}, bf16[128,512]{1,0:T(8,128)(2,1)S(1)}, u32[]{:S(2)}, u32[]{:S(2)}) collective-permute-start(bf16[128,512]{1,0:T(8,128)(2,1)S(1)} %collective-permute-done.3.refs_4_), channel_id=1, source_target_pairs={{0,4},{4,0},{1,5},{5,1},{2,6},{6,2},{3,7},{7,3},{8,12},{12,8},{9,1... | collective-permute-start | bytes 393224 | tf_op jit(solution)/shard_map/ppermute | solution.py:152
  26.5 1.0 copy-start.5
  33.2 14.2 %collective-permute-start.13 = (bf16[128,2048]{1,0:T(8,128)(2,1)S(1)}, bf16[128,2048]{1,0:T(8,128)(2,1)S(1)}, u32[]{:S(2)}, u32[]{:S(2)}) collective-permute-start(bf16[128,2048]{1,0:T(8,128)(2,1)S(1)} %shard_map.65.refs_0_), channel_id=1, source_target_pairs={{0,8},{8,16},{16,24},{24,0},{1,9},{9,17},{17,25},{25,1},{2,10},{10... | collective-permute-start | bytes 1572872 | tf_op jit(solution)/shard_map/ppermute | solution.py:148
  35.5 14.3 %collective-permute-start.15 = (bf16[128,2048]{1,0:T(8,128)(2,1)S(1)}, bf16[128,2048]{1,0:T(8,128)(2,1)S(1)}, u32[]{:S(2)}, u32[]{:S(2)}) collective-permute-start(bf16[128,2048]{1,0:T(8,128)(2,1)S(1)} %shard_map.65.refs_0_), channel_id=1, source_target_pairs={{0,24},{8,0},{16,8},{24,16},{1,25},{9,1},{17,9},{25,17},{2,26},{10... | collective-permute-start | bytes 1572872 | tf_op jit(solution)/shard_map/ppermute | solution.py:148
  35.5 22.2 %collective-permute-start.9 = (bf16[128,2048]{1,0:T(8,128)(2,1)S(1)}, bf16[128,2048]{1,0:T(8,128)(2,1)S(1)}, u32[]{:S(2)}, u32[]{:S(2)}) collective-permute-start(bf16[128,2048]{1,0:T(8,128)(2,1)S(1)} %shard_map.65.refs_0_), channel_id=1, source_target_pairs={{0,4},{4,0},{1,5},{5,1},{2,6},{6,2},{3,7},{7,3},{8,12},{12,8},{9,1... | collective-permute-start | bytes 1572872 | tf_op jit(solution)/shard_map/ppermute | solution.py:152
  47.4 9.5 %collective-permute-start.20 = (bf16[64,2048]{1,0:T(8,128)(2,1)S(1)}, bf16[64,2048]{1,0:T(8,128)(2,1)S(1)}, u32[]{:S(2)}, u32[]{:S(2)}) collective-permute-start(bf16[64,2048]{1,0:T(8,128)(2,1)S(1)} %slice.8), channel_id=1, source_target_pairs={{0,8},{8,16},{16,24},{24,0},{1,9},{9,17},{17,25},{25,1},{2,10},{10... | collective-permute-start | bytes 786440 | tf_op jit(solution)/shard_map/ppermute | solution.py:148
  49.8 7.9 %collective-permute-start.21 = (bf16[64,2048]{1,0:T(8,128)(2,1)S(1)}, bf16[64,2048]{1,0:T(8,128)(2,1)}, u32[]{:S(2)}, u32[]{:S(2)}) collective-permute-start(bf16[64,2048]{1,0:T(8,128)(2,1)S(1)} %slice.9), channel_id=1, source_target_pairs={{0,24},{8,0},{16,8},{24,16},{1,25},{9,1},{17,9},{25,17},{2,26},{10... | collective-permute-start | bytes 786440 | tf_op jit(solution)/shard_map/ppermute | solution.py:148
  50.9 16.2 %collective-permute-start.14 = (bf16[128,2048]{1,0:T(8,128)(2,1)S(1)}, bf16[128,2048]{1,0:T(8,128)(2,1)S(1)}, u32[]{:S(2)}, u32[]{:S(2)}) collective-permute-start(bf16[128,2048]{1,0:T(8,128)(2,1)S(1)} %collective-permute-done.13.refs_0_), channel_id=1, source_target_pairs={{0,4},{4,0},{1,5},{5,1},{2,6},{6,2},{3,7},{7,3},{8,12},{12,8},{9,1... | collective-permute-start | bytes 1572872 | tf_op jit(solution)/shard_map/ppermute | solution.py:152
  50.9 16.9 %collective-permute-start.16 = (bf16[128,2048]{1,0:T(8,128)(2,1)S(1)}, bf16[128,2048]{1,0:T(8,128)(2,1)S(1)}, u32[]{:S(2)}, u32[]{:S(2)}) collective-permute-start(bf16[128,2048]{1,0:T(8,128)(2,1)S(1)} %collective-permute-done.15.refs_2_), channel_id=1, source_target_pairs={{0,4},{4,0},{1,5},{5,1},{2,6},{6,2},{3,7},{7,3},{8,12},{12,8},{9,1... | collective-permute-start | bytes 1572872 | tf_op jit(solution)/shard_map/ppermute | solution.py:152
  57.0 4.7 %collective-permute-start.22 = (bf16[64,2048]{1,0:T(8,128)(2,1)S(1)}, bf16[64,2048]{1,0:T(8,128)(2,1)}, u32[]{:S(2)}, u32[]{:S(2)}) collective-permute-start(bf16[64,2048]{1,0:T(8,128)(2,1)S(1)} %collective-permute-done.20.refs_0_), channel_id=1, source_target_pairs={{0,4},{4,0},{1,5},{5,1},{2,6},{6,2},{3,7},{7,3},{8,12},{12,8},{9,1... | collective-permute-start | bytes 786440 | tf_op jit(solution)/shard_map/ppermute | solution.py:152
  57.7 5.7 %collective-permute-start.23 = (bf16[64,2048]{1,0:T(8,128)(2,1)}, bf16[64,2048]{1,0:T(8,128)(2,1)}, u32[]{:S(2)}, u32[]{:S(2)}) collective-permute-start(bf16[64,2048]{1,0:T(8,128)(2,1)} %collective-permute-done.21.refs_1_), channel_id=1, source_target_pairs={{0,4},{4,0},{1,5},{5,1},{2,6},{6,2},{3,7},{7,3},{8,12},{12,8},{9,1... | collective-permute-start | bytes 786440 | tf_op jit(solution)/shard_map/ppermute | solution.py:152
  57.7 1.6 %copy-start.1 = (bf16[512,2048]{1,0:T(8,128)(2,1)S(1)}, bf16[512,2048]{1,0:T(8,128)(2,1)}, u32[]{:S(2)}) copy-start(bf16[512,2048]{1,0:T(8,128)(2,1)} %all-gather.2.cloned.1.call-done.w_ref) | copy-start | bytes 6291460
  59.3 5.9 %copy-start.2 = (bf16[512,2048]{1,0:T(8,128)(2,1)S(1)}, bf16[512,2048]{1,0:T(8,128)(2,1)}, u32[]{:S(2)}) copy-start(bf16[512,2048]{1,0:T(8,128)(2,1)} %all-gather.2.cloned.1.call-done.w_ref) | copy-start | bytes 6291460
  60.1 10.1 %collective-permute-start.10 = (bf16[256,128]{1,0:T(8,128)(2,1)S(1)}, bf16[256,128]{1,0:T(8,128)(2,1)S(1)}, u32[]{:S(2)}, u32[]{:S(2)}) collective-permute-start(bf16[256,128]{1,0:T(8,128)(2,1)S(1)} %get-tuple-element.18), channel_id=1, source_target_pairs={{0,1},{1,2},{2,3},{3,0},{4,5},{5,6},{6,7},{7,4},{8,9},{9,10},{10,1... | collective-permute-start | bytes 196616 | tf_op jit(solution)/shard_map/ppermute | solution.py:148
  61.7 10.7 %collective-permute-start.11 = (bf16[256,128]{1,0:T(8,128)(2,1)S(1)}, bf16[256,128]{1,0:T(8,128)(2,1)S(1)}, u32[]{:S(2)}, u32[]{:S(2)}) collective-permute-start(bf16[256,128]{1,0:T(8,128)(2,1)S(1)} %get-tuple-element.19), channel_id=1, source_target_pairs={{0,3},{1,0},{2,1},{3,2},{4,7},{5,4},{6,5},{7,6},{8,11},{9,8},{10,9... | collective-permute-start | bytes 196616 | tf_op jit(solution)/shard_map/ppermute | solution.py:148
  63.4 10.0 %collective-permute-start.12 = (bf16[256,128]{1,0:T(8,128)(2,1)S(1)}, bf16[256,128]{1,0:T(8,128)(2,1)S(1)}, u32[]{:S(2)}, u32[]{:S(2)}) collective-permute-start(bf16[256,128]{1,0:T(8,128)(2,1)S(1)} %get-tuple-element.20), channel_id=1, source_target_pairs={{0,2},{1,3},{2,0},{3,1},{4,6},{5,7},{6,4},{7,5},{8,10},{9,11},{10,... | collective-permute-start | bytes 196616 | tf_op jit(solution)/shard_map/ppermute | solution.py:148
  67.2 7.8 %collective-permute-start.24 = (bf16[256,128]{1,0:T(8,128)(2,1)S(1)}, bf16[256,128]{1,0:T(8,128)(2,1)S(1)}, u32[]{:S(2)}, u32[]{:S(2)}) collective-permute-start(bf16[256,128]{1,0:T(8,128)(2,1)S(1)} %get-tuple-element.26), channel_id=1, source_target_pairs={{0,1},{1,2},{2,3},{3,0},{4,5},{5,6},{6,7},{7,4},{8,9},{9,10},{10,1... | collective-permute-start | bytes 196616 | tf_op jit(solution)/shard_map/ppermute | solution.py:148
  69.1 11.6 %collective-permute-start.17 = (bf16[512,128]{1,0:T(8,128)(2,1)S(1)}, bf16[512,128]{1,0:T(8,128)(2,1)S(1)}, u32[]{:S(2)}, u32[]{:S(2)}) collective-permute-start(bf16[512,128]{1,0:T(8,128)(2,1)S(1)} %get-tuple-element.22), channel_id=1, source_target_pairs={{0,1},{1,2},{2,3},{3,0},{4,5},{5,6},{6,7},{7,4},{8,9},{9,10},{10,1... | collective-permute-start | bytes 393224 | tf_op jit(solution)/shard_map/ppermute | solution.py:148
  70.2 10.5 %collective-permute-start.18 = (bf16[512,128]{1,0:T(8,128)(2,1)S(1)}, bf16[512,128]{1,0:T(8,128)(2,1)S(1)}, u32[]{:S(2)}, u32[]{:S(2)}) collective-permute-start(bf16[512,128]{1,0:T(8,128)(2,1)S(1)} %get-tuple-element.23), channel_id=1, source_target_pairs={{0,3},{1,0},{2,1},{3,2},{4,7},{5,4},{6,5},{7,6},{8,11},{9,8},{10,9... | collective-permute-start | bytes 393224 | tf_op jit(solution)/shard_map/ppermute | solution.py:148
  72.5 8.3 %collective-permute-start.19 = (bf16[512,128]{1,0:T(8,128)(2,1)S(1)}, bf16[512,128]{1,0:T(8,128)(2,1)S(1)}, u32[]{:S(2)}, u32[]{:S(2)}) collective-permute-start(bf16[512,128]{1,0:T(8,128)(2,1)S(1)} %get-tuple-element.24), channel_id=1, source_target_pairs={{0,2},{1,3},{2,0},{3,1},{4,6},{5,7},{6,4},{7,5},{8,10},{9,11},{10,... | collective-permute-start | bytes 393224 | tf_op jit(solution)/shard_map/ppermute | solution.py:148
  73.4 7.0 %collective-permute-start.25 = (bf16[256,128]{1,0:T(8,128)(2,1)S(1)}, bf16[256,128]{1,0:T(8,128)(2,1)S(1)}, u32[]{:S(2)}, u32[]{:S(2)}) collective-permute-start(bf16[256,128]{1,0:T(8,128)(2,1)S(1)} %get-tuple-element.27), channel_id=1, source_target_pairs={{0,3},{1,0},{2,1},{3,2},{4,7},{5,4},{6,5},{7,6},{8,11},{9,8},{10,9... | collective-permute-start | bytes 196616 | tf_op jit(solution)/shard_map/ppermute | solution.py:148
  74.9 5.8 %collective-permute-start.26 = (bf16[256,128]{1,0:T(8,128)(2,1)S(1)}, bf16[256,128]{1,0:T(8,128)(2,1)S(1)}, u32[]{:S(2)}, u32[]{:S(2)}) collective-permute-start(bf16[256,128]{1,0:T(8,128)(2,1)S(1)} %get-tuple-element.28), channel_id=1, source_target_pairs={{0,2},{1,3},{2,0},{3,1},{4,6},{5,7},{6,4},{7,5},{8,10},{9,11},{10,... | collective-permute-start | bytes 196616 | tf_op jit(solution)/shard_map/ppermute | solution.py:148
Sparse Core Ops, SparseCore 0:
  9.1 43.9 all-gather.1

commit v3 on v2

v3 whole, which is shorter than its diff:
```python
import functools
import math

import jax
import jax.numpy as jnp
from jax import lax
from jax.experimental import pallas as pl
from jax.experimental.pallas import tpu as pltpu
from jax.sharding import Mesh
from jax.sharding import PartitionSpec as P

HEAD = 128
BLOCK = 128
NEG = -1e30
BF16 = jnp.bfloat16
F32 = jnp.float32
NZ, NY, NC, NX = 8, 4, 2, 4
ROW = NY * NC
CTX = NZ * ROW
CHIPS = NZ * NY
REACH = 4
KEYS = 2 * (REACH + 1) * BLOCK
CHUNKS = [(0, 1, NY - 1), (2,)]


def fetch(copies):
    for copy in copies:
        copy.start()
    for copy in copies:
        copy.wait()


def join_kernel(k_ref, v_ref, o_ref, sems):
    width = k_ref.shape[1]
    fetch(
        [
            pltpu.make_async_copy(ref, o_ref.at[:, n * width : (n + 1) * width], sems.at[n])
            for n, ref in enumerate((k_ref, v_ref))
        ]
    )


def prepare_kernel(place_ref, homes_ref, ends_ref, q_ref, keep_ref, give_ref, bias_ref):
    index, core = place_ref[0], place_ref[1]
    swapped = index + 1 - 2 * core
    rows = lax.broadcasted_iota(jnp.int32, (BLOCK, BLOCK), 0)
    lanes = lax.broadcasted_iota(jnp.int32, (BLOCK, BLOCK), 1)
    parity = lanes % 2 == rows // CHIPS % 2
    half = rows // CTX
    own, other = homes_ref[0:1, :], homes_ref[1:2, :]

    select = (own == rows % CHIPS * NC + (half + core) % NC) & parity
    queries = jnp.dot(
        jnp.where(select, 1.0, 0.0).astype(BF16), q_ref[...], preferred_element_type=F32
    ).astype(BF16)
    keep_ref[...] = queries[:CTX]
    give_ref[...] = queries[CTX:]

    attended = (jnp.where(half == 0, own, other) == rows % CHIPS * NC + core) & parity
    token = jnp.sum(jnp.where(attended, lanes, 0), axis=1, keepdims=True)
    query_pos = jnp.where(half[:, :1] == 0, index, swapped) * BLOCK + token
    ends = ends_ref[...]
    doc_start = jnp.max(jnp.where(ends <= query_pos, ends, 0), axis=1, keepdims=True)
    blocks = [start - 2 * s for start in (index, swapped) for s in range(REACH + 1)]
    for n, block in enumerate(blocks):
        key_pos = block * BLOCK + lanes
        admitted = (key_pos <= query_pos) & (key_pos >= doc_start)
        bias_ref[:, n * BLOCK : (n + 1) * BLOCK] = jnp.where(admitted, 0.0, NEG)


def attend_kernel(bias_ref, keep_ref, got_ref, *refs):
    blocks, out_ref = refs[:-1], refs[-1]
    kv_heads = blocks[0].shape[1] // HEAD // 2
    group = keep_ref.shape[1] // HEAD // kv_heads

    scale = math.log2(math.e) / math.sqrt(HEAD)
    step = 2
    bias = jnp.concatenate([bias_ref[...]] * step, axis=0)
    for k in range(kv_heads):
        keys, values = [
            jnp.concatenate([ref[:, n * HEAD : (n + 1) * HEAD] for ref in blocks], axis=0)
            for n in (k, kv_heads + k)
        ]
        for g in range(0, group, step):
            columns = [(k * group + g + n) * HEAD for n in range(step)]
            stacked = jnp.concatenate(
                [ref[:, c : c + HEAD] for c in columns for ref in (keep_ref, got_ref)], axis=0
            )
            scores = lax.dot_general(
                stacked, keys, (((1,), (1,)), ((), ())), preferred_element_type=F32
            )
            scores = scores + bias
            top = jnp.max(scores, axis=1, keepdims=True)
            weights = jnp.exp2((scores - top) * scale)
            total = jnp.sum(weights, axis=1, keepdims=True)
            summed = jnp.dot(weights.astype(BF16), values, preferred_element_type=F32)
            attended = (summed / total).astype(BF16)
            for n, c in enumerate(columns):
                out_ref[:, c : c + HEAD] = attended[n * BLOCK : (n + 1) * BLOCK]


def project_kernel(x_ref, w_ref, *refs):
    *refs, sorted_ref, sems = refs
    blocks, outs = refs[:-NX], refs[-NX:]
    width = w_ref.shape[0] // NX
    copies = [
        pltpu.make_async_copy(
            w_ref.at[pl.ds(pl.multiple_of((x_ref[0] + n) % NX * width, width), width), :],
            sorted_ref.at[n],
            sems.at[n],
        )
        for n in range(NX)
    ]
    for copy in copies:
        copy.start()
    rows = jnp.concatenate([ref[...] for ref in blocks], axis=0)
    for n, out in enumerate(outs):
        copies[n].wait()
        out[...] = lax.dot_general(
            rows, sorted_ref[n], (((1,), (1,)), ((), ())), preferred_element_type=F32
        ).astype(out.dtype)


def reduce_kernel(place_ref, *refs):
    shares, o_ref, total = refs[:-2], refs[-2], refs[-1]
    y, core = place_ref[0], place_ref[1]
    for chunk, sources in enumerate(CHUNKS):
        summed = shares[NX * chunk][...]
        for n in range(1, NX):
            summed = summed + shares[NX * chunk + n][...].astype(F32)
        for n in range(len(sources) * NC):
            row = ((y + sources[n // NC]) % NY * NC + (core + n) % NC) * CTX
            for half in range(2):
                total[half, pl.ds(pl.multiple_of(row, CTX), CTX), :] = summed[
                    n * CTX : (n + 1) * CTX, half * 128 : half * 128 + 128
                ]
    for half in range(2):
        for chip in range(CHIPS):
            o_ref[chip, :, half * 128 : half * 128 + 128] = total[
                half, pl.ds(chip, 16, stride=CHIPS), :
            ].astype(BF16)


def place_kernel(x_ref, o_ref):
    for z in range(NZ):
        for y in range(NY):
            for half in range(2):
                column = half * 512 + y * 128
                o_ref[z * 16 : z * 16 + 16, column : column + 128] = x_ref[
                    z * NY + y, :, half * 128 : half * 128 + 128
                ]


def call(kernel, out_shape, flops, moved, vmem=16, **kwargs):
    return pl.pallas_call(
        kernel,
        out_shape=out_shape,
        cost_estimate=pl.CostEstimate(flops=flops, bytes_accessed=moved, transcendentals=0),
        compiler_params=pltpu.CompilerParams(vmem_limit_bytes=vmem << 20),
        **kwargs,
    )


def chip_shift(value, steps):
    pairs = [
        (chip * NC + core, (chip + steps) % CHIPS * NC + core)
        for chip in range(CHIPS)
        for core in range(NC)
    ]
    return lax.ppermute(value, ("z", "y", "core"), pairs)


def ring_shift(value, axis, steps):
    count = lax.axis_size(axis)
    return lax.ppermute(value, axis, [(n, (n + steps) % count) for n in range(count)])


def core_swap(value):
    return lax.ppermute(value, "core", [(0, 1), (1, 0)])


def after(value, *earlier):
    return lax.optimization_barrier((value, *earlier))[0]


def on_device(queries, rotated_keys, value_vectors, doc_lengths, owner_lists, out_weight):
    index = lax.axis_index(("z", "y", "core")).astype(jnp.int32)
    at = {name: lax.axis_index(name).astype(jnp.int32) for name in ("z", "y", "core", "tp")}
    tokens, row_width = queries.shape
    vmem = pl.BlockSpec(memory_space=pltpu.VMEM)
    smem = pl.BlockSpec(memory_space=pltpu.SMEM)
    hbm = pl.BlockSpec(memory_space=pltpu.HBM)

    weight = lax.all_gather(out_weight, ("z", "core"), axis=0, tiled=True)
    features = weight.shape[0]

    own = call(
        join_kernel,
        jax.ShapeDtypeStruct((tokens, 2 * rotated_keys.shape[1]), BF16),
        0,
        1 << 18,
        in_specs=[hbm] * 2,
        out_specs=vmem,
        scratch_shapes=[pltpu.SemaphoreType.DMA((2,))],
    )(rotated_keys, value_vectors)
    mine = [own] + [chip_shift(own, s) for s in range(1, REACH + 1)]
    other = [core_swap(v) for v in mine]

    order = jnp.arange(doc_lengths.shape[0])
    ends = jnp.sum(jnp.where(order[None, :] <= order[:, None], doc_lengths[None, :], 0), axis=1)
    ends = jnp.pad(ends, (0, BLOCK - ends.shape[0]), constant_values=1 << 30).reshape(1, BLOCK)
    pair = lax.dynamic_slice_in_dim(owner_lists, index - at["core"], NC, axis=0)
    pair = jnp.where(at["core"] == 0, pair, pair[::-1])
    homes = jnp.broadcast_to(pair[:, :, None], (NC, CTX, tokens // CTX)).reshape(NC, tokens)
    half_rows = jax.ShapeDtypeStruct((tokens // 2, row_width), BF16)
    keep, give, bias = call(
        prepare_kernel,
        [half_rows, half_rows, jax.ShapeDtypeStruct((tokens, KEYS), F32)],
        2 * tokens * tokens * row_width,
        2 << 20,
        in_specs=[smem] + [vmem] * 3,
        out_specs=[vmem] * 3,
    )(
        jnp.stack([index, at["core"]]),
        homes.astype(jnp.int32),
        ends.astype(jnp.int32),
        queries,
    )
    attended = call(
        attend_kernel,
        jax.ShapeDtypeStruct((tokens, row_width), BF16),
        4 * tokens * row_width * KEYS,
        8 << 20,
        in_specs=[vmem] * (3 + 2 * (REACH + 1)),
        out_specs=vmem,
    )(bias, keep, core_swap(give), *mine, *other)
    rows = {0: attended} | {d: ring_shift(attended, "y", -d) for d in (1, 3)}
    rows[2] = ring_shift(after(attended, rows[1], rows[3]), "y", 2)

    def project(blocks):
        count = sum(block.shape[0] for block in blocks)
        shape = (count, features // NX)
        shares = call(
            project_kernel,
            [jax.ShapeDtypeStruct(shape, F32)] + [jax.ShapeDtypeStruct(shape, BF16)] * 3,
            2 * count * features * row_width,
            (4 << 20) + count * (2 * row_width + 2560),
            in_specs=[smem, hbm] + [vmem] * len(blocks),
            out_specs=[vmem] * NX,
            scratch_shapes=[
                pltpu.VMEM((NX, features // NX, row_width), BF16),
                pltpu.SemaphoreType.DMA((NX,)),
            ],
        )(at["tp"].reshape(1), weight, *blocks)
        return [shares[0]] + [ring_shift(shares[d], "tp", d) for d in (1, 3, 2)]

    shares = []
    for chunk in CHUNKS:
        shares += project([rows[d] for d in chunk])
    sent = call(
        reduce_kernel,
        jax.ShapeDtypeStruct((CHIPS, 16, features // NX), BF16),
        4 << 20,
        2 << 20,
        in_specs=[smem] + [vmem] * len(shares),
        out_specs=vmem,
        scratch_shapes=[pltpu.VMEM((2, ROW * CTX, 128), F32)],
    )(jnp.stack([at["y"], at["core"]]), *shares)
    received = lax.all_to_all(sent, ("z", "y"), 0, 0, tiled=True)
    return call(
        place_kernel,
        jax.ShapeDtypeStruct((tokens, features), BF16),
        1 << 20,
        1 << 19,
        in_specs=[vmem],
        out_specs=vmem,
    )(received)


def solution(mesh):
    split = Mesh(mesh.devices.reshape(NZ, NY, NC, NX), ("z", "y", "core", "tp"))
    ctx = ("z", "y", "core")
    placed = (P(ctx, "tp"), P(ctx, "tp"), P(ctx, "tp"), P(), P(), P(ctx, "tp"))
    return jax.shard_map(
        on_device, mesh=split, in_specs=placed, out_specs=P(ctx, "tp"), check_vma=False
    )
```

time: 116 us -> 110 us (0.948)
  starting transfers between devices: 29.2 us -> 21.5 us
  blocking collectives: 24.7 us -> 17.5 us
  Pallas kernels: 11.4 us -> 15.3 us
  waiting for transfers between devices: 29.8 us -> 33.6 us
  local copies, waits for them, and re-layouts: 4.57 us -> 5.86 us
    ppermute x13 -> x9, starting transfers between devices: 19.2 us -> 11.9 us  [ring_shift(): lax.ppermute(value, axis, [(n, (n + steps) % count) for n in range(count)])]
    all_to_all x1, blocking collectives: 24.7 us -> 17.5 us  [on_device(): received = lax.all_to_all(sent, ('z', 'y'), 0, 0, tiled=True)]
    all_gather x1, waiting for transfers between devices: 0.01 us -> 4.13 us  [on_device(): weight = lax.all_gather(out_weight, ('z', 'core'), axis=0, tiled=True)]
    pallas_call x3 -> x2, Pallas kernels: 3.87 us -> 7.56 us  [project(): call(project_kernel, [jax.ShapeDtypeStruct(shape, F32)] + [jax.ShapeDtype...]
    unnamed x12 -> x10, local copies, waits for them, and re-layouts: 4.31 us -> 4.91 us
    ppermute x13 -> x9, waiting for transfers between devices: 22 us -> 22.4 us  [ring_shift(): lax.ppermute(value, axis, [(n, (n + steps) % count) for n in range(count)])]
    pallas_call x3 -> x4, Pallas kernels: 7.5 us -> 7.72 us  [the longest x1 5 us: on_device(): call(attend_kernel, jax.ShapeDtypeStruct((tokens, row_width), BF16), 4 *...]
  transfers between devices with their start and end apart: 28 -> 20, of which waited for: 10 -> 9; matrix products, arithmetic and copies ran while one was open for 1% -> 2% of each run, Pallas kernels for 8% -> 12%
where the time goes in v3:
time: 110 us; the launch traced here: 109 us
  waiting for transfers between devices  33.6 us (31%)
  starting transfers between devices  21.5 us (20%)
  blocking collectives  17.5 us (16%)
  Pallas kernels  15.3 us (14%)
  between operations  13.5 us (12%)
  local copies, waits for them, and re-layouts  5.86 us (5%)
  other arithmetic  1.63 us (1%)
    ppermute x9, waiting for transfers between devices, ring_shift(): lax.ppermute(value, axis, [(n, (n + steps) % count) for n in range(count)])  22.4 us
    all_to_all x1, blocking collectives, on_device(): received = lax.all_to_all(sent, ('z', 'y'), 0, 0, tiled=True)  17.5 us
    ppermute x9, starting transfers between devices, ring_shift(): lax.ppermute(value, axis, [(n, (n + steps) % count) for n in range(count)])  11.9 us
    ppermute x4, starting transfers between devices, chip_shift(): return lax.ppermute(value, ('z', 'y', 'core'), pairs)  8.34 us
    pallas_call x2, Pallas kernels, project(): call(project_kernel, [jax.ShapeDtypeStruct(shape, F32)] + [jax.ShapeDtype...  7.56 us
    ppermute x4, waiting for transfers between devices, chip_shift(): return lax.ppermute(value, ('z', 'y', 'core'), pairs)  5.34 us
    pallas_call x1, Pallas kernels, on_device(): call(attend_kernel, jax.ShapeDtypeStruct((tokens, row_width), BF16), 4 *...  5 us
    unnamed x10, local copies, waits for them, and re-layouts  4.91 us
  transfers between devices with their start and end apart: 20, of which 9 were waited for; matrix products, arithmetic and copies ran while one was open for 2% of the time, Pallas kernels for 12%

profile of v3, /device:TPU:8, one launch (start us, length us, event | category | flops | bytes accessed | tf_op | source)
XLA Modules:
  0.0 108.9 jit_solution(6912243499757677972)
XLA Ops:
  6.5 0.7 all-gather.2.cloned.1.call-update
  7.3 0.8 copy-done.3
  8.1 0.8 copy-done.4
  9.0 1.7 %collective-permute-start.1 = (bf16[128,512]{1,0:T(8,128)(2,1)S(1)}, bf16[128,512]{1,0:T(8,128)(2,1)S(1)}, u32[]{:S(2)}, u32[]{:S(2)}) collective-permute-start(bf16[128,512]{1,0:T(8,128)(2,1)S(1)} %shard_map.65.refs_0_), channel_id=1, source_target_pairs={{0,8},{4,12},{8,16},{12,20},{16,24},{20,28},{24,32},{28,36},{32,40... | collective-permute-start | bytes 393224 | tf_op jit(solution)/shard_map/ppermute | solution.py:170
  10.6 2.3 %collective-permute-start.2 = (bf16[128,512]{1,0:T(8,128)(2,1)S(1)}, bf16[128,512]{1,0:T(8,128)(2,1)S(1)}, u32[]{:S(2)}, u32[]{:S(2)}) collective-permute-start(bf16[128,512]{1,0:T(8,128)(2,1)S(1)} %shard_map.65.refs_0_), channel_id=1, source_target_pairs={{0,16},{4,20},{8,24},{12,28},{16,32},{20,36},{24,40},{28,44},{32,4... | collective-permute-start | bytes 393224 | tf_op jit(solution)/shard_map/ppermute | solution.py:170
  12.9 2.4 %collective-permute-start.3 = (bf16[128,512]{1,0:T(8,128)(2,1)S(1)}, bf16[128,512]{1,0:T(8,128)(2,1)S(1)}, u32[]{:S(2)}, u32[]{:S(2)}) collective-permute-start(bf16[128,512]{1,0:T(8,128)(2,1)S(1)} %shard_map.65.refs_0_), channel_id=1, source_target_pairs={{0,24},{4,28},{8,32},{12,36},{16,40},{20,44},{24,48},{28,52},{32,5... | collective-permute-start | bytes 393224 | tf_op jit(solution)/shard_map/ppermute | solution.py:170
  15.3 0.7 constant_dynamic-slice_fusion
  16.1 0.8 select_reduce_fusion
  16.8 0.7 broadcast_select_fusion
  17.5 0.1 broadcast_in_dim.14
  17.6 0.1 reshape.13.homes_ref
  17.8 0.1 pad_add_fusion.1.place_ref
  17.9 1.0 copy-done.2
  18.9 1.0 shard_map.64
  19.9 0.1 collective-permute-start
  20.0 2.0 %collective-permute-start.4 = (bf16[128,512]{1,0:T(8,128)(2,1)S(1)}, bf16[128,512]{1,0:T(8,128)(2,1)S(1)}, u32[]{:S(2)}, u32[]{:S(2)}) collective-permute-start(bf16[128,512]{1,0:T(8,128)(2,1)S(1)} %shard_map.65.refs_0_), channel_id=1, source_target_pairs={{0,32},{4,36},{8,40},{12,44},{16,48},{20,52},{24,56},{28,60},{32,6... | collective-permute-start | bytes 393224 | tf_op jit(solution)/shard_map/ppermute | solution.py:170
  21.9 0.0 collective-permute-done.1.refs_1_
  22.0 0.2 collective-permute-start.5
  22.1 2.8 %collective-permute-done.2.refs_2_ = bf16[128,512]{1,0:T(8,128)(2,1)S(1)} collective-permute-done((bf16[128,512]{1,0:T(8,128)(2,1)S(1)}, bf16[128,512]{1,0:T(8,128)(2,1)S(1)}, u32[]{:S(2)}, u32[]{:S(2)}) %collective-permute-start.2) | collective-permute-done | bytes 131104 | tf_op jit(solution)/shard_map/ppermute | solution.py:170
  24.9 0.0 collective-permute-done.3.refs_3_
  24.9 0.5 collective-permute-start.7
  25.4 2.5 %collective-permute-done.4.refs_4_ = bf16[128,512]{1,0:T(8,128)(2,1)S(1)} collective-permute-done((bf16[128,512]{1,0:T(8,128)(2,1)S(1)}, bf16[128,512]{1,0:T(8,128)(2,1)S(1)}, u32[]{:S(2)}, u32[]{:S(2)}) %collective-permute-start.4) | collective-permute-done | bytes 131104 | tf_op jit(solution)/shard_map/ppermute | solution.py:170
  28.0 0.5 collective-permute-start.9
  28.5 0.0 collective-permute-done.7.refs_7_
  28.5 0.8 collective-permute-done.8.refs_8_
  29.3 0.2 collective-permute-done.9.refs_9_
  29.5 5.0 %shard_map.66.refs_0_ = bf16[128,2048]{1,0:T(8,128)(2,1)S(1)} custom-call(f32[128,1280]{1,0:T(8,128)S(1)} %get-tuple-element.17.bias_ref, bf16[64,2048]{1,0:T(8,128)(2,1)S(1)} %get-tuple-element.18.keep_ref, bf16[64,2048]{1,0:T(8,128)(2,1)S(1)} %collective-permute-done.got_ref, bf16[128,512]{1,0:T(8,128)(2,1)S(1)} %shard_map.65.refs_0_, ...), custom_call_target="tpu_custom_call" | custom-call | flops 1342177280 | bytes 8388608 | tf_op jit(solution)/shard_map/pallas_call | solution.py:229
  34.5 2.1 %collective-permute-start.10 = (bf16[128,2048]{1,0:T(8,128)(2,1)S(1)}, bf16[128,2048]{1,0:T(8,128)(2,1)S(1)}, u32[]{:S(2)}, u32[]{:S(2)}) collective-permute-start(bf16[128,2048]{1,0:T(8,128)(2,1)S(1)} %shard_map.66.refs_0_), channel_id=1, source_target_pairs={{0,24},{8,0},{16,8},{24,16},{1,25},{9,1},{17,9},{25,17},{2,26},{10... | collective-permute-start | bytes 1572872 | tf_op jit(solution)/shard_map/ppermute | solution.py:175
  36.6 0.0 collective-permute-start.11
  36.6 12.1 %collective-permute-done.10.refs_1_ = bf16[128,2048]{1,0:T(8,128)(2,1)S(1)} collective-permute-done((bf16[128,2048]{1,0:T(8,128)(2,1)S(1)}, bf16[128,2048]{1,0:T(8,128)(2,1)S(1)}, u32[]{:S(2)}, u32[]{:S(2)}) %collective-permute-start.10) | collective-permute-done | bytes 524320 | tf_op jit(solution)/shard_map/ppermute | solution.py:175
  48.7 1.6 %collective-permute-done.11.refs_2_ = bf16[128,2048]{1,0:T(8,128)(2,1)S(1)} collective-permute-done((bf16[128,2048]{1,0:T(8,128)(2,1)S(1)}, bf16[128,2048]{1,0:T(8,128)(2,1)S(1)}, u32[]{:S(2)}, u32[]{:S(2)}) %collective-permute-start.11) | collective-permute-done | bytes 524320 | tf_op jit(solution)/shard_map/ppermute | solution.py:175
  50.4 0.8 collective-permute-start.15
  51.1 4.1 %all-gather.2.cloned.1.call-done.w_ref = bf16[1024,2048]{1,0:T(8,128)(2,1)} async-done(((bf16[64,2048]{1,0:T(8,128)(2,1)}), bf16[1024,2048]{1,0:T(8,128)(2,1)}) %all-gather.2.cloned.1.call-update) | async-done | bytes 4194320 | tf_op jit(solution)/shard_map/all_gather | solution.py:194
  55.3 2.2 %copy-done = bf16[1024,2048]{1,0:T(8,128)(2,1)S(1)} copy-done((bf16[1024,2048]{1,0:T(8,128)(2,1)S(1)}, bf16[1024,2048]{1,0:T(8,128)(2,1)}, u32[]{:S(2)}) %copy-start) | copy-done | bytes 4194328
  57.5 4.4 %shard_map.67 = (f32[384,256]{1,0:T(8,128)S(1)}, bf16[384,256]{1,0:T(8,128)(2,1)S(1)}, bf16[384,256]{1,0:T(8,128)(2,1)S(1)}, bf16[384,256]{1,0:T(8,128)(2,1)S(1)}) custom-call(s32[1]{0:T(128)} %bitcast.2.x_ref, bf16[1024,2048]{1,0:T(8,128)(2,1)S(1)} %copy-done, bf16[128,2048]{1,0:T(8,128)(2,1)S(1)} %shard_map.66.refs_0_, ...), custom_call_target="tpu_custom_call" | custom-call | flops 1610612736 | bytes 6750208 | tf_op jit(solution)/shard_map/pallas_call | solution.py:243
  61.9 1.6 %collective-permute-start.12 = (bf16[384,256]{1,0:T(8,128)(2,1)S(1)}, bf16[384,256]{1,0:T(8,128)(2,1)S(1)}, u32[]{:S(2)}, u32[]{:S(2)}) collective-permute-start(bf16[384,256]{1,0:T(8,128)(2,1)S(1)} %get-tuple-element.21), channel_id=1, source_target_pairs={{0,1},{1,2},{2,3},{3,0},{4,5},{5,6},{6,7},{7,4},{8,9},{9,10},{10,1... | collective-permute-start | bytes 589832 | tf_op jit(solution)/shard_map/ppermute | solution.py:175
  63.4 1.7 %collective-permute-start.13 = (bf16[384,256]{1,0:T(8,128)(2,1)S(1)}, bf16[384,256]{1,0:T(8,128)(2,1)S(1)}, u32[]{:S(2)}, u32[]{:S(2)}) collective-permute-start(bf16[384,256]{1,0:T(8,128)(2,1)S(1)} %get-tuple-element.22), channel_id=1, source_target_pairs={{0,3},{1,0},{2,1},{3,2},{4,7},{5,4},{6,5},{7,6},{8,11},{9,8},{10,9... | collective-permute-start | bytes 589832 | tf_op jit(solution)/shard_map/ppermute | solution.py:175
  65.2 1.8 %collective-permute-start.14 = (bf16[384,256]{1,0:T(8,128)(2,1)S(1)}, bf16[384,256]{1,0:T(8,128)(2,1)S(1)}, u32[]{:S(2)}, u32[]{:S(2)}) collective-permute-start(bf16[384,256]{1,0:T(8,128)(2,1)S(1)} %get-tuple-element.23), channel_id=1, source_target_pairs={{0,2},{1,3},{2,0},{3,1},{4,6},{5,7},{6,4},{7,5},{8,10},{9,11},{10,... | collective-permute-start | bytes 589832 | tf_op jit(solution)/shard_map/ppermute | solution.py:175
  66.9 3.2 %shard_map.68 = (f32[128,256]{1,0:T(8,128)S(1)}, bf16[128,256]{1,0:T(8,128)(2,1)S(1)}, bf16[128,256]{1,0:T(8,128)(2,1)S(1)}, bf16[128,256]{1,0:T(8,128)(2,1)S(1)}) custom-call(s32[1]{0:T(128)} %bitcast.2.x_ref, bf16[1024,2048]{1,0:T(8,128)(2,1)S(1)} %copy-done.1, bf16[128,2048]{1,0:T(8,128)(2,1)S(1)} %collective-permute-done.15.refs_0_), custom_call_target="tpu_custom_call" | custom-call | flops 536870912 | bytes 5046272 | tf_op jit(solution)/shard_map/pallas_call | solution.py:243
  70.1 0.9 collective-permute-start.16
  71.0 2.4 %collective-permute-start.17 = (bf16[128,256]{1,0:T(8,128)(2,1)S(1)}, bf16[128,256]{1,0:T(8,128)(2,1)S(1)}, u32[]{:S(2)}, u32[]{:S(2)}) collective-permute-start(bf16[128,256]{1,0:T(8,128)(2,1)S(1)} %get-tuple-element.27), channel_id=1, source_target_pairs={{0,3},{1,0},{2,1},{3,2},{4,7},{5,4},{6,5},{7,6},{8,11},{9,8},{10,9... | collective-permute-start | bytes 196616 | tf_op jit(solution)/shard_map/ppermute | solution.py:175
  73.4 3.5 %collective-permute-done.16.refs_5_ = bf16[128,256]{1,0:T(8,128)(2,1)S(1)} collective-permute-done((bf16[128,256]{1,0:T(8,128)(2,1)S(1)}, bf16[128,256]{1,0:T(8,128)(2,1)S(1)}, u32[]{:S(2)}, u32[]{:S(2)}) %collective-permute-start.16) | collective-permute-done | bytes 65568 | tf_op jit(solution)/shard_map/ppermute | solution.py:175
  77.0 0.6 collective-permute-start.18
  77.6 0.1 pad_add_fusion.place_ref
  77.7 5.1 %collective-permute-done.18.refs_7_ = bf16[128,256]{1,0:T(8,128)(2,1)S(1)} collective-permute-done((bf16[128,256]{1,0:T(8,128)(2,1)S(1)}, bf16[128,256]{1,0:T(8,128)(2,1)S(1)}, u32[]{:S(2)}, u32[]{:S(2)}) %collective-permute-start.18) | collective-permute-done | bytes 65568 | tf_op jit(solution)/shard_map/ppermute | solution.py:175
  82.8 1.0 shard_map.69
  83.8 17.5 %all_to_all.5.x_ref = bf16[32,16,256]{2,1,0:T(8,128)(2,1)S(1)} all-to-all(bf16[32,16,256]{2,1,0:T(8,128)(2,1)S(1)} %shard_map.69), channel_id=1, replica_groups=mesh['z'=8,'y'=4,'core'=2,'tp'=4] {'z','y'}, dimensions={0} | all-to-all | bytes 524288 | tf_op jit(solution)/shard_map/all_to_all | solution.py:269
  101.3 0.7 shard_map.70
  (20 shorter events, 0.1 us)
Async XLA Ops:
  6.5 48.7 %all-gather.2.cloned.1.call-start = ((), (), s32[]{:S(2)}) async-start(), calls=%async_computation.1 | async-start | bytes 4456448 | tf_op jit(solution)/shard_map/all_gather | solution.py:194
  7.3 0.8 copy-start.3
  8.1 0.8 copy-start.4
  9.0 13.0 %collective-permute-start.1 = (bf16[128,512]{1,0:T(8,128)(2,1)S(1)}, bf16[128,512]{1,0:T(8,128)(2,1)S(1)}, u32[]{:S(2)}, u32[]{:S(2)}) collective-permute-start(bf16[128,512]{1,0:T(8,128)(2,1)S(1)} %shard_map.65.refs_0_), channel_id=1, source_target_pairs={{0,8},{4,12},{8,16},{12,20},{16,24},{20,28},{24,32},{28,36},{32,40... | collective-permute-start | bytes 393224 | tf_op jit(solution)/shard_map/ppermute | solution.py:170
  10.6 14.3 %collective-permute-start.2 = (bf16[128,512]{1,0:T(8,128)(2,1)S(1)}, bf16[128,512]{1,0:T(8,128)(2,1)S(1)}, u32[]{:S(2)}, u32[]{:S(2)}) collective-permute-start(bf16[128,512]{1,0:T(8,128)(2,1)S(1)} %shard_map.65.refs_0_), channel_id=1, source_target_pairs={{0,16},{4,20},{8,24},{12,28},{16,32},{20,36},{24,40},{28,44},{32,4... | collective-permute-start | bytes 393224 | tf_op jit(solution)/shard_map/ppermute | solution.py:170
  12.9 12.0 %collective-permute-start.3 = (bf16[128,512]{1,0:T(8,128)(2,1)S(1)}, bf16[128,512]{1,0:T(8,128)(2,1)S(1)}, u32[]{:S(2)}, u32[]{:S(2)}) collective-permute-start(bf16[128,512]{1,0:T(8,128)(2,1)S(1)} %shard_map.65.refs_0_), channel_id=1, source_target_pairs={{0,24},{4,28},{8,32},{12,36},{16,40},{20,44},{24,48},{28,52},{32,5... | collective-permute-start | bytes 393224 | tf_op jit(solution)/shard_map/ppermute | solution.py:170
  17.9 1.0 copy-start.2
  19.9 8.6 %collective-permute-start = (bf16[64,2048]{1,0:T(8,128)(2,1)S(1)}, bf16[64,2048]{1,0:T(8,128)(2,1)S(1)}, u32[]{:S(2)}, u32[]{:S(2)}) collective-permute-start(bf16[64,2048]{1,0:T(8,128)(2,1)S(1)} %get-tuple-element.19), channel_id=1, source_target_pairs={{0,4},{4,0},{1,5},{5,1},{2,6},{6,2},{3,7},{7,3},{8,12},{12,8},{9,1... | collective-permute-start | bytes 786440 | tf_op jit(solution)/shard_map/ppermute | solution.py:179
  20.0 8.0 %collective-permute-start.4 = (bf16[128,512]{1,0:T(8,128)(2,1)S(1)}, bf16[128,512]{1,0:T(8,128)(2,1)S(1)}, u32[]{:S(2)}, u32[]{:S(2)}) collective-permute-start(bf16[128,512]{1,0:T(8,128)(2,1)S(1)} %shard_map.65.refs_0_), channel_id=1, source_target_pairs={{0,32},{4,36},{8,40},{12,44},{16,48},{20,52},{24,56},{28,60},{32,6... | collective-permute-start | bytes 393224 | tf_op jit(solution)/shard_map/ppermute | solution.py:170
  22.0 6.0 %collective-permute-start.5 = (bf16[128,512]{1,0:T(8,128)(2,1)S(1)}, bf16[128,512]{1,0:T(8,128)(2,1)S(1)}, u32[]{:S(2)}, u32[]{:S(2)}) collective-permute-start(bf16[128,512]{1,0:T(8,128)(2,1)S(1)} %shard_map.65.refs_0_), channel_id=1, source_target_pairs={{0,4},{4,0},{1,5},{5,1},{2,6},{6,2},{3,7},{7,3},{8,12},{12,8},{9,1... | collective-permute-start | bytes 393224 | tf_op jit(solution)/shard_map/ppermute | solution.py:179
  24.9 3.6 %collective-permute-start.6 = (bf16[128,512]{1,0:T(8,128)(2,1)S(1)}, bf16[128,512]{1,0:T(8,128)(2,1)S(1)}, u32[]{:S(2)}, u32[]{:S(2)}) collective-permute-start(bf16[128,512]{1,0:T(8,128)(2,1)S(1)} %collective-permute-done.1.refs_1_), channel_id=1, source_target_pairs={{0,4},{4,0},{1,5},{5,1},{2,6},{6,2},{3,7},{7,3},{8,12},{12,8},{9,1... | collective-permute-start | bytes 393224 | tf_op jit(solution)/shard_map/ppermute | solution.py:179
  24.9 3.6 %collective-permute-start.7 = (bf16[128,512]{1,0:T(8,128)(2,1)S(1)}, bf16[128,512]{1,0:T(8,128)(2,1)S(1)}, u32[]{:S(2)}, u32[]{:S(2)}) collective-permute-start(bf16[128,512]{1,0:T(8,128)(2,1)S(1)} %collective-permute-done.2.refs_2_), channel_id=1, source_target_pairs={{0,4},{4,0},{1,5},{5,1},{2,6},{6,2},{3,7},{7,3},{8,12},{12,8},{9,1... | collective-permute-start | bytes 393224 | tf_op jit(solution)/shard_map/ppermute | solution.py:179
  28.0 1.3 %collective-permute-start.8 = (bf16[128,512]{1,0:T(8,128)(2,1)S(1)}, bf16[128,512]{1,0:T(8,128)(2,1)S(1)}, u32[]{:S(2)}, u32[]{:S(2)}) collective-permute-start(bf16[128,512]{1,0:T(8,128)(2,1)S(1)} %collective-permute-done.3.refs_3_), channel_id=1, source_target_pairs={{0,4},{4,0},{1,5},{5,1},{2,6},{6,2},{3,7},{7,3},{8,12},{12,8},{9,1... | collective-permute-start | bytes 393224 | tf_op jit(solution)/shard_map/ppermute | solution.py:179
  28.0 1.5 %collective-permute-start.9 = (bf16[128,512]{1,0:T(8,128)(2,1)S(1)}, bf16[128,512]{1,0:T(8,128)(2,1)S(1)}, u32[]{:S(2)}, u32[]{:S(2)}) collective-permute-start(bf16[128,512]{1,0:T(8,128)(2,1)S(1)} %collective-permute-done.4.refs_4_), channel_id=1, source_target_pairs={{0,4},{4,0},{1,5},{5,1},{2,6},{6,2},{3,7},{7,3},{8,12},{12,8},{9,1... | collective-permute-start | bytes 393224 | tf_op jit(solution)/shard_map/ppermute | solution.py:179
  34.5 14.2 %collective-permute-start.10 = (bf16[128,2048]{1,0:T(8,128)(2,1)S(1)}, bf16[128,2048]{1,0:T(8,128)(2,1)S(1)}, u32[]{:S(2)}, u32[]{:S(2)}) collective-permute-start(bf16[128,2048]{1,0:T(8,128)(2,1)S(1)} %shard_map.66.refs_0_), channel_id=1, source_target_pairs={{0,24},{8,0},{16,8},{24,16},{1,25},{9,1},{17,9},{25,17},{2,26},{10... | collective-permute-start | bytes 1572872 | tf_op jit(solution)/shard_map/ppermute | solution.py:175
  36.6 13.8 %collective-permute-start.11 = (bf16[128,2048]{1,0:T(8,128)(2,1)S(1)}, bf16[128,2048]{1,0:T(8,128)(2,1)S(1)}, u32[]{:S(2)}, u32[]{:S(2)}) collective-permute-start(bf16[128,2048]{1,0:T(8,128)(2,1)S(1)} %shard_map.66.refs_0_), channel_id=1, source_target_pairs={{0,8},{8,16},{16,24},{24,0},{1,9},{9,17},{17,25},{25,1},{2,10},{10... | collective-permute-start | bytes 1572872 | tf_op jit(solution)/shard_map/ppermute | solution.py:175
  50.4 16.6 %collective-permute-start.15 = (bf16[128,2048]{1,0:T(8,128)(2,1)S(1)}, bf16[128,2048]{1,0:T(8,128)(2,1)S(1)}, u32[]{:S(2)}, u32[]{:S(2)}) collective-permute-start(bf16[128,2048]{1,0:T(8,128)(2,1)S(1)} %shard_map.66.refs_0_), channel_id=1, source_target_pairs={{0,16},{8,24},{16,0},{24,8},{1,17},{9,25},{17,1},{25,9},{2,18},{10... | collective-permute-start | bytes 1572872 | tf_op jit(solution)/shard_map/ppermute | solution.py:175
  55.3 2.2 %copy-start = (bf16[1024,2048]{1,0:T(8,128)(2,1)S(1)}, bf16[1024,2048]{1,0:T(8,128)(2,1)}, u32[]{:S(2)}) copy-start(bf16[1024,2048]{1,0:T(8,128)(2,1)} %all-gather.2.cloned.1.call-done.w_ref) | copy-start | bytes 12582916
  57.5 9.5 %copy-start.1 = (bf16[1024,2048]{1,0:T(8,128)(2,1)S(1)}, bf16[1024,2048]{1,0:T(8,128)(2,1)}, u32[]{:S(2)}) copy-start(bf16[1024,2048]{1,0:T(8,128)(2,1)} %all-gather.2.cloned.1.call-done.w_ref) | copy-start | bytes 12582916
  61.9 20.9 %collective-permute-start.12 = (bf16[384,256]{1,0:T(8,128)(2,1)S(1)}, bf16[384,256]{1,0:T(8,128)(2,1)S(1)}, u32[]{:S(2)}, u32[]{:S(2)}) collective-permute-start(bf16[384,256]{1,0:T(8,128)(2,1)S(1)} %get-tuple-element.21), channel_id=1, source_target_pairs={{0,1},{1,2},{2,3},{3,0},{4,5},{5,6},{6,7},{7,4},{8,9},{9,10},{10,1... | collective-permute-start | bytes 589832 | tf_op jit(solution)/shard_map/ppermute | solution.py:175
  63.4 19.3 %collective-permute-start.13 = (bf16[384,256]{1,0:T(8,128)(2,1)S(1)}, bf16[384,256]{1,0:T(8,128)(2,1)S(1)}, u32[]{:S(2)}, u32[]{:S(2)}) collective-permute-start(bf16[384,256]{1,0:T(8,128)(2,1)S(1)} %get-tuple-element.22), channel_id=1, source_target_pairs={{0,3},{1,0},{2,1},{3,2},{4,7},{5,4},{6,5},{7,6},{8,11},{9,8},{10,9... | collective-permute-start | bytes 589832 | tf_op jit(solution)/shard_map/ppermute | solution.py:175
  65.2 17.6 %collective-permute-start.14 = (bf16[384,256]{1,0:T(8,128)(2,1)S(1)}, bf16[384,256]{1,0:T(8,128)(2,1)S(1)}, u32[]{:S(2)}, u32[]{:S(2)}) collective-permute-start(bf16[384,256]{1,0:T(8,128)(2,1)S(1)} %get-tuple-element.23), channel_id=1, source_target_pairs={{0,2},{1,3},{2,0},{3,1},{4,6},{5,7},{6,4},{7,5},{8,10},{9,11},{10,... | collective-permute-start | bytes 589832 | tf_op jit(solution)/shard_map/ppermute | solution.py:175
  70.1 6.9 %collective-permute-start.16 = (bf16[128,256]{1,0:T(8,128)(2,1)S(1)}, bf16[128,256]{1,0:T(8,128)(2,1)S(1)}, u32[]{:S(2)}, u32[]{:S(2)}) collective-permute-start(bf16[128,256]{1,0:T(8,128)(2,1)S(1)} %get-tuple-element.26), channel_id=1, source_target_pairs={{0,1},{1,2},{2,3},{3,0},{4,5},{5,6},{6,7},{7,4},{8,9},{9,10},{10,1... | collective-permute-start | bytes 196616 | tf_op jit(solution)/shard_map/ppermute | solution.py:175
  71.0 6.7 %collective-permute-start.17 = (bf16[128,256]{1,0:T(8,128)(2,1)S(1)}, bf16[128,256]{1,0:T(8,128)(2,1)S(1)}, u32[]{:S(2)}, u32[]{:S(2)}) collective-permute-start(bf16[128,256]{1,0:T(8,128)(2,1)S(1)} %get-tuple-element.27), channel_id=1, source_target_pairs={{0,3},{1,0},{2,1},{3,2},{4,7},{5,4},{6,5},{7,6},{8,11},{9,8},{10,9... | collective-permute-start | bytes 196616 | tf_op jit(solution)/shard_map/ppermute | solution.py:175
  77.0 5.8 %collective-permute-start.18 = (bf16[128,256]{1,0:T(8,128)(2,1)S(1)}, bf16[128,256]{1,0:T(8,128)(2,1)S(1)}, u32[]{:S(2)}, u32[]{:S(2)}) collective-permute-start(bf16[128,256]{1,0:T(8,128)(2,1)S(1)} %get-tuple-element.28), channel_id=1, source_target_pairs={{0,2},{1,3},{2,0},{3,1},{4,6},{5,7},{6,4},{7,5},{8,10},{9,11},{10,... | collective-permute-start | bytes 196616 | tf_op jit(solution)/shard_map/ppermute | solution.py:175
Sparse Core Ops, SparseCore 0:
  9.2 46.0 all-gather.1

commit v4 on v3

--- a/solution.py
+++ b/solution.py
@@ -20,6 +20,8 @@
 CHIPS = NZ * NY
 REACH = 4
 KEYS = 2 * (REACH + 1) * BLOCK
+PROJECT_VMEM = 52
+OFFSETS = [0, -1, 1, -2, 2, -3, 3, 4, 4]
 CHUNKS = [(0, 1, NY - 1), (2,)]
 
 
@@ -99,25 +101,30 @@
                 out_ref[:, c : c + HEAD] = attended[n * BLOCK : (n + 1) * BLOCK]
 
 
-def project_kernel(x_ref, w_ref, *refs):
+def project_kernel(place_ref, *refs):
     *refs, sorted_ref, sems = refs
-    blocks, outs = refs[:-NX], refs[-NX:]
-    width = w_ref.shape[0] // NX
-    copies = [
-        pltpu.make_async_copy(
-            w_ref.at[pl.ds(pl.multiple_of((x_ref[0] + n) % NX * width, width), width), :],
-            sorted_ref.at[n],
-            sems.at[n],
-        )
-        for n in range(NX)
-    ]
-    for copy in copies:
-        copy.start()
-    rows = jnp.concatenate([ref[...] for ref in blocks], axis=0)
+    count = NC * len(OFFSETS)
+    pieces, blocks, outs = refs[:count], refs[count:-NX], refs[-NX:]
+    z, x, core = place_ref[0], place_ref[1], place_ref[2]
+    rows = pieces[0].shape[0]
+    copies = []
+    for side in range(NC):
+        done = 0
+        for n, offset in enumerate(OFFSETS):
+            piece = pieces[side * len(OFFSETS) + n]
+            source = (z + offset + NZ) % NZ
+            row = source % 2 * 128 + (core + side) % NC * rows
+            if piece.shape[0] != rows:
+                row, done = row + done, done + piece.shape[0]
+            target = sorted_ref.at[
+                (source // 2 - x + NX) % NX, pl.ds(pl.multiple_of(row, 32), piece.shape[0]), :
+            ]
+            copies.append(pltpu.make_async_copy(piece, target, sems.at[len(copies)]))
+    fetch(copies)
+    attended = jnp.concatenate([ref[...] for ref in blocks], axis=0)
     for n, out in enumerate(outs):
-        copies[n].wait()
         out[...] = lax.dot_general(
-            rows, sorted_ref[n], (((1,), (1,)), ((), ())), preferred_element_type=F32
+            attended, sorted_ref[n], (((1,), (1,)), ((), ())), preferred_element_type=F32
         ).astype(out.dtype)
 
 
@@ -191,8 +198,10 @@
     smem = pl.BlockSpec(memory_space=pltpu.SMEM)
     hbm = pl.BlockSpec(memory_space=pltpu.HBM)
 
-    weight = lax.all_gather(out_weight, ("z", "core"), axis=0, tiled=True)
-    features = weight.shape[0]
+    up, down = [out_weight], [out_weight]
+    for _ in range(2):
+        up.append(ring_shift(up[-1], "z", 1))
+        down.append(ring_shift(down[-1], "z", -1))
 
     own = call(
         join_kernel,
@@ -224,7 +233,7 @@
         jnp.stack([index, at["core"]]),
         homes.astype(jnp.int32),
         ends.astype(jnp.int32),
-        queries,
+        after(queries, up[1], down[1]),
     )
     attended = call(
         attend_kernel,
@@ -233,9 +242,19 @@
         8 << 20,
         in_specs=[vmem] * (3 + 2 * (REACH + 1)),
         out_specs=vmem,
-    )(bias, keep, core_swap(give), *mine, *other)
+    )(after(bias, up[2], down[2]), keep, core_swap(give), *mine, *other)
     rows = {0: attended} | {d: ring_shift(attended, "y", -d) for d in (1, 3)}
-    rows[2] = ring_shift(after(attended, rows[1], rows[3]), "y", 2)
+    up.append(ring_shift(up[2], "z", 1))
+    down.append(ring_shift(down[2], "z", -1))
+    rows[2] = ring_shift(after(attended, rows[1], rows[3], up[3], down[3]), "y", 2)
+    middle = out_weight.shape[0] // 2
+    pieces = [out_weight]
+    for n in range(1, 4):
+        pieces += [up[n], down[n]]
+    pieces += [ring_shift(up[3][:middle], "z", 1), ring_shift(down[3][middle:], "z", -1)]
+    pieces += [core_swap(piece) for piece in pieces]
+    features = NZ * NC * out_weight.shape[0]
+    corner = jnp.stack([at["z"], at["tp"], at["core"]])
 
     def project(blocks):
         count = sum(block.shape[0] for block in blocks)
@@ -245,13 +264,14 @@
             [jax.ShapeDtypeStruct(shape, F32)] + [jax.ShapeDtypeStruct(shape, BF16)] * 3,
             2 * count * features * row_width,
             (4 << 20) + count * (2 * row_width + 2560),
-            in_specs=[smem, hbm] + [vmem] * len(blocks),
+            vmem=PROJECT_VMEM,
+            in_specs=[smem] + [hbm] * len(pieces) + [vmem] * len(blocks),
             out_specs=[vmem] * NX,
             scratch_shapes=[
                 pltpu.VMEM((NX, features // NX, row_width), BF16),
-                pltpu.SemaphoreType.DMA((NX,)),
+                pltpu.SemaphoreType.DMA((len(pieces),)),
             ],
-        )(at["tp"].reshape(1), weight, *blocks)
+        )(corner, *pieces, *blocks)
         return [shares[0]] + [ring_shift(shares[d], "tp", d) for d in (1, 3, 2)]
 
     shares = []

time: 110 us -> 103 us (0.936)
  starting transfers between devices: 21.5 us -> 40 us
  waiting for transfers between devices: 33.6 us -> 19.6 us
  between operations: 13.5 us -> 0.3 us
  Pallas kernels: 15.3 us -> 18 us
  local copies, waits for them, and re-layouts: 5.86 us -> 4.57 us
    ppermute x9 -> x17, starting transfers between devices: 11.9 us -> 33.3 us  [ring_shift(): lax.ppermute(value, axis, [(n, (n + steps) % count) for n in range(count)])]
    ppermute x9 -> x17, waiting for transfers between devices: 22.4 us -> 13.4 us  [ring_shift(): lax.ppermute(value, axis, [(n, (n + steps) % count) for n in range(count)])]
    ppermute x4, starting transfers between devices: 8.34 us -> 3.4 us  [chip_shift(): return lax.ppermute(value, ('z', 'y', 'core'), pairs)]
    all_gather x1 -> x0, waiting for transfers between devices: 4.13 us -> none  [on_device(): weight = lax.all_gather(out_weight, ('z', 'core'), axis=0, tiled=True)]
    pallas_call x2, Pallas kernels: 7.56 us -> 10.3 us  [project(): call(project_kernel, [jax.ShapeDtypeStruct(shape, F32)] + [jax.ShapeDtype...]
    ppermute x6 -> x15, starting transfers between devices: 1.27 us -> 3.26 us  [core_swap(): return lax.ppermute(value, 'core', [(0, 1), (1, 0)])]
    unnamed x10 -> x40, local copies, waits for them, and re-layouts: 4.91 us -> 3.59 us
  transfers between devices with their start and end apart: 20 -> 36, of which waited for: 9 -> 12; matrix products, arithmetic and copies ran while one was open for 2% -> 2% of each run, Pallas kernels for 12% -> 16%
where the time goes in v4:
time: 103 us; the launch traced here: 102 us
  starting transfers between devices  40 us (39%)
  waiting for transfers between devices  19.6 us (19%)
  blocking collectives  18.5 us (18%)
  Pallas kernels  18 us (17%)
  local copies, waits for them, and re-layouts  4.57 us (4%)
  other arithmetic  1.05 us (1%)
    ppermute x17, starting transfers between devices, ring_shift(): lax.ppermute(value, axis, [(n, (n + steps) % count) for n in range(count)])  33.3 us
    all_to_all x1, blocking collectives, on_device(): received = lax.all_to_all(sent, ('z', 'y'), 0, 0, tiled=True)  18.5 us
    ppermute x17, waiting for transfers between devices, ring_shift(): lax.ppermute(value, axis, [(n, (n + steps) % count) for n in range(count)])  13.4 us
    pallas_call x2, Pallas kernels, project(): call(project_kernel, [jax.ShapeDtypeStruct(shape, F32)] + [jax.ShapeDtype...  10.3 us
    pallas_call x1, Pallas kernels, on_device(): call(attend_kernel, jax.ShapeDtypeStruct((tokens, row_width), BF16), 4 *...  5.03 us
    ppermute x4, waiting for transfers between devices, chip_shift(): return lax.ppermute(value, ('z', 'y', 'core'), pairs)  4.82 us
    unnamed x40, local copies, waits for them, and re-layouts  3.59 us
    ppermute x4, starting transfers between devices, chip_shift(): return lax.ppermute(value, ('z', 'y', 'core'), pairs)  3.4 us
  transfers between devices with their start and end apart: 36, of which 12 were waited for; matrix products, arithmetic and copies ran while one was open for 2% of the time, Pallas kernels for 16%

profile of v4, /device:TPU:8, one launch (start us, length us, event | category | flops | bytes accessed | tf_op | source)
XLA Modules:
  0.0 102.0 jit_solution(4243443395866517766)
XLA Ops:
  0.0 1.9 %collective-permute-start = (bf16[64,2048]{1,0:T(8,128)(2,1)}, bf16[64,2048]{1,0:T(8,128)(2,1)S(1)}, u32[]{:S(2)}, u32[]{:S(2)}) collective-permute-start(bf16[64,2048]{1,0:T(8,128)(2,1)} %refs_0_.3), channel_id=1, source_target_pairs={{0,32},{32,64},{64,96},{96,128},{128,160},{160,192},{192,224},{224... | collective-permute-start | bytes 786440 | tf_op jit(solution)/shard_map/ppermute | solution.py:182
  1.9 3.9 %collective-permute-start.1 = (bf16[64,2048]{1,0:T(8,128)(2,1)}, bf16[64,2048]{1,0:T(8,128)(2,1)S(1)}, u32[]{:S(2)}, u32[]{:S(2)}) collective-permute-start(bf16[64,2048]{1,0:T(8,128)(2,1)} %refs_0_.3), channel_id=1, source_target_pairs={{0,224},{32,0},{64,32},{96,64},{128,96},{160,128},{192,160},{224,1... | collective-permute-start | bytes 786440 | tf_op jit(solution)/shard_map/ppermute | solution.py:182
  5.9 0.8 copy-done.5
  6.7 0.8 copy-done.6
  7.6 1.7 %collective-permute-start.18 = (bf16[128,512]{1,0:T(8,128)(2,1)S(1)}, bf16[128,512]{1,0:T(8,128)(2,1)S(1)}, u32[]{:S(2)}, u32[]{:S(2)}) collective-permute-start(bf16[128,512]{1,0:T(8,128)(2,1)S(1)} %shard_map.65.refs_0_), channel_id=1, source_target_pairs={{0,8},{4,12},{8,16},{12,20},{16,24},{20,28},{24,32},{28,36},{32,40... | collective-permute-start | bytes 393224 | tf_op jit(solution)/shard_map/ppermute | solution.py:177
  9.2 0.8 collective-permute-start.19
  10.1 0.7 constant_dynamic-slice_fusion
  10.8 0.7 broadcast_select_fusion
  11.7 1.1 %collective-permute-done.18.refs_1_ = bf16[128,512]{1,0:T(8,128)(2,1)S(1)} collective-permute-done((bf16[128,512]{1,0:T(8,128)(2,1)S(1)}, bf16[128,512]{1,0:T(8,128)(2,1)S(1)}, u32[]{:S(2)}, u32[]{:S(2)}) %collective-permute-start.18) | collective-permute-done | bytes 131104 | tf_op jit(solution)/shard_map/ppermute | solution.py:177
  12.8 0.9 collective-permute-start.21
  13.7 3.0 %collective-permute-start.2 = (bf16[64,2048]{1,0:T(8,128)(2,1)S(1)}, bf16[64,2048]{1,0:T(8,128)(2,1)S(1)}, u32[]{:S(2)}, u32[]{:S(2)}) collective-permute-start(bf16[64,2048]{1,0:T(8,128)(2,1)S(1)} %collective-permute-done.refs_1_), channel_id=1, source_target_pairs={{0,32},{32,64},{64,96},{96,128},{128,160},{160,192},{192,224},{224... | collective-permute-start | bytes 786440 | tf_op jit(solution)/shard_map/ppermute | solution.py:182
  16.9 0.4 collective-permute-start.3
  17.4 3.7 %collective-permute-done.19.refs_2_ = bf16[128,512]{1,0:T(8,128)(2,1)S(1)} collective-permute-done((bf16[128,512]{1,0:T(8,128)(2,1)S(1)}, bf16[128,512]{1,0:T(8,128)(2,1)S(1)}, u32[]{:S(2)}, u32[]{:S(2)}) %collective-permute-start.19) | collective-permute-done | bytes 131104 | tf_op jit(solution)/shard_map/ppermute | solution.py:177
  21.1 0.5 collective-permute-start.23
  21.6 1.0 %copy-done = bf16[128,2048]{1,0:T(8,128)(2,1)S(1)} copy-done((bf16[128,2048]{1,0:T(8,128)(2,1)S(1)}, bf16[128,2048]{1,0:T(8,128)(2,1)}, u32[]{:S(2)}) %copy-start) | copy-done | bytes 524312
  22.6 1.0 shard_map.64
  23.7 0.5 collective-permute-start.24
  24.3 2.0 %collective-permute-done.2.refs_3_ = bf16[64,2048]{1,0:T(8,128)(2,1)S(1)} collective-permute-done((bf16[64,2048]{1,0:T(8,128)(2,1)S(1)}, bf16[64,2048]{1,0:T(8,128)(2,1)S(1)}, u32[]{:S(2)}, u32[]{:S(2)}) %collective-permute-start.2) | collective-permute-done | bytes 262176 | tf_op jit(solution)/shard_map/ppermute | solution.py:182
  26.3 0.6 collective-permute-start.8
  27.2 0.5 collective-permute-done.26.refs_9_
  27.6 5.0 %shard_map.66.refs_18_ = bf16[128,2048]{1,0:T(8,128)(2,1)S(1)} custom-call(f32[128,1280]{1,0:T(8,128)S(1)} %get-tuple-element.21.bias_ref, bf16[64,2048]{1,0:T(8,128)(2,1)S(1)} %get-tuple-element.22.keep_ref, bf16[64,2048]{1,0:T(8,128)(2,1)S(1)} %collective-permute-done.17.got_ref, bf16[128,512]{1,0:T(8,128)(2,1)S(1)} %shard_map.65.refs_0_, ...), custom_call_target="tpu_custom_call" | custom-call | flops 1342177280 | bytes 8388608 | tf_op jit(solution)/shard_map/pallas_call | solution.py:238
  32.7 4.3 %collective-permute-start.27 = (bf16[128,2048]{1,0:T(8,128)(2,1)S(1)}, bf16[128,2048]{1,0:T(8,128)(2,1)S(1)}, u32[]{:S(2)}, u32[]{:S(2)}) collective-permute-start(bf16[128,2048]{1,0:T(8,128)(2,1)S(1)} %shard_map.66.refs_18_), channel_id=1, source_target_pairs={{0,24},{8,0},{16,8},{24,16},{1,25},{9,1},{17,9},{25,17},{2,26},{10... | collective-permute-start | bytes 1572872 | tf_op jit(solution)/shard_map/ppermute | solution.py:182
  36.9 2.8 %collective-permute-start.5 = (bf16[64,2048]{1,0:T(8,128)(2,1)S(1)}, bf16[64,2048]{1,0:T(8,128)(2,1)S(1)}, u32[]{:S(2)}, u32[]{:S(2)}) collective-permute-start(bf16[64,2048]{1,0:T(8,128)(2,1)S(1)} %collective-permute-done.3.refs_4_), channel_id=1, source_target_pairs={{0,224},{32,0},{64,32},{96,64},{128,96},{160,128},{192,160},{224,1... | collective-permute-start | bytes 786440 | tf_op jit(solution)/shard_map/ppermute | solution.py:182
  39.8 0.6 collective-permute-start.11
  40.4 4.8 %collective-permute-done.5.refs_6_ = bf16[64,2048]{1,0:T(8,128)(2,1)S(1)} collective-permute-done((bf16[64,2048]{1,0:T(8,128)(2,1)S(1)}, bf16[64,2048]{1,0:T(8,128)(2,1)S(1)}, u32[]{:S(2)}, u32[]{:S(2)}) %collective-permute-start.5) | collective-permute-done | bytes 262176 | tf_op jit(solution)/shard_map/ppermute | solution.py:182
  45.3 1.2 %collective-permute-start.6 = (bf16[32,2048]{1,0:T(8,128)(2,1)S(1)}, bf16[32,2048]{1,0:T(8,128)(2,1)S(1)}, u32[]{:S(2)}, u32[]{:S(2)}) collective-permute-start(bf16[32,2048]{1,0:T(8,128)(2,1)S(1)} %slice.8), channel_id=1, source_target_pairs={{0,32},{32,64},{64,96},{96,128},{128,160},{160,192},{192,224},{224... | collective-permute-start | bytes 393224 | tf_op jit(solution)/shard_map/ppermute | solution.py:182
  46.4 2.7 %collective-permute-start.7 = (bf16[32,2048]{1,0:T(8,128)(2,1)S(1)}, bf16[32,2048]{1,0:T(8,128)(2,1)S(1)}, u32[]{:S(2)}, u32[]{:S(2)}) collective-permute-start(bf16[32,2048]{1,0:T(8,128)(2,1)S(1)} %slice.9), channel_id=1, source_target_pairs={{0,224},{32,0},{64,32},{96,64},{128,96},{160,128},{192,160},{224,1... | collective-permute-start | bytes 393224 | tf_op jit(solution)/shard_map/ppermute | solution.py:182
  49.4 1.7 %collective-permute-done.28.refs_20_ = bf16[128,2048]{1,0:T(8,128)(2,1)S(1)} collective-permute-done((bf16[128,2048]{1,0:T(8,128)(2,1)S(1)}, bf16[128,2048]{1,0:T(8,128)(2,1)S(1)}, u32[]{:S(2)}, u32[]{:S(2)}) %collective-permute-start.28) | collective-permute-done | bytes 524320 | tf_op jit(solution)/shard_map/ppermute | solution.py:182
  51.2 2.7 %collective-permute-start.32 = (bf16[128,2048]{1,0:T(8,128)(2,1)S(1)}, bf16[128,2048]{1,0:T(8,128)(2,1)S(1)}, u32[]{:S(2)}, u32[]{:S(2)}) collective-permute-start(bf16[128,2048]{1,0:T(8,128)(2,1)S(1)} %shard_map.66.refs_18_), channel_id=1, source_target_pairs={{0,16},{8,24},{16,0},{24,8},{1,17},{9,25},{17,1},{25,9},{2,18},{10... | collective-permute-start | bytes 1572872 | tf_op jit(solution)/shard_map/ppermute | solution.py:182
  53.9 0.6 collective-permute-start.16
  54.5 0.6 collective-permute-done.15.refs_16_
  55.2 0.3 collective-permute-done.16.refs_17_
  55.5 5.5 %shard_map.67 = (f32[384,256]{1,0:T(8,128)}, bf16[384,256]{1,0:T(8,128)(2,1)S(1)}, bf16[384,256]{1,0:T(8,128)(2,1)S(1)}, bf16[384,256]{1,0:T(8,128)(2,1)S(1)}) custom-call(s32[3]{0:T(128)S(1)} %pad_add_fusion.1.place_ref, bf16[64,2048]{1,0:T(8,128)(2,1)S(1)} %copy-done.2, bf16[64,2048]{1,0:T(8,128)(2,1)S(1)} %collective-permute-done.refs_1_, ...), custom_call_target="tpu_custom_call" | custom-call | flops 1610612736 | bytes 6750208 | tf_op jit(solution)/shard_map/pallas_call | solution.py:262
  60.9 1.6 %collective-permute-start.29 = (bf16[384,256]{1,0:T(8,128)(2,1)S(1)}, bf16[384,256]{1,0:T(8,128)(2,1)S(1)}, u32[]{:S(2)}, u32[]{:S(2)}) collective-permute-start(bf16[384,256]{1,0:T(8,128)(2,1)S(1)} %get-tuple-element.25), channel_id=1, source_target_pairs={{0,1},{1,2},{2,3},{3,0},{4,5},{5,6},{6,7},{7,4},{8,9},{9,10},{10,1... | collective-permute-start | bytes 589832 | tf_op jit(solution)/shard_map/ppermute | solution.py:182
  62.5 1.7 %collective-permute-start.30 = (bf16[384,256]{1,0:T(8,128)(2,1)S(1)}, bf16[384,256]{1,0:T(8,128)(2,1)S(1)}, u32[]{:S(2)}, u32[]{:S(2)}) collective-permute-start(bf16[384,256]{1,0:T(8,128)(2,1)S(1)} %get-tuple-element.26), channel_id=1, source_target_pairs={{0,3},{1,0},{2,1},{3,2},{4,7},{5,4},{6,5},{7,6},{8,11},{9,8},{10,9... | collective-permute-start | bytes 589832 | tf_op jit(solution)/shard_map/ppermute | solution.py:182
  64.3 1.8 %collective-permute-start.31 = (bf16[384,256]{1,0:T(8,128)(2,1)S(1)}, bf16[384,256]{1,0:T(8,128)(2,1)S(1)}, u32[]{:S(2)}, u32[]{:S(2)}) collective-permute-start(bf16[384,256]{1,0:T(8,128)(2,1)S(1)} %get-tuple-element.27), channel_id=1, source_target_pairs={{0,2},{1,3},{2,0},{3,1},{4,6},{5,7},{6,4},{7,5},{8,10},{9,11},{10,... | collective-permute-start | bytes 589832 | tf_op jit(solution)/shard_map/ppermute | solution.py:182
  66.1 1.0 collective-permute-done.32.refs_18_
  67.1 0.8 copy-done.10
  67.9 4.8 %shard_map.68 = (f32[128,256]{1,0:T(8,128)S(1)}, bf16[128,256]{1,0:T(8,128)(2,1)S(1)}, bf16[128,256]{1,0:T(8,128)(2,1)S(1)}, bf16[128,256]{1,0:T(8,128)(2,1)S(1)}) custom-call(s32[3]{0:T(128)S(1)} %pad_add_fusion.1.place_ref, bf16[64,2048]{1,0:T(8,128)(2,1)S(1)} %copy-done.2, bf16[64,2048]{1,0:T(8,128)(2,1)S(1)} %collective-permute-done.refs_1_, ...), custom_call_target="tpu_custom_call" | custom-call | flops 536870912 | bytes 5046272 | tf_op jit(solution)/shard_map/pallas_call | solution.py:262
  72.7 1.6 %collective-permute-start.33 = (bf16[128,256]{1,0:T(8,128)(2,1)S(1)}, bf16[128,256]{1,0:T(8,128)(2,1)S(1)}, u32[]{:S(2)}, u32[]{:S(2)}) collective-permute-start(bf16[128,256]{1,0:T(8,128)(2,1)S(1)} %get-tuple-element.30), channel_id=1, source_target_pairs={{0,1},{1,2},{2,3},{3,0},{4,5},{5,6},{6,7},{7,4},{8,9},{9,10},{10,1... | collective-permute-start | bytes 196616 | tf_op jit(solution)/shard_map/ppermute | solution.py:182
  74.3 1.7 %collective-permute-start.34 = (bf16[128,256]{1,0:T(8,128)(2,1)S(1)}, bf16[128,256]{1,0:T(8,128)(2,1)S(1)}, u32[]{:S(2)}, u32[]{:S(2)}) collective-permute-start(bf16[128,256]{1,0:T(8,128)(2,1)S(1)} %get-tuple-element.31), channel_id=1, source_target_pairs={{0,3},{1,0},{2,1},{3,2},{4,7},{5,4},{6,5},{7,6},{8,11},{9,8},{10,9... | collective-permute-start | bytes 196616 | tf_op jit(solution)/shard_map/ppermute | solution.py:182
  76.0 1.8 %collective-permute-start.35 = (bf16[128,256]{1,0:T(8,128)(2,1)S(1)}, bf16[128,256]{1,0:T(8,128)(2,1)S(1)}, u32[]{:S(2)}, u32[]{:S(2)}) collective-permute-start(bf16[128,256]{1,0:T(8,128)(2,1)S(1)} %get-tuple-element.32), channel_id=1, source_target_pairs={{0,2},{1,3},{2,0},{3,1},{4,6},{5,7},{6,4},{7,5},{8,10},{9,11},{10,... | collective-permute-start | bytes 196616 | tf_op jit(solution)/shard_map/ppermute | solution.py:182
  77.9 0.3 collective-permute-done.33.refs_5_
  78.3 0.7 collective-permute-done.34.refs_6_
  78.9 2.9 %collective-permute-done.35.refs_7_ = bf16[128,256]{1,0:T(8,128)(2,1)S(1)} collective-permute-done((bf16[128,256]{1,0:T(8,128)(2,1)S(1)}, bf16[128,256]{1,0:T(8,128)(2,1)S(1)}, u32[]{:S(2)}, u32[]{:S(2)}) %collective-permute-start.35) | collective-permute-done | bytes 65568 | tf_op jit(solution)/shard_map/ppermute | solution.py:182
  81.8 1.0 shard_map.69
  82.8 18.5 %all_to_all.5.x_ref = bf16[32,16,256]{2,1,0:T(8,128)(2,1)S(1)} all-to-all(bf16[32,16,256]{2,1,0:T(8,128)(2,1)S(1)} %shard_map.69), channel_id=1, replica_groups=mesh['z'=8,'y'=4,'core'=2,'tp'=4] {'z','y'}, dimensions={0} | all-to-all | bytes 524288 | tf_op jit(solution)/shard_map/all_to_all | solution.py:289
  101.3 0.7 shard_map.70
  (84 shorter events, 1.5 us)
Async XLA Ops:
  0.0 13.7 %collective-permute-start = (bf16[64,2048]{1,0:T(8,128)(2,1)}, bf16[64,2048]{1,0:T(8,128)(2,1)S(1)}, u32[]{:S(2)}, u32[]{:S(2)}) collective-permute-start(bf16[64,2048]{1,0:T(8,128)(2,1)} %refs_0_.3), channel_id=1, source_target_pairs={{0,32},{32,64},{64,96},{96,128},{128,160},{160,192},{192,224},{224... | collective-permute-start | bytes 786440 | tf_op jit(solution)/shard_map/ppermute | solution.py:182
  1.9 15.0 %collective-permute-start.1 = (bf16[64,2048]{1,0:T(8,128)(2,1)}, bf16[64,2048]{1,0:T(8,128)(2,1)S(1)}, u32[]{:S(2)}, u32[]{:S(2)}) collective-permute-start(bf16[64,2048]{1,0:T(8,128)(2,1)} %refs_0_.3), channel_id=1, source_target_pairs={{0,224},{32,0},{64,32},{96,64},{128,96},{160,128},{192,160},{224,1... | collective-permute-start | bytes 786440 | tf_op jit(solution)/shard_map/ppermute | solution.py:182
  7.6 5.2 %collective-permute-start.18 = (bf16[128,512]{1,0:T(8,128)(2,1)S(1)}, bf16[128,512]{1,0:T(8,128)(2,1)S(1)}, u32[]{:S(2)}, u32[]{:S(2)}) collective-permute-start(bf16[128,512]{1,0:T(8,128)(2,1)S(1)} %shard_map.65.refs_0_), channel_id=1, source_target_pairs={{0,8},{4,12},{8,16},{12,20},{16,24},{20,28},{24,32},{28,36},{32,40... | collective-permute-start | bytes 393224 | tf_op jit(solution)/shard_map/ppermute | solution.py:177
  9.2 11.9 %collective-permute-start.19 = (bf16[128,512]{1,0:T(8,128)(2,1)S(1)}, bf16[128,512]{1,0:T(8,128)(2,1)S(1)}, u32[]{:S(2)}, u32[]{:S(2)}) collective-permute-start(bf16[128,512]{1,0:T(8,128)(2,1)S(1)} %shard_map.65.refs_0_), channel_id=1, source_target_pairs={{0,16},{4,20},{8,24},{12,28},{16,32},{20,36},{24,40},{28,44},{32,4... | collective-permute-start | bytes 393224 | tf_op jit(solution)/shard_map/ppermute | solution.py:177
  10.0 11.1 %collective-permute-start.20 = (bf16[128,512]{1,0:T(8,128)(2,1)S(1)}, bf16[128,512]{1,0:T(8,128)(2,1)S(1)}, u32[]{:S(2)}, u32[]{:S(2)}) collective-permute-start(bf16[128,512]{1,0:T(8,128)(2,1)S(1)} %shard_map.65.refs_0_), channel_id=1, source_target_pairs={{0,24},{4,28},{8,32},{12,36},{16,40},{20,44},{24,48},{28,52},{32,5... | collective-permute-start | bytes 393224 | tf_op jit(solution)/shard_map/ppermute | solution.py:177
  12.8 10.8 %collective-permute-start.21 = (bf16[128,512]{1,0:T(8,128)(2,1)S(1)}, bf16[128,512]{1,0:T(8,128)(2,1)S(1)}, u32[]{:S(2)}, u32[]{:S(2)}) collective-permute-start(bf16[128,512]{1,0:T(8,128)(2,1)S(1)} %shard_map.65.refs_0_), channel_id=1, source_target_pairs={{0,32},{4,36},{8,40},{12,44},{16,48},{20,52},{24,56},{28,60},{32,6... | collective-permute-start | bytes 393224 | tf_op jit(solution)/shard_map/ppermute | solution.py:177
  13.7 12.6 %collective-permute-start.2 = (bf16[64,2048]{1,0:T(8,128)(2,1)S(1)}, bf16[64,2048]{1,0:T(8,128)(2,1)S(1)}, u32[]{:S(2)}, u32[]{:S(2)}) collective-permute-start(bf16[64,2048]{1,0:T(8,128)(2,1)S(1)} %collective-permute-done.refs_1_), channel_id=1, source_target_pairs={{0,32},{32,64},{64,96},{96,128},{128,160},{160,192},{192,224},{224... | collective-permute-start | bytes 786440 | tf_op jit(solution)/shard_map/ppermute | solution.py:182
  16.9 9.4 %collective-permute-start.3 = (bf16[64,2048]{1,0:T(8,128)(2,1)S(1)}, bf16[64,2048]{1,0:T(8,128)(2,1)S(1)}, u32[]{:S(2)}, u32[]{:S(2)}) collective-permute-start(bf16[64,2048]{1,0:T(8,128)(2,1)S(1)} %collective-permute-done.1.refs_2_), channel_id=1, source_target_pairs={{0,224},{32,0},{64,32},{96,64},{128,96},{160,128},{192,160},{224,1... | collective-permute-start | bytes 786440 | tf_op jit(solution)/shard_map/ppermute | solution.py:182
  21.1 2.6 %collective-permute-start.22 = (bf16[128,512]{1,0:T(8,128)(2,1)S(1)}, bf16[128,512]{1,0:T(8,128)(2,1)S(1)}, u32[]{:S(2)}, u32[]{:S(2)}) collective-permute-start(bf16[128,512]{1,0:T(8,128)(2,1)S(1)} %shard_map.65.refs_0_), channel_id=1, source_target_pairs={{0,4},{4,0},{1,5},{5,1},{2,6},{6,2},{3,7},{7,3},{8,12},{12,8},{9,1... | collective-permute-start | bytes 393224 | tf_op jit(solution)/shard_map/ppermute | solution.py:186
  21.1 3.1 %collective-permute-start.23 = (bf16[128,512]{1,0:T(8,128)(2,1)S(1)}, bf16[128,512]{1,0:T(8,128)(2,1)S(1)}, u32[]{:S(2)}, u32[]{:S(2)}) collective-permute-start(bf16[128,512]{1,0:T(8,128)(2,1)S(1)} %collective-permute-done.18.refs_1_), channel_id=1, source_target_pairs={{0,4},{4,0},{1,5},{5,1},{2,6},{6,2},{3,7},{7,3},{8,12},{12,8},{9,1... | collective-permute-start | bytes 393224 | tf_op jit(solution)/shard_map/ppermute | solution.py:186
  23.6 4.0 %collective-permute-start.17 = (bf16[64,2048]{1,0:T(8,128)(2,1)S(1)}, bf16[64,2048]{1,0:T(8,128)(2,1)S(1)}, u32[]{:S(2)}, u32[]{:S(2)}) collective-permute-start(bf16[64,2048]{1,0:T(8,128)(2,1)S(1)} %get-tuple-element.23), channel_id=1, source_target_pairs={{0,4},{4,0},{1,5},{5,1},{2,6},{6,2},{3,7},{7,3},{8,12},{12,8},{9,1... | collective-permute-start | bytes 786440 | tf_op jit(solution)/shard_map/ppermute | solution.py:186
  23.7 3.2 %collective-permute-start.24 = (bf16[128,512]{1,0:T(8,128)(2,1)S(1)}, bf16[128,512]{1,0:T(8,128)(2,1)S(1)}, u32[]{:S(2)}, u32[]{:S(2)}) collective-permute-start(bf16[128,512]{1,0:T(8,128)(2,1)S(1)} %collective-permute-done.19.refs_2_), channel_id=1, source_target_pairs={{0,4},{4,0},{1,5},{5,1},{2,6},{6,2},{3,7},{7,3},{8,12},{12,8},{9,1... | collective-permute-start | bytes 393224 | tf_op jit(solution)/shard_map/ppermute | solution.py:186
  24.2 2.8 %collective-permute-start.25 = (bf16[128,512]{1,0:T(8,128)(2,1)S(1)}, bf16[128,512]{1,0:T(8,128)(2,1)S(1)}, u32[]{:S(2)}, u32[]{:S(2)}) collective-permute-start(bf16[128,512]{1,0:T(8,128)(2,1)S(1)} %collective-permute-done.20.refs_3_), channel_id=1, source_target_pairs={{0,4},{4,0},{1,5},{5,1},{2,6},{6,2},{3,7},{7,3},{8,12},{12,8},{9,1... | collective-permute-start | bytes 393224 | tf_op jit(solution)/shard_map/ppermute | solution.py:186
  26.3 13.5 %copy-start.3 = (bf16[64,2048]{1,0:T(8,128)(2,1)}, bf16[64,2048]{1,0:T(8,128)(2,1)S(1)}, u32[]{:S(2)}) copy-start(bf16[64,2048]{1,0:T(8,128)(2,1)S(1)} %collective-permute-done.2.refs_3_) | copy-start | bytes 786436
  26.3 1.3 %collective-permute-start.26 = (bf16[128,512]{1,0:T(8,128)(2,1)S(1)}, bf16[128,512]{1,0:T(8,128)(2,1)S(1)}, u32[]{:S(2)}, u32[]{:S(2)}) collective-permute-start(bf16[128,512]{1,0:T(8,128)(2,1)S(1)} %collective-permute-done.21.refs_4_), channel_id=1, source_target_pairs={{0,4},{4,0},{1,5},{5,1},{2,6},{6,2},{3,7},{7,3},{8,12},{12,8},{9,1... | collective-permute-start | bytes 393224 | tf_op jit(solution)/shard_map/ppermute | solution.py:186
  26.3 18.9 %copy-start.11 = (bf16[64,2048]{1,0:T(8,128)(2,1)}, bf16[64,2048]{1,0:T(8,128)(2,1)S(1)}, u32[]{:S(2)}) copy-start(bf16[64,2048]{1,0:T(8,128)(2,1)S(1)} %collective-permute-done.3.refs_4_) | copy-start | bytes 786436
  26.3 10.6 %collective-permute-start.8 = (bf16[64,2048]{1,0:T(8,128)(2,1)S(1)}, bf16[64,2048]{1,0:T(8,128)(2,1)S(1)}, u32[]{:S(2)}, u32[]{:S(2)}) collective-permute-start(bf16[64,2048]{1,0:T(8,128)(2,1)S(1)} %copy-done.2), channel_id=1, source_target_pairs={{0,4},{4,0},{1,5},{5,1},{2,6},{6,2},{3,7},{7,3},{8,12},{12,8},{9,1... | collective-permute-start | bytes 786440 | tf_op jit(solution)/shard_map/ppermute | solution.py:186
  26.9 12.9 %collective-permute-start.10 = (bf16[64,2048]{1,0:T(8,128)(2,1)S(1)}, bf16[64,2048]{1,0:T(8,128)(2,1)S(1)}, u32[]{:S(2)}, u32[]{:S(2)}) collective-permute-start(bf16[64,2048]{1,0:T(8,128)(2,1)S(1)} %collective-permute-done.1.refs_2_), channel_id=1, source_target_pairs={{0,4},{4,0},{1,5},{5,1},{2,6},{6,2},{3,7},{7,3},{8,12},{12,8},{9,1... | collective-permute-start | bytes 786440 | tf_op jit(solution)/shard_map/ppermute | solution.py:186
  27.0 12.8 %collective-permute-start.4 = (bf16[64,2048]{1,0:T(8,128)(2,1)S(1)}, bf16[64,2048]{1,0:T(8,128)(2,1)S(1)}, u32[]{:S(2)}, u32[]{:S(2)}) collective-permute-start(bf16[64,2048]{1,0:T(8,128)(2,1)S(1)} %collective-permute-done.2.refs_3_), channel_id=1, source_target_pairs={{0,32},{32,64},{64,96},{96,128},{128,160},{160,192},{192,224},{224... | collective-permute-start | bytes 786440 | tf_op jit(solution)/shard_map/ppermute | solution.py:182
  32.7 22.8 %copy-start.7 = (bf16[128,2048]{1,0:T(8,128)(2,1)}, bf16[128,2048]{1,0:T(8,128)(2,1)S(1)}, u32[]{:S(2)}) copy-start(bf16[128,2048]{1,0:T(8,128)(2,1)S(1)} %shard_map.66.refs_18_) | copy-start | bytes 1572868
  32.7 16.5 %collective-permute-start.27 = (bf16[128,2048]{1,0:T(8,128)(2,1)S(1)}, bf16[128,2048]{1,0:T(8,128)(2,1)S(1)}, u32[]{:S(2)}, u32[]{:S(2)}) collective-permute-start(bf16[128,2048]{1,0:T(8,128)(2,1)S(1)} %shard_map.66.refs_18_), channel_id=1, source_target_pairs={{0,24},{8,0},{16,8},{24,16},{1,25},{9,1},{17,9},{25,17},{2,26},{10... | collective-permute-start | bytes 1572872 | tf_op jit(solution)/shard_map/ppermute | solution.py:182
  36.9 14.2 %collective-permute-start.28 = (bf16[128,2048]{1,0:T(8,128)(2,1)S(1)}, bf16[128,2048]{1,0:T(8,128)(2,1)S(1)}, u32[]{:S(2)}, u32[]{:S(2)}) collective-permute-start(bf16[128,2048]{1,0:T(8,128)(2,1)S(1)} %shard_map.66.refs_18_), channel_id=1, source_target_pairs={{0,8},{8,16},{16,24},{24,0},{1,9},{9,17},{17,25},{25,1},{2,10},{10... | collective-permute-start | bytes 1572872 | tf_op jit(solution)/shard_map/ppermute | solution.py:182
  36.9 16.9 %copy-start.12 = (bf16[64,2048]{1,0:T(8,128)(2,1)}, bf16[64,2048]{1,0:T(8,128)(2,1)S(1)}, u32[]{:S(2)}) copy-start(bf16[64,2048]{1,0:T(8,128)(2,1)S(1)} %collective-permute-done.8.refs_9_) | copy-start | bytes 786436
  36.9 8.3 %collective-permute-start.5 = (bf16[64,2048]{1,0:T(8,128)(2,1)S(1)}, bf16[64,2048]{1,0:T(8,128)(2,1)S(1)}, u32[]{:S(2)}, u32[]{:S(2)}) collective-permute-start(bf16[64,2048]{1,0:T(8,128)(2,1)S(1)} %collective-permute-done.3.refs_4_), channel_id=1, source_target_pairs={{0,224},{32,0},{64,32},{96,64},{128,96},{160,128},{192,160},{224,1... | collective-permute-start | bytes 786440 | tf_op jit(solution)/shard_map/ppermute | solution.py:182
  39.8 11.3 %copy-start.13 = (bf16[64,2048]{1,0:T(8,128)(2,1)}, bf16[64,2048]{1,0:T(8,128)(2,1)S(1)}, u32[]{:S(2)}) copy-start(bf16[64,2048]{1,0:T(8,128)(2,1)S(1)} %collective-permute-done.10.refs_11_) | copy-start | bytes 786436
  39.8 5.5 %collective-permute-start.9 = (bf16[64,2048]{1,0:T(8,128)(2,1)S(1)}, bf16[64,2048]{1,0:T(8,128)(2,1)S(1)}, u32[]{:S(2)}, u32[]{:S(2)}) collective-permute-start(bf16[64,2048]{1,0:T(8,128)(2,1)S(1)} %collective-permute-done.refs_1_), channel_id=1, source_target_pairs={{0,4},{4,0},{1,5},{5,1},{2,6},{6,2},{3,7},{7,3},{8,12},{12,8},{9,1... | collective-permute-start | bytes 786440 | tf_op jit(solution)/shard_map/ppermute | solution.py:186
  39.8 15.6 %copy-start.8 = (bf16[64,2048]{1,0:T(8,128)(2,1)}, bf16[64,2048]{1,0:T(8,128)(2,1)S(1)}, u32[]{:S(2)}) copy-start(bf16[64,2048]{1,0:T(8,128)(2,1)S(1)} %collective-permute-done.4.refs_5_) | copy-start | bytes 786436
  39.8 6.6 %collective-permute-start.11 = (bf16[64,2048]{1,0:T(8,128)(2,1)S(1)}, bf16[64,2048]{1,0:T(8,128)(2,1)S(1)}, u32[]{:S(2)}, u32[]{:S(2)}) collective-permute-start(bf16[64,2048]{1,0:T(8,128)(2,1)S(1)} %collective-permute-done.2.refs_3_), channel_id=1, source_target_pairs={{0,4},{4,0},{1,5},{5,1},{2,6},{6,2},{3,7},{7,3},{8,12},{12,8},{9,1... | collective-permute-start | bytes 786440 | tf_op jit(solution)/shard_map/ppermute | solution.py:186
  45.2 10.2 %copy-start.9 = (bf16[64,2048]{1,0:T(8,128)(2,1)}, bf16[64,2048]{1,0:T(8,128)(2,1)S(1)}, u32[]{:S(2)}) copy-start(bf16[64,2048]{1,0:T(8,128)(2,1)S(1)} %collective-permute-done.5.refs_6_) | copy-start | bytes 786436
  45.2 5.9 %collective-permute-start.12 = (bf16[64,2048]{1,0:T(8,128)(2,1)S(1)}, bf16[64,2048]{1,0:T(8,128)(2,1)S(1)}, u32[]{:S(2)}, u32[]{:S(2)}) collective-permute-start(bf16[64,2048]{1,0:T(8,128)(2,1)S(1)} %collective-permute-done.3.refs_4_), channel_id=1, source_target_pairs={{0,4},{4,0},{1,5},{5,1},{2,6},{6,2},{3,7},{7,3},{8,12},{12,8},{9,1... | collective-permute-start | bytes 786440 | tf_op jit(solution)/shard_map/ppermute | solution.py:186
  45.3 10.2 %copy-start.14 = (bf16[64,2048]{1,0:T(8,128)(2,1)}, bf16[64,2048]{1,0:T(8,128)(2,1)S(1)}, u32[]{:S(2)}) copy-start(bf16[64,2048]{1,0:T(8,128)(2,1)S(1)} %collective-permute-done.9.refs_10_) | copy-start | bytes 786436
  45.3 8.5 %collective-permute-start.6 = (bf16[32,2048]{1,0:T(8,128)(2,1)S(1)}, bf16[32,2048]{1,0:T(8,128)(2,1)S(1)}, u32[]{:S(2)}, u32[]{:S(2)}) collective-permute-start(bf16[32,2048]{1,0:T(8,128)(2,1)S(1)} %slice.8), channel_id=1, source_target_pairs={{0,32},{32,64},{64,96},{96,128},{128,160},{160,192},{192,224},{224... | collective-permute-start | bytes 393224 | tf_op jit(solution)/shard_map/ppermute | solution.py:182
  46.4 4.7 %copy-start.15 = (bf16[64,2048]{1,0:T(8,128)(2,1)}, bf16[64,2048]{1,0:T(8,128)(2,1)S(1)}, u32[]{:S(2)}) copy-start(bf16[64,2048]{1,0:T(8,128)(2,1)S(1)} %collective-permute-done.11.refs_12_) | copy-start | bytes 786436
  46.4 7.4 %collective-permute-start.7 = (bf16[32,2048]{1,0:T(8,128)(2,1)S(1)}, bf16[32,2048]{1,0:T(8,128)(2,1)S(1)}, u32[]{:S(2)}, u32[]{:S(2)}) collective-permute-start(bf16[32,2048]{1,0:T(8,128)(2,1)S(1)} %slice.9), channel_id=1, source_target_pairs={{0,224},{32,0},{64,32},{96,64},{128,96},{160,128},{192,160},{224,1... | collective-permute-start | bytes 393224 | tf_op jit(solution)/shard_map/ppermute | solution.py:182
  49.2 4.7 %copy-start.17 = (bf16[128,2048]{1,0:T(8,128)(2,1)}, bf16[128,2048]{1,0:T(8,128)(2,1)S(1)}, u32[]{:S(2)}) copy-start(bf16[128,2048]{1,0:T(8,128)(2,1)S(1)} %collective-permute-done.27.refs_19_) | copy-start | bytes 1572868
  49.2 6.3 %collective-permute-start.13 = (bf16[64,2048]{1,0:T(8,128)(2,1)S(1)}, bf16[64,2048]{1,0:T(8,128)(2,1)}, u32[]{:S(2)}, u32[]{:S(2)}) collective-permute-start(bf16[64,2048]{1,0:T(8,128)(2,1)S(1)} %collective-permute-done.4.refs_5_), channel_id=1, source_target_pairs={{0,4},{4,0},{1,5},{5,1},{2,6},{6,2},{3,7},{7,3},{8,12},{12,8},{9,1... | collective-permute-start | bytes 786440 | tf_op jit(solution)/shard_map/ppermute | solution.py:186
  51.1 4.3 %collective-permute-start.14 = (bf16[64,2048]{1,0:T(8,128)(2,1)S(1)}, bf16[64,2048]{1,0:T(8,128)(2,1)}, u32[]{:S(2)}, u32[]{:S(2)}) collective-permute-start(bf16[64,2048]{1,0:T(8,128)(2,1)S(1)} %collective-permute-done.5.refs_6_), channel_id=1, source_target_pairs={{0,4},{4,0},{1,5},{5,1},{2,6},{6,2},{3,7},{7,3},{8,12},{12,8},{9,1... | collective-permute-start | bytes 786440 | tf_op jit(solution)/shard_map/ppermute | solution.py:186
  51.2 15.9 %collective-permute-start.32 = (bf16[128,2048]{1,0:T(8,128)(2,1)S(1)}, bf16[128,2048]{1,0:T(8,128)(2,1)S(1)}, u32[]{:S(2)}, u32[]{:S(2)}) collective-permute-start(bf16[128,2048]{1,0:T(8,128)(2,1)S(1)} %shard_map.66.refs_18_), channel_id=1, source_target_pairs={{0,16},{8,24},{16,0},{24,8},{1,17},{9,25},{17,1},{25,9},{2,18},{10... | collective-permute-start | bytes 1572872 | tf_op jit(solution)/shard_map/ppermute | solution.py:182
  53.8 1.3 %collective-permute-start.15 = (bf16[32,2048]{1,0:T(8,128)(2,1)S(1)}, bf16[32,2048]{1,0:T(8,128)(2,1)S(1)}, u32[]{:S(2)}, u32[]{:S(2)}) collective-permute-start(bf16[32,2048]{1,0:T(8,128)(2,1)S(1)} %collective-permute-done.6.refs_7_), channel_id=1, source_target_pairs={{0,4},{4,0},{1,5},{5,1},{2,6},{6,2},{3,7},{7,3},{8,12},{12,8},{9,1... | collective-permute-start | bytes 393224 | tf_op jit(solution)/shard_map/ppermute | solution.py:186
  53.9 1.6 %collective-permute-start.16 = (bf16[32,2048]{1,0:T(8,128)(2,1)S(1)}, bf16[32,2048]{1,0:T(8,128)(2,1)S(1)}, u32[]{:S(2)}, u32[]{:S(2)}) collective-permute-start(bf16[32,2048]{1,0:T(8,128)(2,1)S(1)} %collective-permute-done.7.refs_8_), channel_id=1, source_target_pairs={{0,4},{4,0},{1,5},{5,1},{2,6},{6,2},{3,7},{7,3},{8,12},{12,8},{9,1... | collective-permute-start | bytes 393224 | tf_op jit(solution)/shard_map/ppermute | solution.py:186
  54.5 13.4 %copy-start.4 = (bf16[64,2048]{1,0:T(8,128)(2,1)S(1)}, bf16[64,2048]{1,0:T(8,128)(2,1)}, u32[]{:S(2)}) copy-start(bf16[64,2048]{1,0:T(8,128)(2,1)} %copy-done.3) | copy-start | bytes 786436
  60.9 15.1 %collective-permute-start.29 = (bf16[384,256]{1,0:T(8,128)(2,1)S(1)}, bf16[384,256]{1,0:T(8,128)(2,1)S(1)}, u32[]{:S(2)}, u32[]{:S(2)}) collective-permute-start(bf16[384,256]{1,0:T(8,128)(2,1)S(1)} %get-tuple-element.25), channel_id=1, source_target_pairs={{0,1},{1,2},{2,3},{3,0},{4,5},{5,6},{6,7},{7,4},{8,9},{9,10},{10,1... | collective-permute-start | bytes 589832 | tf_op jit(solution)/shard_map/ppermute | solution.py:182
  62.5 15.4 %collective-permute-start.30 = (bf16[384,256]{1,0:T(8,128)(2,1)S(1)}, bf16[384,256]{1,0:T(8,128)(2,1)S(1)}, u32[]{:S(2)}, u32[]{:S(2)}) collective-permute-start(bf16[384,256]{1,0:T(8,128)(2,1)S(1)} %get-tuple-element.26), channel_id=1, source_target_pairs={{0,3},{1,0},{2,1},{3,2},{4,7},{5,4},{6,5},{7,6},{8,11},{9,8},{10,9... | collective-permute-start | bytes 589832 | tf_op jit(solution)/shard_map/ppermute | solution.py:182
  64.3 17.5 %copy-start.1 = (f32[384,256]{1,0:T(8,128)S(1)}, f32[384,256]{1,0:T(8,128)}, u32[]{:S(2)}) copy-start(f32[384,256]{1,0:T(8,128)} %get-tuple-element.24.refs_0_) | copy-start | bytes 1179652
  64.3 13.6 %collective-permute-start.31 = (bf16[384,256]{1,0:T(8,128)(2,1)S(1)}, bf16[384,256]{1,0:T(8,128)(2,1)S(1)}, u32[]{:S(2)}, u32[]{:S(2)}) collective-permute-start(bf16[384,256]{1,0:T(8,128)(2,1)S(1)} %get-tuple-element.27), channel_id=1, source_target_pairs={{0,2},{1,3},{2,0},{3,1},{4,6},{5,7},{6,4},{7,5},{8,10},{9,11},{10,... | collective-permute-start | bytes 589832 | tf_op jit(solution)/shard_map/ppermute | solution.py:182
  72.7 5.6 %collective-permute-start.33 = (bf16[128,256]{1,0:T(8,128)(2,1)S(1)}, bf16[128,256]{1,0:T(8,128)(2,1)S(1)}, u32[]{:S(2)}, u32[]{:S(2)}) collective-permute-start(bf16[128,256]{1,0:T(8,128)(2,1)S(1)} %get-tuple-element.30), channel_id=1, source_target_pairs={{0,1},{1,2},{2,3},{3,0},{4,5},{5,6},{6,7},{7,4},{8,9},{9,10},{10,1... | collective-permute-start | bytes 196616 | tf_op jit(solution)/shard_map/ppermute | solution.py:182
  74.3 4.7 %collective-permute-start.34 = (bf16[128,256]{1,0:T(8,128)(2,1)S(1)}, bf16[128,256]{1,0:T(8,128)(2,1)S(1)}, u32[]{:S(2)}, u32[]{:S(2)}) collective-permute-start(bf16[128,256]{1,0:T(8,128)(2,1)S(1)} %get-tuple-element.31), channel_id=1, source_target_pairs={{0,3},{1,0},{2,1},{3,2},{4,7},{5,4},{6,5},{7,6},{8,11},{9,8},{10,9... | collective-permute-start | bytes 196616 | tf_op jit(solution)/shard_map/ppermute | solution.py:182
  76.0 5.8 %collective-permute-start.35 = (bf16[128,256]{1,0:T(8,128)(2,1)S(1)}, bf16[128,256]{1,0:T(8,128)(2,1)S(1)}, u32[]{:S(2)}, u32[]{:S(2)}) collective-permute-start(bf16[128,256]{1,0:T(8,128)(2,1)S(1)} %get-tuple-element.32), channel_id=1, source_target_pairs={{0,2},{1,3},{2,0},{3,1},{4,6},{5,7},{6,4},{7,5},{8,10},{9,11},{10,... | collective-permute-start | bytes 196616 | tf_op jit(solution)/shard_map/ppermute | solution.py:182
  (8 other events, 13.3 us)

commit v5 on v3

--- a/solution.py
+++ b/solution.py
@@ -20,6 +20,8 @@
 CHIPS = NZ * NY
 REACH = 4
 KEYS = 2 * (REACH + 1) * BLOCK
+PROJECT_VMEM = 52
+OFFSETS = [0, 1, 2, 3, 4, -1, -2, -3]
 CHUNKS = [(0, 1, NY - 1), (2,)]
 
 
@@ -99,25 +101,41 @@
                 out_ref[:, c : c + HEAD] = attended[n * BLOCK : (n + 1) * BLOCK]
 
 
-def project_kernel(x_ref, w_ref, *refs):
-    *refs, sorted_ref, sems = refs
-    blocks, outs = refs[:-NX], refs[-NX:]
-    width = w_ref.shape[0] // NX
+def sort_kernel(place_ref, *refs):
+    *refs, sems = refs
+    count = NC * len(OFFSETS)
+    pieces, blocks, outs, sorted_ref = refs[:count], refs[count : -NX - 1], refs[-NX - 1 : -1], refs[-1]
+    z, x, core = place_ref[0], place_ref[1], place_ref[2]
+    rows = pieces[0].shape[0]
+    copies = []
+    for n, piece in enumerate(pieces):
+        side, offset = n // len(OFFSETS), OFFSETS[n % len(OFFSETS)]
+        source = (z + offset + NZ) % NZ
+        row = pl.multiple_of(source % 2 * 128 + (core + side) % NC * rows, rows)
+        target = sorted_ref.at[(source // 2 - x + NX) % NX, pl.ds(row, rows), :]
+        copies.append(pltpu.make_async_copy(piece, target, sems.at[n]))
+    fetch(copies)
+    project_kernel(sorted_ref, *blocks, *outs)
+
+
+def again_kernel(sorted_ref, *refs):
+    *refs, held_ref, sems = refs
     copies = [
-        pltpu.make_async_copy(
-            w_ref.at[pl.ds(pl.multiple_of((x_ref[0] + n) % NX * width, width), width), :],
-            sorted_ref.at[n],
-            sems.at[n],
-        )
-        for n in range(NX)
+        pltpu.make_async_copy(sorted_ref.at[n], held_ref.at[n], sems.at[n]) for n in range(NX)
     ]
     for copy in copies:
         copy.start()
-    rows = jnp.concatenate([ref[...] for ref in blocks], axis=0)
+    project_kernel(held_ref, *refs, copies=copies)
+
+
+def project_kernel(sorted_ref, *refs, copies=()):
+    blocks, outs = refs[:-NX], refs[-NX:]
+    attended = jnp.concatenate([ref[...] for ref in blocks], axis=0)
     for n, out in enumerate(outs):
-        copies[n].wait()
+        if copies:
+            copies[n].wait()
         out[...] = lax.dot_general(
-            rows, sorted_ref[n], (((1,), (1,)), ((), ())), preferred_element_type=F32
+            attended, sorted_ref[n], (((1,), (1,)), ((), ())), preferred_element_type=F32
         ).astype(out.dtype)
 
 
@@ -191,8 +209,9 @@
     smem = pl.BlockSpec(memory_space=pltpu.SMEM)
     hbm = pl.BlockSpec(memory_space=pltpu.HBM)
 
-    weight = lax.all_gather(out_weight, ("z", "core"), axis=0, tiled=True)
-    features = weight.shape[0]
+    down = [out_weight]
+    for _ in range(2):
+        down.append(ring_shift(down[-1], "z", -1))
 
     own = call(
         join_kernel,
@@ -204,7 +223,7 @@
         scratch_shapes=[pltpu.SemaphoreType.DMA((2,))],
     )(rotated_keys, value_vectors)
     mine = [own] + [chip_shift(own, s) for s in range(1, REACH + 1)]
-    other = [core_swap(v) for v in mine]
+    other = [core_swap(after(own, mine[1]))] + [core_swap(v) for v in mine[1:]]
 
     order = jnp.arange(doc_lengths.shape[0])
     ends = jnp.sum(jnp.where(order[None, :] <= order[:, None], doc_lengths[None, :], 0), axis=1)
@@ -224,7 +243,7 @@
         jnp.stack([index, at["core"]]),
         homes.astype(jnp.int32),
         ends.astype(jnp.int32),
-        queries,
+        after(queries, mine[1]),
     )
     attended = call(
         attend_kernel,
@@ -235,28 +254,54 @@
         out_specs=vmem,
     )(bias, keep, core_swap(give), *mine, *other)
     rows = {0: attended} | {d: ring_shift(attended, "y", -d) for d in (1, 3)}
-    rows[2] = ring_shift(after(attended, rows[1], rows[3]), "y", 2)
-
-    def project(blocks):
+    for _ in range(2):
+        down.append(ring_shift(down[-1], "z", -1))
+    up = [after(out_weight, mine[1])]
+    for _ in range(3):
+        up.append(ring_shift(up[-1], "z", 1))
+    middle = tokens // 2
+    far = [rows[NY - 1][:middle], rows[1][middle:]]
+    far = [ring_shift(far[0], "y", 1), ring_shift(far[1], "y", -1)]
+    rows = {d: [block] for d, block in rows.items()} | {2: far}
+    pieces = down + up[1:]
+    pieces += [core_swap(after(piece, attended)) for piece in pieces]
+    features = NZ * NC * out_weight.shape[0]
+    corner = jnp.stack([at["z"], at["tp"], at["core"]])
+
+    shares, weight = [], None
+    for chunk in CHUNKS:
+        blocks = [block for d in chunk for block in rows[d]]
         count = sum(block.shape[0] for block in blocks)
         shape = (count, features // NX)
-        shares = call(
-            project_kernel,
-            [jax.ShapeDtypeStruct(shape, F32)] + [jax.ShapeDtypeStruct(shape, BF16)] * 3,
-            2 * count * features * row_width,
-            (4 << 20) + count * (2 * row_width + 2560),
-            in_specs=[smem, hbm] + [vmem] * len(blocks),
-            out_specs=[vmem] * NX,
-            scratch_shapes=[
-                pltpu.VMEM((NX, features // NX, row_width), BF16),
-                pltpu.SemaphoreType.DMA((NX,)),
-            ],
-        )(at["tp"].reshape(1), weight, *blocks)
-        return [shares[0]] + [ring_shift(shares[d], "tp", d) for d in (1, 3, 2)]
-
-    shares = []
-    for chunk in CHUNKS:
-        shares += project([rows[d] for d in chunk])
+        out_shapes = [jax.ShapeDtypeStruct(shape, F32)] + [jax.ShapeDtypeStruct(shape, BF16)] * 3
+        flops = 2 * count * features * row_width
+        if weight is None:
+            *parts, weight = call(
+                sort_kernel,
+                out_shapes + [jax.ShapeDtypeStruct((NX, features // NX, row_width), BF16)],
+                flops,
+                8 << 20,
+                vmem=PROJECT_VMEM,
+                in_specs=[smem] + [hbm] * len(pieces) + [vmem] * len(blocks),
+                out_specs=[vmem] * (NX + 1),
+                scratch_shapes=[pltpu.SemaphoreType.DMA((len(pieces),))],
+            )(corner, *pieces, *blocks)
+        else:
+            parts = call(
+                again_kernel,
+                out_shapes,
+                flops,
+                6 << 20,
+                vmem=PROJECT_VMEM,
+                in_specs=[hbm] + [vmem] * len(blocks),
+                out_specs=[vmem] * NX,
+                scratch_shapes=[
+                    pltpu.VMEM(weight.shape, BF16),
+                    pltpu.SemaphoreType.DMA((NX,)),
+                ],
+            )(weight, *blocks)
+        shares += [parts[0]] + [ring_shift(parts[d], "tp", d) for d in (1, 3, 2)]
+
     sent = call(
         reduce_kernel,
         jax.ShapeDtypeStruct((CHIPS, 16, features // NX), BF16),

time: 110 us -> 100 us (0.909)
  starting transfers between devices: 21.5 us -> 36 us
  between operations: 13.5 us -> 0.24 us
  waiting for transfers between devices: 33.6 us -> 21.2 us
  Pallas kernels: 15.3 us -> 17.4 us
  local copies, waits for them, and re-layouts: 5.86 us -> 4.44 us
    ppermute x9 -> x17, starting transfers between devices: 11.9 us -> 24.7 us  [ring_shift(): lax.ppermute(value, axis, [(n, (n + steps) % count) for n in range(count)])]
    ppermute x9 -> x17, waiting for transfers between devices: 22.4 us -> 18 us  [ring_shift(): lax.ppermute(value, axis, [(n, (n + steps) % count) for n in range(count)])]
    all_gather x1 -> x0, waiting for transfers between devices: 4.13 us -> none  [on_device(): weight = lax.all_gather(out_weight, ('z', 'core'), axis=0, tiled=True)]
    ppermute x4, waiting for transfers between devices: 5.34 us -> 2.74 us  [chip_shift(): return lax.ppermute(value, ('z', 'y', 'core'), pairs)]
    pallas_call x2, Pallas kernels: 7.56 us -> 9.65 us  [the longest x1 5.55 us: on_device(): call(sort_kernel, out_shapes + [jax.ShapeDtypeStruct((NX, features // NX,...]
    ppermute x6 -> x14, starting transfers between devices: 1.27 us -> 2.95 us  [core_swap(): return lax.ppermute(value, 'core', [(0, 1), (1, 0)])]
    unnamed x10 -> x26, local copies, waits for them, and re-layouts: 4.91 us -> 3.45 us
  transfers between devices with their start and end apart: 20 -> 35, of which waited for: 9 -> 9; matrix products, arithmetic and copies ran while one was open for 2% -> 3% of each run, Pallas kernels for 12% -> 16%
where the time goes in v5:
time: 100 us; the launch traced here: 99.3 us
  starting transfers between devices  36 us (36%)
  waiting for transfers between devices  21.2 us (21%)
  blocking collectives  18.4 us (18%)
  Pallas kernels  17.4 us (17%)
  local copies, waits for them, and re-layouts  4.44 us (4%)
  other arithmetic  1.69 us (2%)
    ppermute x17, starting transfers between devices, ring_shift(): lax.ppermute(value, axis, [(n, (n + steps) % count) for n in range(count)])  24.7 us
    all_to_all x1, blocking collectives, on_device(): received = lax.all_to_all(sent, ('z', 'y'), 0, 0, tiled=True)  18.4 us
    ppermute x17, waiting for transfers between devices, ring_shift(): lax.ppermute(value, axis, [(n, (n + steps) % count) for n in range(count)])  18 us
    ppermute x4, starting transfers between devices, chip_shift(): return lax.ppermute(value, ('z', 'y', 'core'), pairs)  8.27 us
    pallas_call x1, Pallas kernels, on_device(): call(sort_kernel, out_shapes + [jax.ShapeDtypeStruct((NX, features // NX,...  5.55 us
    pallas_call x1, Pallas kernels, on_device(): call(attend_kernel, jax.ShapeDtypeStruct((tokens, row_width), BF16), 4 *...  5 us
    pallas_call x1, Pallas kernels, on_device(): call(again_kernel, out_shapes, flops, 6 << 20, vmem=PROJECT_VMEM, in_spec...  4.09 us
    unnamed x26, local copies, waits for them, and re-layouts  3.45 us
  transfers between devices with their start and end apart: 35, of which 9 were waited for; matrix products, arithmetic and copies ran while one was open for 3% of the time, Pallas kernels for 16%

profile of v5, /device:TPU:8, one launch (start us, length us, event | category | flops | bytes accessed | tf_op | source)
XLA Modules:
  0.0 99.3 jit_solution(11594857114027750894)
XLA Ops:
  0.0 0.8 copy-done.2
  0.8 0.8 copy-done.3
  1.7 1.7 %collective-permute-start.4 = (bf16[128,512]{1,0:T(8,128)(2,1)S(1)}, bf16[128,512]{1,0:T(8,128)(2,1)S(1)}, u32[]{:S(2)}, u32[]{:S(2)}) collective-permute-start(bf16[128,512]{1,0:T(8,128)(2,1)S(1)} %shard_map.64.refs_0_), channel_id=1, source_target_pairs={{0,8},{4,12},{8,16},{12,20},{16,24},{20,28},{24,32},{28,36},{32,40... | collective-permute-start | bytes 393224 | tf_op jit(solution)/shard_map/ppermute | solution.py:188
  3.4 2.3 %collective-permute-start.9 = (bf16[128,512]{1,0:T(8,128)(2,1)S(1)}, bf16[128,512]{1,0:T(8,128)(2,1)S(1)}, u32[]{:S(2)}, u32[]{:S(2)}) collective-permute-start(bf16[128,512]{1,0:T(8,128)(2,1)S(1)} %shard_map.64.refs_0_), channel_id=1, source_target_pairs={{0,16},{4,20},{8,24},{12,28},{16,32},{20,36},{24,40},{28,44},{32,4... | collective-permute-start | bytes 393224 | tf_op jit(solution)/shard_map/ppermute | solution.py:188
  5.7 2.4 %collective-permute-start.10 = (bf16[128,512]{1,0:T(8,128)(2,1)S(1)}, bf16[128,512]{1,0:T(8,128)(2,1)S(1)}, u32[]{:S(2)}, u32[]{:S(2)}) collective-permute-start(bf16[128,512]{1,0:T(8,128)(2,1)S(1)} %shard_map.64.refs_0_), channel_id=1, source_target_pairs={{0,24},{4,28},{8,32},{12,36},{16,40},{20,44},{24,48},{28,52},{32,5... | collective-permute-start | bytes 393224 | tf_op jit(solution)/shard_map/ppermute | solution.py:188
  8.1 1.9 %collective-permute-start.11 = (bf16[128,512]{1,0:T(8,128)(2,1)S(1)}, bf16[128,512]{1,0:T(8,128)(2,1)S(1)}, u32[]{:S(2)}, u32[]{:S(2)}) collective-permute-start(bf16[128,512]{1,0:T(8,128)(2,1)S(1)} %shard_map.64.refs_0_), channel_id=1, source_target_pairs={{0,32},{4,36},{8,40},{12,44},{16,48},{20,52},{24,56},{28,60},{32,6... | collective-permute-start | bytes 393224 | tf_op jit(solution)/shard_map/ppermute | solution.py:188
  10.0 1.3 %collective-permute-start = (bf16[64,2048]{1,0:T(8,128)(2,1)}, bf16[64,2048]{1,0:T(8,128)(2,1)S(1)}, u32[]{:S(2)}, u32[]{:S(2)}) collective-permute-start(bf16[64,2048]{1,0:T(8,128)(2,1)} %refs_0_.1), channel_id=1, source_target_pairs={{0,224},{32,0},{64,32},{96,64},{128,96},{160,128},{192,160},{224,1... | collective-permute-start | bytes 786440 | tf_op jit(solution)/shard_map/ppermute | solution.py:193
  11.3 0.7 constant_dynamic-slice_fusion
  12.1 0.7 broadcast_select_fusion
  12.8 0.8 select_reduce_fusion
  13.5 0.8 collective-permute-start.5
  14.6 2.7 %collective-permute-done.9.refs_2_ = bf16[128,512]{1,0:T(8,128)(2,1)S(1)} collective-permute-done((bf16[128,512]{1,0:T(8,128)(2,1)S(1)}, bf16[128,512]{1,0:T(8,128)(2,1)S(1)}, u32[]{:S(2)}, u32[]{:S(2)}) %collective-permute-start.9) | collective-permute-done | bytes 131104 | tf_op jit(solution)/shard_map/ppermute | solution.py:188
  17.4 1.0 %copy-done = bf16[128,2048]{1,0:T(8,128)(2,1)S(1)} copy-done((bf16[128,2048]{1,0:T(8,128)(2,1)S(1)}, bf16[128,2048]{1,0:T(8,128)(2,1)}, u32[]{:S(2)}) %copy-start) | copy-done | bytes 524312
  18.4 1.0 shard_map.65
  19.4 0.6 collective-permute-start.13
  20.1 0.4 collective-permute-start.8
  20.5 1.4 %collective-permute-start.1 = (bf16[64,2048]{1,0:T(8,128)(2,1)S(1)}, bf16[64,2048]{1,0:T(8,128)(2,1)S(1)}, u32[]{:S(2)}, u32[]{:S(2)}) collective-permute-start(bf16[64,2048]{1,0:T(8,128)(2,1)S(1)} %collective-permute-done.refs_1_), channel_id=1, source_target_pairs={{0,224},{32,0},{64,32},{96,64},{128,96},{160,128},{192,160},{224,1... | collective-permute-start | bytes 786440 | tf_op jit(solution)/shard_map/ppermute | solution.py:193
  21.9 0.5 collective-permute-start.16
  22.5 0.6 collective-permute-start.6
  23.0 0.2 collective-permute-done.15.refs_8_
  23.5 5.0 %shard_map.66.refs_16_ = bf16[128,2048]{1,0:T(8,128)(2,1)S(1)} custom-call(f32[128,1280]{1,0:T(8,128)S(1)} %get-tuple-element.30.bias_ref, bf16[64,2048]{1,0:T(8,128)(2,1)S(1)} %get-tuple-element.31.keep_ref, bf16[64,2048]{1,0:T(8,128)(2,1)S(1)} %collective-permute-done.8.got_ref, bf16[128,512]{1,0:T(8,128)(2,1)S(1)} %shard_map.64.refs_0_, ...), custom_call_target="tpu_custom_call" | custom-call | flops 1342177280 | bytes 8388608 | tf_op jit(solution)/shard_map/pallas_call | solution.py:248
  28.5 0.4 collective-permute-start.17
  28.9 2.5 %collective-permute-start.2 = (bf16[64,2048]{1,0:T(8,128)(2,1)S(1)}, bf16[64,2048]{1,0:T(8,128)(2,1)S(1)}, u32[]{:S(2)}, u32[]{:S(2)}) collective-permute-start(bf16[64,2048]{1,0:T(8,128)(2,1)S(1)} %collective-permute-done.1.refs_2_), channel_id=1, source_target_pairs={{0,224},{32,0},{64,32},{96,64},{128,96},{160,128},{192,160},{224,1... | collective-permute-start | bytes 786440 | tf_op jit(solution)/shard_map/ppermute | solution.py:193
  31.5 0.9 collective-permute-start.25
  32.4 1.3 %collective-permute-start.26 = (bf16[128,2048]{1,0:T(8,128)(2,1)S(1)}, bf16[128,2048]{1,0:T(8,128)(2,1)S(1)}, u32[]{:S(2)}, u32[]{:S(2)}) collective-permute-start(bf16[128,2048]{1,0:T(8,128)(2,1)S(1)} %shard_map.66.refs_16_), channel_id=1, source_target_pairs={{0,8},{8,16},{16,24},{24,0},{1,9},{9,17},{17,25},{25,1},{2,10},{10... | collective-permute-start | bytes 1572872 | tf_op jit(solution)/shard_map/ppermute | solution.py:193
  33.7 0.7 copy-done.10
  34.4 2.9 %collective-permute-done.2.refs_3_ = bf16[64,2048]{1,0:T(8,128)(2,1)S(1)} collective-permute-done((bf16[64,2048]{1,0:T(8,128)(2,1)S(1)}, bf16[64,2048]{1,0:T(8,128)(2,1)S(1)}, u32[]{:S(2)}, u32[]{:S(2)}) %collective-permute-start.2) | collective-permute-done | bytes 262176 | tf_op jit(solution)/shard_map/ppermute | solution.py:193
  37.3 3.4 %collective-permute-start.3 = (bf16[64,2048]{1,0:T(8,128)(2,1)S(1)}, bf16[64,2048]{1,0:T(8,128)(2,1)S(1)}, u32[]{:S(2)}, u32[]{:S(2)}) collective-permute-start(bf16[64,2048]{1,0:T(8,128)(2,1)S(1)} %collective-permute-done.2.refs_3_), channel_id=1, source_target_pairs={{0,224},{32,0},{64,32},{96,64},{128,96},{160,128},{192,160},{224,1... | collective-permute-start | bytes 786440 | tf_op jit(solution)/shard_map/ppermute | solution.py:193
  40.8 2.5 %collective-permute-done.7.refs_7_ = bf16[64,2048]{1,0:T(8,128)(2,1)} collective-permute-done((bf16[64,2048]{1,0:T(8,128)(2,1)S(1)}, bf16[64,2048]{1,0:T(8,128)(2,1)}, u32[]{:S(2)}, u32[]{:S(2)}) %collective-permute-start.7) | collective-permute-done | bytes 262176 | tf_op jit(solution)/shard_map/ppermute | solution.py:193
  43.3 2.2 %collective-permute-done.3.refs_4_ = bf16[64,2048]{1,0:T(8,128)(2,1)S(1)} collective-permute-done((bf16[64,2048]{1,0:T(8,128)(2,1)S(1)}, bf16[64,2048]{1,0:T(8,128)(2,1)S(1)}, u32[]{:S(2)}, u32[]{:S(2)}) %collective-permute-start.3) | collective-permute-done | bytes 262176 | tf_op jit(solution)/shard_map/ppermute | solution.py:193
  45.5 0.5 collective-permute-start.20
  46.0 0.3 collective-permute-start.24
  46.3 3.1 %collective-permute-done.26.refs_18_ = bf16[128,2048]{1,0:T(8,128)(2,1)S(1)} collective-permute-done((bf16[128,2048]{1,0:T(8,128)(2,1)S(1)}, bf16[128,2048]{1,0:T(8,128)(2,1)S(1)}, u32[]{:S(2)}, u32[]{:S(2)}) %collective-permute-start.26) | collective-permute-done | bytes 524320 | tf_op jit(solution)/shard_map/ppermute | solution.py:193
  49.6 0.4 collective-permute-start.30
  50.0 2.7 %collective-permute-start.31 = (bf16[64,2048]{1,0:T(8,128)(2,1)S(1)}, bf16[64,2048]{1,0:T(8,128)(2,1)S(1)}, u32[]{:S(2)}, u32[]{:S(2)}) collective-permute-start(bf16[64,2048]{1,0:T(8,128)(2,1)S(1)} %slice.9), channel_id=1, source_target_pairs={{0,24},{8,0},{16,8},{24,16},{1,25},{9,1},{17,9},{25,17},{2,26},{10... | collective-permute-start | bytes 786440 | tf_op jit(solution)/shard_map/ppermute | solution.py:193
  52.9 5.6 %shard_map.67 = (f32[384,256]{1,0:T(8,128)}, bf16[384,256]{1,0:T(8,128)(2,1)S(1)}, bf16[384,256]{1,0:T(8,128)(2,1)S(1)}, bf16[384,256]{1,0:T(8,128)(2,1)S(1)}, bf16[4,256,2048]{2,1,0:T(8,128)(2,1)}) custom-call(s32[3]{0:T(128)S(1)} %pad_add_fusion.1.place_ref, bf16[64,2048]{1,0:T(8,128)(2,1)S(1)} %copy-done.5, ...), custom_call_target="tpu_custom_call" | custom-call | flops 1610612736 | bytes 8388608 | tf_op jit(solution)/shard_map/pallas_call | solution.py:279
  58.5 1.6 %collective-permute-start.27 = (bf16[384,256]{1,0:T(8,128)(2,1)S(1)}, bf16[384,256]{1,0:T(8,128)(2,1)S(1)}, u32[]{:S(2)}, u32[]{:S(2)}) collective-permute-start(bf16[384,256]{1,0:T(8,128)(2,1)S(1)} %get-tuple-element.43), channel_id=1, source_target_pairs={{0,1},{1,2},{2,3},{3,0},{4,5},{5,6},{6,7},{7,4},{8,9},{9,10},{10,1... | collective-permute-start | bytes 589832 | tf_op jit(solution)/shard_map/ppermute | solution.py:193
  60.0 1.8 %collective-permute-start.28 = (bf16[384,256]{1,0:T(8,128)(2,1)S(1)}, bf16[384,256]{1,0:T(8,128)(2,1)S(1)}, u32[]{:S(2)}, u32[]{:S(2)}) collective-permute-start(bf16[384,256]{1,0:T(8,128)(2,1)S(1)} %get-tuple-element.44), channel_id=1, source_target_pairs={{0,3},{1,0},{2,1},{3,2},{4,7},{5,4},{6,5},{7,6},{8,11},{9,8},{10,9... | collective-permute-start | bytes 589832 | tf_op jit(solution)/shard_map/ppermute | solution.py:193
  61.8 1.8 %collective-permute-start.29 = (bf16[384,256]{1,0:T(8,128)(2,1)S(1)}, bf16[384,256]{1,0:T(8,128)(2,1)S(1)}, u32[]{:S(2)}, u32[]{:S(2)}) collective-permute-start(bf16[384,256]{1,0:T(8,128)(2,1)S(1)} %get-tuple-element.45), channel_id=1, source_target_pairs={{0,2},{1,3},{2,0},{3,1},{4,6},{5,7},{6,4},{7,5},{8,10},{9,11},{10,... | collective-permute-start | bytes 589832 | tf_op jit(solution)/shard_map/ppermute | solution.py:193
  63.6 4.1 %shard_map.68 = (f32[128,256]{1,0:T(8,128)S(1)}, bf16[128,256]{1,0:T(8,128)(2,1)S(1)}, bf16[128,256]{1,0:T(8,128)(2,1)S(1)}, bf16[128,256]{1,0:T(8,128)(2,1)S(1)}) custom-call(bf16[4,256,2048]{2,1,0:T(8,128)(2,1)} %get-tuple-element.46.sorted_ref, bf16[64,2048]{1,0:T(8,128)(2,1)S(1)} %collective-permute-done.30.refs_0_, ...), custom_call_target="tpu_custom_call" | custom-call | flops 536870912 | bytes 6291456 | tf_op jit(solution)/shard_map/pallas_call | solution.py:290
  67.7 0.7 collective-permute-start.32
  68.4 2.7 %collective-permute-start.33 = (bf16[128,256]{1,0:T(8,128)(2,1)S(1)}, bf16[128,256]{1,0:T(8,128)(2,1)S(1)}, u32[]{:S(2)}, u32[]{:S(2)}) collective-permute-start(bf16[128,256]{1,0:T(8,128)(2,1)S(1)} %get-tuple-element.49), channel_id=1, source_target_pairs={{0,3},{1,0},{2,1},{3,2},{4,7},{5,4},{6,5},{7,6},{8,11},{9,8},{10,9... | collective-permute-start | bytes 196616 | tf_op jit(solution)/shard_map/ppermute | solution.py:193
  71.0 2.3 %collective-permute-done.32.refs_5_ = bf16[128,256]{1,0:T(8,128)(2,1)S(1)} collective-permute-done((bf16[128,256]{1,0:T(8,128)(2,1)S(1)}, bf16[128,256]{1,0:T(8,128)(2,1)S(1)}, u32[]{:S(2)}, u32[]{:S(2)}) %collective-permute-start.32) | collective-permute-done | bytes 65568 | tf_op jit(solution)/shard_map/ppermute | solution.py:193
  73.4 0.8 collective-permute-start.34
  74.3 4.9 %collective-permute-done.34.refs_7_ = bf16[128,256]{1,0:T(8,128)(2,1)S(1)} collective-permute-done((bf16[128,256]{1,0:T(8,128)(2,1)S(1)}, bf16[128,256]{1,0:T(8,128)(2,1)S(1)}, u32[]{:S(2)}, u32[]{:S(2)}) %collective-permute-start.34) | collective-permute-done | bytes 65568 | tf_op jit(solution)/shard_map/ppermute | solution.py:193
  79.2 1.0 %shard_map.69 = bf16[32,16,256]{2,1,0:T(8,128)(2,1)S(1)} custom-call(s32[2]{0:T(128)S(1)} %pad_add_fusion.place_ref, f32[384,256]{1,0:T(8,128)S(1)} %copy-done.1, bf16[384,256]{1,0:T(8,128)(2,1)S(1)} %collective-permute-done.27.refs_1_, bf16[384,256]{1,0:T(8,128)(2,1)S(1)} %collective-permute-done.28.refs_2_, ...), custom_call_target="tpu_custom_call" | custom-call | flops 4194304 | bytes 2097152 | tf_op jit(solution)/shard_map/pallas_call | solution.py:305
  80.2 18.4 %all_to_all.5.x_ref = bf16[32,16,256]{2,1,0:T(8,128)(2,1)S(1)} all-to-all(bf16[32,16,256]{2,1,0:T(8,128)(2,1)S(1)} %shard_map.69), channel_id=1, replica_groups=mesh['z'=8,'y'=4,'core'=2,'tp'=4] {'z','y'}, dimensions={0} | all-to-all | bytes 524288 | tf_op jit(solution)/shard_map/all_to_all | solution.py:314
  98.6 0.7 shard_map.70
  (68 shorter events, 1.1 us)
Async XLA Ops:
  0.0 0.8 copy-start.2
  0.8 0.8 copy-start.3
  1.7 26.8 %copy-start.5 = (bf16[64,2048]{1,0:T(8,128)(2,1)S(1)}, bf16[64,2048]{1,0:T(8,128)(2,1)}, u32[]{:S(2)}) copy-start(bf16[64,2048]{1,0:T(8,128)(2,1)} %refs_0_.1) | copy-start | bytes 786436
  1.7 11.8 %collective-permute-start.4 = (bf16[128,512]{1,0:T(8,128)(2,1)S(1)}, bf16[128,512]{1,0:T(8,128)(2,1)S(1)}, u32[]{:S(2)}, u32[]{:S(2)}) collective-permute-start(bf16[128,512]{1,0:T(8,128)(2,1)S(1)} %shard_map.64.refs_0_), channel_id=1, source_target_pairs={{0,8},{4,12},{8,16},{12,20},{16,24},{20,28},{24,32},{28,36},{32,40... | collective-permute-start | bytes 393224 | tf_op jit(solution)/shard_map/ppermute | solution.py:188
  3.4 14.0 %collective-permute-start.9 = (bf16[128,512]{1,0:T(8,128)(2,1)S(1)}, bf16[128,512]{1,0:T(8,128)(2,1)S(1)}, u32[]{:S(2)}, u32[]{:S(2)}) collective-permute-start(bf16[128,512]{1,0:T(8,128)(2,1)S(1)} %shard_map.64.refs_0_), channel_id=1, source_target_pairs={{0,16},{4,20},{8,24},{12,28},{16,32},{20,36},{24,40},{28,44},{32,4... | collective-permute-start | bytes 393224 | tf_op jit(solution)/shard_map/ppermute | solution.py:188
  5.7 13.7 %collective-permute-start.10 = (bf16[128,512]{1,0:T(8,128)(2,1)S(1)}, bf16[128,512]{1,0:T(8,128)(2,1)S(1)}, u32[]{:S(2)}, u32[]{:S(2)}) collective-permute-start(bf16[128,512]{1,0:T(8,128)(2,1)S(1)} %shard_map.64.refs_0_), channel_id=1, source_target_pairs={{0,24},{4,28},{8,32},{12,36},{16,40},{20,44},{24,48},{28,52},{32,5... | collective-permute-start | bytes 393224 | tf_op jit(solution)/shard_map/ppermute | solution.py:188
  8.1 11.9 %collective-permute-start.11 = (bf16[128,512]{1,0:T(8,128)(2,1)S(1)}, bf16[128,512]{1,0:T(8,128)(2,1)S(1)}, u32[]{:S(2)}, u32[]{:S(2)}) collective-permute-start(bf16[128,512]{1,0:T(8,128)(2,1)S(1)} %shard_map.64.refs_0_), channel_id=1, source_target_pairs={{0,32},{4,36},{8,40},{12,44},{16,48},{20,52},{24,56},{28,60},{32,6... | collective-permute-start | bytes 393224 | tf_op jit(solution)/shard_map/ppermute | solution.py:188
  10.0 10.1 %collective-permute-start = (bf16[64,2048]{1,0:T(8,128)(2,1)}, bf16[64,2048]{1,0:T(8,128)(2,1)S(1)}, u32[]{:S(2)}, u32[]{:S(2)}) collective-permute-start(bf16[64,2048]{1,0:T(8,128)(2,1)} %refs_0_.1), channel_id=1, source_target_pairs={{0,224},{32,0},{64,32},{96,64},{128,96},{160,128},{192,160},{224,1... | collective-permute-start | bytes 786440 | tf_op jit(solution)/shard_map/ppermute | solution.py:193
  13.5 8.9 %collective-permute-start.5 = (bf16[64,2048]{1,0:T(8,128)(2,1)}, bf16[64,2048]{1,0:T(8,128)(2,1)S(1)}, u32[]{:S(2)}, u32[]{:S(2)}) collective-permute-start(bf16[64,2048]{1,0:T(8,128)(2,1)} %refs_0_.1), channel_id=1, source_target_pairs={{0,32},{32,64},{64,96},{96,128},{128,160},{160,192},{192,224},{224... | collective-permute-start | bytes 786440 | tf_op jit(solution)/shard_map/ppermute | solution.py:193
  17.4 3.1 %collective-permute-start.12 = (bf16[128,512]{1,0:T(8,128)(2,1)S(1)}, bf16[128,512]{1,0:T(8,128)(2,1)S(1)}, u32[]{:S(2)}, u32[]{:S(2)}) collective-permute-start(bf16[128,512]{1,0:T(8,128)(2,1)S(1)} %shard_map.64.refs_0_), channel_id=1, source_target_pairs={{0,4},{4,0},{1,5},{5,1},{2,6},{6,2},{3,7},{7,3},{8,12},{12,8},{9,1... | collective-permute-start | bytes 393224 | tf_op jit(solution)/shard_map/ppermute | solution.py:197
  17.4 1.0 %copy-start = (bf16[128,2048]{1,0:T(8,128)(2,1)S(1)}, bf16[128,2048]{1,0:T(8,128)(2,1)}, u32[]{:S(2)}) copy-start(bf16[128,2048]{1,0:T(8,128)(2,1)} %q_ref) | copy-start | bytes 1572868
  19.4 2.5 %collective-permute-start.13 = (bf16[128,512]{1,0:T(8,128)(2,1)S(1)}, bf16[128,512]{1,0:T(8,128)(2,1)S(1)}, u32[]{:S(2)}, u32[]{:S(2)}) collective-permute-start(bf16[128,512]{1,0:T(8,128)(2,1)S(1)} %collective-permute-done.4.refs_1_), channel_id=1, source_target_pairs={{0,4},{4,0},{1,5},{5,1},{2,6},{6,2},{3,7},{7,3},{8,12},{12,8},{9,1... | collective-permute-start | bytes 393224 | tf_op jit(solution)/shard_map/ppermute | solution.py:197
  20.0 2.0 %collective-permute-start.14 = (bf16[128,512]{1,0:T(8,128)(2,1)S(1)}, bf16[128,512]{1,0:T(8,128)(2,1)S(1)}, u32[]{:S(2)}, u32[]{:S(2)}) collective-permute-start(bf16[128,512]{1,0:T(8,128)(2,1)S(1)} %collective-permute-done.9.refs_2_), channel_id=1, source_target_pairs={{0,4},{4,0},{1,5},{5,1},{2,6},{6,2},{3,7},{7,3},{8,12},{12,8},{9,1... | collective-permute-start | bytes 393224 | tf_op jit(solution)/shard_map/ppermute | solution.py:197
  20.1 3.4 %collective-permute-start.8 = (bf16[64,2048]{1,0:T(8,128)(2,1)S(1)}, bf16[64,2048]{1,0:T(8,128)(2,1)S(1)}, u32[]{:S(2)}, u32[]{:S(2)}) collective-permute-start(bf16[64,2048]{1,0:T(8,128)(2,1)S(1)} %get-tuple-element.32), channel_id=1, source_target_pairs={{0,4},{4,0},{1,5},{5,1},{2,6},{6,2},{3,7},{7,3},{8,12},{12,8},{9,1... | collective-permute-start | bytes 786440 | tf_op jit(solution)/shard_map/ppermute | solution.py:197
  20.5 8.4 %collective-permute-start.1 = (bf16[64,2048]{1,0:T(8,128)(2,1)S(1)}, bf16[64,2048]{1,0:T(8,128)(2,1)S(1)}, u32[]{:S(2)}, u32[]{:S(2)}) collective-permute-start(bf16[64,2048]{1,0:T(8,128)(2,1)S(1)} %collective-permute-done.refs_1_), channel_id=1, source_target_pairs={{0,224},{32,0},{64,32},{96,64},{128,96},{160,128},{192,160},{224,1... | collective-permute-start | bytes 786440 | tf_op jit(solution)/shard_map/ppermute | solution.py:193
  21.9 1.3 %collective-permute-start.15 = (bf16[128,512]{1,0:T(8,128)(2,1)S(1)}, bf16[128,512]{1,0:T(8,128)(2,1)S(1)}, u32[]{:S(2)}, u32[]{:S(2)}) collective-permute-start(bf16[128,512]{1,0:T(8,128)(2,1)S(1)} %collective-permute-done.10.refs_3_), channel_id=1, source_target_pairs={{0,4},{4,0},{1,5},{5,1},{2,6},{6,2},{3,7},{7,3},{8,12},{12,8},{9,1... | collective-permute-start | bytes 393224 | tf_op jit(solution)/shard_map/ppermute | solution.py:197
  21.9 1.5 %collective-permute-start.16 = (bf16[128,512]{1,0:T(8,128)(2,1)S(1)}, bf16[128,512]{1,0:T(8,128)(2,1)S(1)}, u32[]{:S(2)}, u32[]{:S(2)}) collective-permute-start(bf16[128,512]{1,0:T(8,128)(2,1)S(1)} %collective-permute-done.11.refs_4_), channel_id=1, source_target_pairs={{0,4},{4,0},{1,5},{5,1},{2,6},{6,2},{3,7},{7,3},{8,12},{12,8},{9,1... | collective-permute-start | bytes 393224 | tf_op jit(solution)/shard_map/ppermute | solution.py:197
  22.4 30.4 %copy-start.8 = (bf16[64,2048]{1,0:T(8,128)(2,1)}, bf16[64,2048]{1,0:T(8,128)(2,1)S(1)}, u32[]{:S(2)}) copy-start(bf16[64,2048]{1,0:T(8,128)(2,1)S(1)} %collective-permute-done.5.refs_5_) | copy-start | bytes 786436
  22.5 9.9 %collective-permute-start.6 = (bf16[64,2048]{1,0:T(8,128)(2,1)S(1)}, bf16[64,2048]{1,0:T(8,128)(2,1)S(1)}, u32[]{:S(2)}, u32[]{:S(2)}) collective-permute-start(bf16[64,2048]{1,0:T(8,128)(2,1)S(1)} %collective-permute-done.5.refs_5_), channel_id=1, source_target_pairs={{0,32},{32,64},{64,96},{96,128},{128,160},{160,192},{192,224},{224... | collective-permute-start | bytes 786440 | tf_op jit(solution)/shard_map/ppermute | solution.py:193
  28.5 24.4 %copy-start.4 = (bf16[128,2048]{1,0:T(8,128)(2,1)}, bf16[128,2048]{1,0:T(8,128)(2,1)S(1)}, u32[]{:S(2)}) copy-start(bf16[128,2048]{1,0:T(8,128)(2,1)S(1)} %shard_map.66.refs_16_) | copy-start | bytes 1572868
  28.5 5.2 %collective-permute-start.17 = (bf16[64,2048]{1,0:T(8,128)(2,1)S(1)}, bf16[64,2048]{1,0:T(8,128)(2,1)S(1)}, u32[]{:S(2)}, u32[]{:S(2)}) collective-permute-start(bf16[64,2048]{1,0:T(8,128)(2,1)S(1)} %copy-done.5), channel_id=1, source_target_pairs={{0,4},{4,0},{1,5},{5,1},{2,6},{6,2},{3,7},{7,3},{8,12},{12,8},{9,1... | collective-permute-start | bytes 786440 | tf_op jit(solution)/shard_map/ppermute | solution.py:197
  28.9 8.4 %collective-permute-start.2 = (bf16[64,2048]{1,0:T(8,128)(2,1)S(1)}, bf16[64,2048]{1,0:T(8,128)(2,1)S(1)}, u32[]{:S(2)}, u32[]{:S(2)}) collective-permute-start(bf16[64,2048]{1,0:T(8,128)(2,1)S(1)} %collective-permute-done.1.refs_2_), channel_id=1, source_target_pairs={{0,224},{32,0},{64,32},{96,64},{128,96},{160,128},{192,160},{224,1... | collective-permute-start | bytes 786440 | tf_op jit(solution)/shard_map/ppermute | solution.py:193
  31.5 9.3 %collective-permute-start.18 = (bf16[64,2048]{1,0:T(8,128)(2,1)S(1)}, bf16[64,2048]{1,0:T(8,128)(2,1)S(1)}, u32[]{:S(2)}, u32[]{:S(2)}) collective-permute-start(bf16[64,2048]{1,0:T(8,128)(2,1)S(1)} %collective-permute-done.refs_1_), channel_id=1, source_target_pairs={{0,4},{4,0},{1,5},{5,1},{2,6},{6,2},{3,7},{7,3},{8,12},{12,8},{9,1... | collective-permute-start | bytes 786440 | tf_op jit(solution)/shard_map/ppermute | solution.py:197
  31.5 14.6 %collective-permute-start.25 = (bf16[128,2048]{1,0:T(8,128)(2,1)S(1)}, bf16[128,2048]{1,0:T(8,128)(2,1)S(1)}, u32[]{:S(2)}, u32[]{:S(2)}) collective-permute-start(bf16[128,2048]{1,0:T(8,128)(2,1)S(1)} %shard_map.66.refs_16_), channel_id=1, source_target_pairs={{0,24},{8,0},{16,8},{24,16},{1,25},{9,1},{17,9},{25,17},{2,26},{10... | collective-permute-start | bytes 1572872 | tf_op jit(solution)/shard_map/ppermute | solution.py:193
  32.4 20.5 %copy-start.9 = (bf16[64,2048]{1,0:T(8,128)(2,1)}, bf16[64,2048]{1,0:T(8,128)(2,1)S(1)}, u32[]{:S(2)}) copy-start(bf16[64,2048]{1,0:T(8,128)(2,1)S(1)} %collective-permute-done.6.refs_6_) | copy-start | bytes 786436
  32.4 17.1 %collective-permute-start.26 = (bf16[128,2048]{1,0:T(8,128)(2,1)S(1)}, bf16[128,2048]{1,0:T(8,128)(2,1)S(1)}, u32[]{:S(2)}, u32[]{:S(2)}) collective-permute-start(bf16[128,2048]{1,0:T(8,128)(2,1)S(1)} %shard_map.66.refs_16_), channel_id=1, source_target_pairs={{0,8},{8,16},{16,24},{24,0},{1,9},{9,17},{17,25},{25,1},{2,10},{10... | collective-permute-start | bytes 1572872 | tf_op jit(solution)/shard_map/ppermute | solution.py:193
  33.7 0.7 copy-start.10
  33.7 9.6 %collective-permute-start.7 = (bf16[64,2048]{1,0:T(8,128)(2,1)S(1)}, bf16[64,2048]{1,0:T(8,128)(2,1)}, u32[]{:S(2)}, u32[]{:S(2)}) collective-permute-start(bf16[64,2048]{1,0:T(8,128)(2,1)S(1)} %collective-permute-done.6.refs_6_), channel_id=1, source_target_pairs={{0,32},{32,64},{64,96},{96,128},{128,160},{160,192},{192,224},{224... | collective-permute-start | bytes 786440 | tf_op jit(solution)/shard_map/ppermute | solution.py:193
  37.3 8.2 %collective-permute-start.3 = (bf16[64,2048]{1,0:T(8,128)(2,1)S(1)}, bf16[64,2048]{1,0:T(8,128)(2,1)S(1)}, u32[]{:S(2)}, u32[]{:S(2)}) collective-permute-start(bf16[64,2048]{1,0:T(8,128)(2,1)S(1)} %collective-permute-done.2.refs_3_), channel_id=1, source_target_pairs={{0,224},{32,0},{64,32},{96,64},{128,96},{160,128},{192,160},{224,1... | collective-permute-start | bytes 786440 | tf_op jit(solution)/shard_map/ppermute | solution.py:193
  40.8 8.7 %copy-start.11 = (bf16[64,2048]{1,0:T(8,128)(2,1)}, bf16[64,2048]{1,0:T(8,128)(2,1)S(1)}, u32[]{:S(2)}) copy-start(bf16[64,2048]{1,0:T(8,128)(2,1)S(1)} %collective-permute-done.18.refs_9_) | copy-start | bytes 786436
  40.8 4.7 %collective-permute-start.22 = (bf16[64,2048]{1,0:T(8,128)(2,1)S(1)}, bf16[64,2048]{1,0:T(8,128)(2,1)S(1)}, u32[]{:S(2)}, u32[]{:S(2)}) collective-permute-start(bf16[64,2048]{1,0:T(8,128)(2,1)S(1)} %collective-permute-done.5.refs_5_), channel_id=1, source_target_pairs={{0,4},{4,0},{1,5},{5,1},{2,6},{6,2},{3,7},{7,3},{8,12},{12,8},{9,1... | collective-permute-start | bytes 786440 | tf_op jit(solution)/shard_map/ppermute | solution.py:197
  43.3 6.3 %collective-permute-start.19 = (bf16[64,2048]{1,0:T(8,128)(2,1)S(1)}, bf16[64,2048]{1,0:T(8,128)(2,1)}, u32[]{:S(2)}, u32[]{:S(2)}) collective-permute-start(bf16[64,2048]{1,0:T(8,128)(2,1)S(1)} %collective-permute-done.1.refs_2_), channel_id=1, source_target_pairs={{0,4},{4,0},{1,5},{5,1},{2,6},{6,2},{3,7},{7,3},{8,12},{12,8},{9,1... | collective-permute-start | bytes 786440 | tf_op jit(solution)/shard_map/ppermute | solution.py:197
  45.5 4.5 %collective-permute-start.23 = (bf16[64,2048]{1,0:T(8,128)(2,1)S(1)}, bf16[64,2048]{1,0:T(8,128)(2,1)}, u32[]{:S(2)}, u32[]{:S(2)}) collective-permute-start(bf16[64,2048]{1,0:T(8,128)(2,1)S(1)} %collective-permute-done.6.refs_6_), channel_id=1, source_target_pairs={{0,4},{4,0},{1,5},{5,1},{2,6},{6,2},{3,7},{7,3},{8,12},{12,8},{9,1... | collective-permute-start | bytes 786440 | tf_op jit(solution)/shard_map/ppermute | solution.py:197
  45.5 4.0 %copy-start.12 = (bf16[64,2048]{1,0:T(8,128)(2,1)}, bf16[64,2048]{1,0:T(8,128)(2,1)S(1)}, u32[]{:S(2)}) copy-start(bf16[64,2048]{1,0:T(8,128)(2,1)S(1)} %collective-permute-done.22.refs_13_) | copy-start | bytes 786436
  45.5 7.3 %collective-permute-start.20 = (bf16[64,2048]{1,0:T(8,128)(2,1)S(1)}, bf16[64,2048]{1,0:T(8,128)(2,1)}, u32[]{:S(2)}, u32[]{:S(2)}) collective-permute-start(bf16[64,2048]{1,0:T(8,128)(2,1)S(1)} %collective-permute-done.2.refs_3_), channel_id=1, source_target_pairs={{0,4},{4,0},{1,5},{5,1},{2,6},{6,2},{3,7},{7,3},{8,12},{12,8},{9,1... | collective-permute-start | bytes 786440 | tf_op jit(solution)/shard_map/ppermute | solution.py:197
  46.0 6.9 %copy-start.6 = (bf16[128,2048]{1,0:T(8,128)(2,1)}, bf16[128,2048]{1,0:T(8,128)(2,1)S(1)}, u32[]{:S(2)}) copy-start(bf16[128,2048]{1,0:T(8,128)(2,1)S(1)} %collective-permute-done.25.refs_17_) | copy-start | bytes 1572868
  46.0 6.8 %collective-permute-start.24 = (bf16[64,2048]{1,0:T(8,128)(2,1)}, bf16[64,2048]{1,0:T(8,128)(2,1)}, u32[]{:S(2)}, u32[]{:S(2)}) collective-permute-start(bf16[64,2048]{1,0:T(8,128)(2,1)} %collective-permute-done.7.refs_7_), channel_id=1, source_target_pairs={{0,4},{4,0},{1,5},{5,1},{2,6},{6,2},{3,7},{7,3},{8,12},{12,8},{9,1... | collective-permute-start | bytes 786440 | tf_op jit(solution)/shard_map/ppermute | solution.py:197
  49.5 3.4 %copy-start.7 = (bf16[128,2048]{1,0:T(8,128)(2,1)}, bf16[128,2048]{1,0:T(8,128)(2,1)S(1)}, u32[]{:S(2)}) copy-start(bf16[128,2048]{1,0:T(8,128)(2,1)S(1)} %collective-permute-done.26.refs_18_) | copy-start | bytes 1572868
  49.5 3.4 %collective-permute-start.21 = (bf16[64,2048]{1,0:T(8,128)(2,1)S(1)}, bf16[64,2048]{1,0:T(8,128)(2,1)}, u32[]{:S(2)}, u32[]{:S(2)}) collective-permute-start(bf16[64,2048]{1,0:T(8,128)(2,1)S(1)} %collective-permute-done.3.refs_4_), channel_id=1, source_target_pairs={{0,4},{4,0},{1,5},{5,1},{2,6},{6,2},{3,7},{7,3},{8,12},{12,8},{9,1... | collective-permute-start | bytes 786440 | tf_op jit(solution)/shard_map/ppermute | solution.py:197
  49.6 14.0 %collective-permute-start.30 = (bf16[64,2048]{1,0:T(8,128)(2,1)S(1)}, bf16[64,2048]{1,0:T(8,128)(2,1)S(1)}, u32[]{:S(2)}, u32[]{:S(2)}) collective-permute-start(bf16[64,2048]{1,0:T(8,128)(2,1)S(1)} %slice.8), channel_id=1, source_target_pairs={{0,8},{8,16},{16,24},{24,0},{1,9},{9,17},{17,25},{25,1},{2,10},{10... | collective-permute-start | bytes 786440 | tf_op jit(solution)/shard_map/ppermute | solution.py:193
  50.0 13.6 %collective-permute-start.31 = (bf16[64,2048]{1,0:T(8,128)(2,1)S(1)}, bf16[64,2048]{1,0:T(8,128)(2,1)S(1)}, u32[]{:S(2)}, u32[]{:S(2)}) collective-permute-start(bf16[64,2048]{1,0:T(8,128)(2,1)S(1)} %slice.9), channel_id=1, source_target_pairs={{0,24},{8,0},{16,8},{24,16},{1,25},{9,1},{17,9},{25,17},{2,26},{10... | collective-permute-start | bytes 786440 | tf_op jit(solution)/shard_map/ppermute | solution.py:193
  58.5 20.7 %copy-start.1 = (f32[384,256]{1,0:T(8,128)S(1)}, f32[384,256]{1,0:T(8,128)}, u32[]{:S(2)}) copy-start(f32[384,256]{1,0:T(8,128)} %get-tuple-element.42.refs_0_) | copy-start | bytes 1179652
  58.5 20.7 %collective-permute-start.27 = (bf16[384,256]{1,0:T(8,128)(2,1)S(1)}, bf16[384,256]{1,0:T(8,128)(2,1)S(1)}, u32[]{:S(2)}, u32[]{:S(2)}) collective-permute-start(bf16[384,256]{1,0:T(8,128)(2,1)S(1)} %get-tuple-element.43), channel_id=1, source_target_pairs={{0,1},{1,2},{2,3},{3,0},{4,5},{5,6},{6,7},{7,4},{8,9},{9,10},{10,1... | collective-permute-start | bytes 589832 | tf_op jit(solution)/shard_map/ppermute | solution.py:193
  60.0 19.1 %collective-permute-start.28 = (bf16[384,256]{1,0:T(8,128)(2,1)S(1)}, bf16[384,256]{1,0:T(8,128)(2,1)S(1)}, u32[]{:S(2)}, u32[]{:S(2)}) collective-permute-start(bf16[384,256]{1,0:T(8,128)(2,1)S(1)} %get-tuple-element.44), channel_id=1, source_target_pairs={{0,3},{1,0},{2,1},{3,2},{4,7},{5,4},{6,5},{7,6},{8,11},{9,8},{10,9... | collective-permute-start | bytes 589832 | tf_op jit(solution)/shard_map/ppermute | solution.py:193
  61.8 17.4 %collective-permute-start.29 = (bf16[384,256]{1,0:T(8,128)(2,1)S(1)}, bf16[384,256]{1,0:T(8,128)(2,1)S(1)}, u32[]{:S(2)}, u32[]{:S(2)}) collective-permute-start(bf16[384,256]{1,0:T(8,128)(2,1)S(1)} %get-tuple-element.45), channel_id=1, source_target_pairs={{0,2},{1,3},{2,0},{3,1},{4,6},{5,7},{6,4},{7,5},{8,10},{9,11},{10,... | collective-permute-start | bytes 589832 | tf_op jit(solution)/shard_map/ppermute | solution.py:193
  67.7 5.7 %collective-permute-start.32 = (bf16[128,256]{1,0:T(8,128)(2,1)S(1)}, bf16[128,256]{1,0:T(8,128)(2,1)S(1)}, u32[]{:S(2)}, u32[]{:S(2)}) collective-permute-start(bf16[128,256]{1,0:T(8,128)(2,1)S(1)} %get-tuple-element.48), channel_id=1, source_target_pairs={{0,1},{1,2},{2,3},{3,0},{4,5},{5,6},{6,7},{7,4},{8,9},{9,10},{10,1... | collective-permute-start | bytes 196616 | tf_op jit(solution)/shard_map/ppermute | solution.py:193
  68.4 5.9 %collective-permute-start.33 = (bf16[128,256]{1,0:T(8,128)(2,1)S(1)}, bf16[128,256]{1,0:T(8,128)(2,1)S(1)}, u32[]{:S(2)}, u32[]{:S(2)}) collective-permute-start(bf16[128,256]{1,0:T(8,128)(2,1)S(1)} %get-tuple-element.49), channel_id=1, source_target_pairs={{0,3},{1,0},{2,1},{3,2},{4,7},{5,4},{6,5},{7,6},{8,11},{9,8},{10,9... | collective-permute-start | bytes 196616 | tf_op jit(solution)/shard_map/ppermute | solution.py:193
  73.4 5.8 %collective-permute-start.34 = (bf16[128,256]{1,0:T(8,128)(2,1)S(1)}, bf16[128,256]{1,0:T(8,128)(2,1)S(1)}, u32[]{:S(2)}, u32[]{:S(2)}) collective-permute-start(bf16[128,256]{1,0:T(8,128)(2,1)S(1)} %get-tuple-element.50), channel_id=1, source_target_pairs={{0,2},{1,3},{2,0},{3,1},{4,6},{5,7},{6,4},{7,5},{8,10},{9,11},{10,... | collective-permute-start | bytes 196616 | tf_op jit(solution)/shard_map/ppermute | solution.py:193

commit v6 on v5

--- a/solution.py
+++ b/solution.py
@@ -218,6 +218,7 @@
         jax.ShapeDtypeStruct((tokens, 2 * rotated_keys.shape[1]), BF16),
         0,
         1 << 18,
+        vmem=PROJECT_VMEM,
         in_specs=[hbm] * 2,
         out_specs=vmem,
         scratch_shapes=[pltpu.SemaphoreType.DMA((2,))],

time: 100 us -> 100 us (level)
  no operation moved by 1% of the time
where the time goes in v6:
time: 100 us; the launch traced here: 99.3 us
  starting transfers between devices  36 us (36%)
  waiting for transfers between devices  21.2 us (21%)
  blocking collectives  18.4 us (18%)
  Pallas kernels  17.4 us (17%)
  local copies, waits for them, and re-layouts  4.44 us (4%)
  other arithmetic  1.69 us (2%)
    ppermute x17, starting transfers between devices, ring_shift(): lax.ppermute(value, axis, [(n, (n + steps) % count) for n in range(count)])  24.7 us
    all_to_all x1, blocking collectives, on_device(): received = lax.all_to_all(sent, ('z', 'y'), 0, 0, tiled=True)  18.4 us
    ppermute x17, waiting for transfers between devices, ring_shift(): lax.ppermute(value, axis, [(n, (n + steps) % count) for n in range(count)])  18 us
    ppermute x4, starting transfers between devices, chip_shift(): return lax.ppermute(value, ('z', 'y', 'core'), pairs)  8.27 us
    pallas_call x1, Pallas kernels, on_device(): call(sort_kernel, out_shapes + [jax.ShapeDtypeStruct((NX, features // NX,...  5.55 us
    pallas_call x1, Pallas kernels, on_device(): call(attend_kernel, jax.ShapeDtypeStruct((tokens, row_width), BF16), 4 *...  5 us
    pallas_call x1, Pallas kernels, on_device(): call(again_kernel, out_shapes, flops, 6 << 20, vmem=PROJECT_VMEM, in_spec...  4.09 us
    unnamed x26, local copies, waits for them, and re-layouts  3.45 us
  transfers between devices with their start and end apart: 35, of which 9 were waited for; matrix products, arithmetic and copies ran while one was open for 3% of the time, Pallas kernels for 16%

profile of v6, /device:TPU:8, one launch (start us, length us, event | category | flops | bytes accessed | tf_op | source)
XLA Modules:
  0.0 99.3 jit_solution(5468953568809391964)
XLA Ops:
  0.0 0.8 copy-done.2
  0.8 0.8 copy-done.3
  1.7 1.7 %collective-permute-start.4 = (bf16[128,512]{1,0:T(8,128)(2,1)S(1)}, bf16[128,512]{1,0:T(8,128)(2,1)S(1)}, u32[]{:S(2)}, u32[]{:S(2)}) collective-permute-start(bf16[128,512]{1,0:T(8,128)(2,1)S(1)} %shard_map.64.refs_0_), channel_id=1, source_target_pairs={{0,8},{4,12},{8,16},{12,20},{16,24},{20,28},{24,32},{28,36},{32,40... | collective-permute-start | bytes 393224 | tf_op jit(solution)/shard_map/ppermute | solution.py:188
  3.4 2.3 %collective-permute-start.9 = (bf16[128,512]{1,0:T(8,128)(2,1)S(1)}, bf16[128,512]{1,0:T(8,128)(2,1)S(1)}, u32[]{:S(2)}, u32[]{:S(2)}) collective-permute-start(bf16[128,512]{1,0:T(8,128)(2,1)S(1)} %shard_map.64.refs_0_), channel_id=1, source_target_pairs={{0,16},{4,20},{8,24},{12,28},{16,32},{20,36},{24,40},{28,44},{32,4... | collective-permute-start | bytes 393224 | tf_op jit(solution)/shard_map/ppermute | solution.py:188
  5.7 2.4 %collective-permute-start.10 = (bf16[128,512]{1,0:T(8,128)(2,1)S(1)}, bf16[128,512]{1,0:T(8,128)(2,1)S(1)}, u32[]{:S(2)}, u32[]{:S(2)}) collective-permute-start(bf16[128,512]{1,0:T(8,128)(2,1)S(1)} %shard_map.64.refs_0_), channel_id=1, source_target_pairs={{0,24},{4,28},{8,32},{12,36},{16,40},{20,44},{24,48},{28,52},{32,5... | collective-permute-start | bytes 393224 | tf_op jit(solution)/shard_map/ppermute | solution.py:188
  8.1 1.9 %collective-permute-start.11 = (bf16[128,512]{1,0:T(8,128)(2,1)S(1)}, bf16[128,512]{1,0:T(8,128)(2,1)S(1)}, u32[]{:S(2)}, u32[]{:S(2)}) collective-permute-start(bf16[128,512]{1,0:T(8,128)(2,1)S(1)} %shard_map.64.refs_0_), channel_id=1, source_target_pairs={{0,32},{4,36},{8,40},{12,44},{16,48},{20,52},{24,56},{28,60},{32,6... | collective-permute-start | bytes 393224 | tf_op jit(solution)/shard_map/ppermute | solution.py:188
  10.0 1.3 %collective-permute-start = (bf16[64,2048]{1,0:T(8,128)(2,1)}, bf16[64,2048]{1,0:T(8,128)(2,1)S(1)}, u32[]{:S(2)}, u32[]{:S(2)}) collective-permute-start(bf16[64,2048]{1,0:T(8,128)(2,1)} %refs_0_.1), channel_id=1, source_target_pairs={{0,224},{32,0},{64,32},{96,64},{128,96},{160,128},{192,160},{224,1... | collective-permute-start | bytes 786440 | tf_op jit(solution)/shard_map/ppermute | solution.py:193
  11.3 0.7 constant_dynamic-slice_fusion
  12.1 0.7 broadcast_select_fusion
  12.8 0.8 select_reduce_fusion
  13.5 0.8 collective-permute-start.5
  14.6 2.7 %collective-permute-done.9.refs_2_ = bf16[128,512]{1,0:T(8,128)(2,1)S(1)} collective-permute-done((bf16[128,512]{1,0:T(8,128)(2,1)S(1)}, bf16[128,512]{1,0:T(8,128)(2,1)S(1)}, u32[]{:S(2)}, u32[]{:S(2)}) %collective-permute-start.9) | collective-permute-done | bytes 131104 | tf_op jit(solution)/shard_map/ppermute | solution.py:188
  17.4 1.0 %copy-done = bf16[128,2048]{1,0:T(8,128)(2,1)S(1)} copy-done((bf16[128,2048]{1,0:T(8,128)(2,1)S(1)}, bf16[128,2048]{1,0:T(8,128)(2,1)}, u32[]{:S(2)}) %copy-start) | copy-done | bytes 524312
  18.4 1.0 shard_map.65
  19.4 0.6 collective-permute-start.13
  20.1 0.4 collective-permute-start.8
  20.5 1.4 %collective-permute-start.1 = (bf16[64,2048]{1,0:T(8,128)(2,1)S(1)}, bf16[64,2048]{1,0:T(8,128)(2,1)S(1)}, u32[]{:S(2)}, u32[]{:S(2)}) collective-permute-start(bf16[64,2048]{1,0:T(8,128)(2,1)S(1)} %collective-permute-done.refs_1_), channel_id=1, source_target_pairs={{0,224},{32,0},{64,32},{96,64},{128,96},{160,128},{192,160},{224,1... | collective-permute-start | bytes 786440 | tf_op jit(solution)/shard_map/ppermute | solution.py:193
  21.9 0.5 collective-permute-start.16
  22.5 0.6 collective-permute-start.6
  23.0 0.2 collective-permute-done.15.refs_8_
  23.5 5.0 %shard_map.66.refs_16_ = bf16[128,2048]{1,0:T(8,128)(2,1)S(1)} custom-call(f32[128,1280]{1,0:T(8,128)S(1)} %get-tuple-element.30.bias_ref, bf16[64,2048]{1,0:T(8,128)(2,1)S(1)} %get-tuple-element.31.keep_ref, bf16[64,2048]{1,0:T(8,128)(2,1)S(1)} %collective-permute-done.8.got_ref, bf16[128,512]{1,0:T(8,128)(2,1)S(1)} %shard_map.64.refs_0_, ...), custom_call_target="tpu_custom_call" | custom-call | flops 1342177280 | bytes 8388608 | tf_op jit(solution)/shard_map/pallas_call | solution.py:249
  28.5 0.4 collective-permute-start.17
  28.9 2.5 %collective-permute-start.2 = (bf16[64,2048]{1,0:T(8,128)(2,1)S(1)}, bf16[64,2048]{1,0:T(8,128)(2,1)S(1)}, u32[]{:S(2)}, u32[]{:S(2)}) collective-permute-start(bf16[64,2048]{1,0:T(8,128)(2,1)S(1)} %collective-permute-done.1.refs_2_), channel_id=1, source_target_pairs={{0,224},{32,0},{64,32},{96,64},{128,96},{160,128},{192,160},{224,1... | collective-permute-start | bytes 786440 | tf_op jit(solution)/shard_map/ppermute | solution.py:193
  31.5 0.9 collective-permute-start.25
  32.4 1.3 %collective-permute-start.26 = (bf16[128,2048]{1,0:T(8,128)(2,1)S(1)}, bf16[128,2048]{1,0:T(8,128)(2,1)S(1)}, u32[]{:S(2)}, u32[]{:S(2)}) collective-permute-start(bf16[128,2048]{1,0:T(8,128)(2,1)S(1)} %shard_map.66.refs_16_), channel_id=1, source_target_pairs={{0,8},{8,16},{16,24},{24,0},{1,9},{9,17},{17,25},{25,1},{2,10},{10... | collective-permute-start | bytes 1572872 | tf_op jit(solution)/shard_map/ppermute | solution.py:193
  33.7 0.7 copy-done.10
  34.4 2.9 %collective-permute-done.2.refs_3_ = bf16[64,2048]{1,0:T(8,128)(2,1)S(1)} collective-permute-done((bf16[64,2048]{1,0:T(8,128)(2,1)S(1)}, bf16[64,2048]{1,0:T(8,128)(2,1)S(1)}, u32[]{:S(2)}, u32[]{:S(2)}) %collective-permute-start.2) | collective-permute-done | bytes 262176 | tf_op jit(solution)/shard_map/ppermute | solution.py:193
  37.3 3.4 %collective-permute-start.3 = (bf16[64,2048]{1,0:T(8,128)(2,1)S(1)}, bf16[64,2048]{1,0:T(8,128)(2,1)S(1)}, u32[]{:S(2)}, u32[]{:S(2)}) collective-permute-start(bf16[64,2048]{1,0:T(8,128)(2,1)S(1)} %collective-permute-done.2.refs_3_), channel_id=1, source_target_pairs={{0,224},{32,0},{64,32},{96,64},{128,96},{160,128},{192,160},{224,1... | collective-permute-start | bytes 786440 | tf_op jit(solution)/shard_map/ppermute | solution.py:193
  40.8 2.5 %collective-permute-done.7.refs_7_ = bf16[64,2048]{1,0:T(8,128)(2,1)} collective-permute-done((bf16[64,2048]{1,0:T(8,128)(2,1)S(1)}, bf16[64,2048]{1,0:T(8,128)(2,1)}, u32[]{:S(2)}, u32[]{:S(2)}) %collective-permute-start.7) | collective-permute-done | bytes 262176 | tf_op jit(solution)/shard_map/ppermute | solution.py:193
  43.3 2.2 %collective-permute-done.3.refs_4_ = bf16[64,2048]{1,0:T(8,128)(2,1)S(1)} collective-permute-done((bf16[64,2048]{1,0:T(8,128)(2,1)S(1)}, bf16[64,2048]{1,0:T(8,128)(2,1)S(1)}, u32[]{:S(2)}, u32[]{:S(2)}) %collective-permute-start.3) | collective-permute-done | bytes 262176 | tf_op jit(solution)/shard_map/ppermute | solution.py:193
  45.5 0.5 collective-permute-start.20
  46.0 0.3 collective-permute-start.24
  46.3 3.1 %collective-permute-done.26.refs_18_ = bf16[128,2048]{1,0:T(8,128)(2,1)S(1)} collective-permute-done((bf16[128,2048]{1,0:T(8,128)(2,1)S(1)}, bf16[128,2048]{1,0:T(8,128)(2,1)S(1)}, u32[]{:S(2)}, u32[]{:S(2)}) %collective-permute-start.26) | collective-permute-done | bytes 524320 | tf_op jit(solution)/shard_map/ppermute | solution.py:193
  49.6 0.4 collective-permute-start.30
  50.0 2.7 %collective-permute-start.31 = (bf16[64,2048]{1,0:T(8,128)(2,1)S(1)}, bf16[64,2048]{1,0:T(8,128)(2,1)S(1)}, u32[]{:S(2)}, u32[]{:S(2)}) collective-permute-start(bf16[64,2048]{1,0:T(8,128)(2,1)S(1)} %slice.9), channel_id=1, source_target_pairs={{0,24},{8,0},{16,8},{24,16},{1,25},{9,1},{17,9},{25,17},{2,26},{10... | collective-permute-start | bytes 786440 | tf_op jit(solution)/shard_map/ppermute | solution.py:193
  52.9 5.6 %shard_map.67 = (f32[384,256]{1,0:T(8,128)}, bf16[384,256]{1,0:T(8,128)(2,1)S(1)}, bf16[384,256]{1,0:T(8,128)(2,1)S(1)}, bf16[384,256]{1,0:T(8,128)(2,1)S(1)}, bf16[4,256,2048]{2,1,0:T(8,128)(2,1)}) custom-call(s32[3]{0:T(128)S(1)} %pad_add_fusion.1.place_ref, bf16[64,2048]{1,0:T(8,128)(2,1)S(1)} %copy-done.5, ...), custom_call_target="tpu_custom_call" | custom-call | flops 1610612736 | bytes 8388608 | tf_op jit(solution)/shard_map/pallas_call | solution.py:280
  58.5 1.6 %collective-permute-start.27 = (bf16[384,256]{1,0:T(8,128)(2,1)S(1)}, bf16[384,256]{1,0:T(8,128)(2,1)S(1)}, u32[]{:S(2)}, u32[]{:S(2)}) collective-permute-start(bf16[384,256]{1,0:T(8,128)(2,1)S(1)} %get-tuple-element.43), channel_id=1, source_target_pairs={{0,1},{1,2},{2,3},{3,0},{4,5},{5,6},{6,7},{7,4},{8,9},{9,10},{10,1... | collective-permute-start | bytes 589832 | tf_op jit(solution)/shard_map/ppermute | solution.py:193
  60.0 1.8 %collective-permute-start.28 = (bf16[384,256]{1,0:T(8,128)(2,1)S(1)}, bf16[384,256]{1,0:T(8,128)(2,1)S(1)}, u32[]{:S(2)}, u32[]{:S(2)}) collective-permute-start(bf16[384,256]{1,0:T(8,128)(2,1)S(1)} %get-tuple-element.44), channel_id=1, source_target_pairs={{0,3},{1,0},{2,1},{3,2},{4,7},{5,4},{6,5},{7,6},{8,11},{9,8},{10,9... | collective-permute-start | bytes 589832 | tf_op jit(solution)/shard_map/ppermute | solution.py:193
  61.8 1.8 %collective-permute-start.29 = (bf16[384,256]{1,0:T(8,128)(2,1)S(1)}, bf16[384,256]{1,0:T(8,128)(2,1)S(1)}, u32[]{:S(2)}, u32[]{:S(2)}) collective-permute-start(bf16[384,256]{1,0:T(8,128)(2,1)S(1)} %get-tuple-element.45), channel_id=1, source_target_pairs={{0,2},{1,3},{2,0},{3,1},{4,6},{5,7},{6,4},{7,5},{8,10},{9,11},{10,... | collective-permute-start | bytes 589832 | tf_op jit(solution)/shard_map/ppermute | solution.py:193
  63.6 4.1 %shard_map.68 = (f32[128,256]{1,0:T(8,128)S(1)}, bf16[128,256]{1,0:T(8,128)(2,1)S(1)}, bf16[128,256]{1,0:T(8,128)(2,1)S(1)}, bf16[128,256]{1,0:T(8,128)(2,1)S(1)}) custom-call(bf16[4,256,2048]{2,1,0:T(8,128)(2,1)} %get-tuple-element.46.sorted_ref, bf16[64,2048]{1,0:T(8,128)(2,1)S(1)} %collective-permute-done.30.refs_0_, ...), custom_call_target="tpu_custom_call" | custom-call | flops 536870912 | bytes 6291456 | tf_op jit(solution)/shard_map/pallas_call | solution.py:291
  67.7 0.7 collective-permute-start.32
  68.4 2.7 %collective-permute-start.33 = (bf16[128,256]{1,0:T(8,128)(2,1)S(1)}, bf16[128,256]{1,0:T(8,128)(2,1)S(1)}, u32[]{:S(2)}, u32[]{:S(2)}) collective-permute-start(bf16[128,256]{1,0:T(8,128)(2,1)S(1)} %get-tuple-element.49), channel_id=1, source_target_pairs={{0,3},{1,0},{2,1},{3,2},{4,7},{5,4},{6,5},{7,6},{8,11},{9,8},{10,9... | collective-permute-start | bytes 196616 | tf_op jit(solution)/shard_map/ppermute | solution.py:193
  71.0 2.3 %collective-permute-done.32.refs_5_ = bf16[128,256]{1,0:T(8,128)(2,1)S(1)} collective-permute-done((bf16[128,256]{1,0:T(8,128)(2,1)S(1)}, bf16[128,256]{1,0:T(8,128)(2,1)S(1)}, u32[]{:S(2)}, u32[]{:S(2)}) %collective-permute-start.32) | collective-permute-done | bytes 65568 | tf_op jit(solution)/shard_map/ppermute | solution.py:193
  73.4 0.8 collective-permute-start.34
  74.3 4.9 %collective-permute-done.34.refs_7_ = bf16[128,256]{1,0:T(8,128)(2,1)S(1)} collective-permute-done((bf16[128,256]{1,0:T(8,128)(2,1)S(1)}, bf16[128,256]{1,0:T(8,128)(2,1)S(1)}, u32[]{:S(2)}, u32[]{:S(2)}) %collective-permute-start.34) | collective-permute-done | bytes 65568 | tf_op jit(solution)/shard_map/ppermute | solution.py:193
  79.2 1.0 %shard_map.69 = bf16[32,16,256]{2,1,0:T(8,128)(2,1)S(1)} custom-call(s32[2]{0:T(128)S(1)} %pad_add_fusion.place_ref, f32[384,256]{1,0:T(8,128)S(1)} %copy-done.1, bf16[384,256]{1,0:T(8,128)(2,1)S(1)} %collective-permute-done.27.refs_1_, bf16[384,256]{1,0:T(8,128)(2,1)S(1)} %collective-permute-done.28.refs_2_, ...), custom_call_target="tpu_custom_call" | custom-call | flops 4194304 | bytes 2097152 | tf_op jit(solution)/shard_map/pallas_call | solution.py:306
  80.2 18.4 %all_to_all.5.x_ref = bf16[32,16,256]{2,1,0:T(8,128)(2,1)S(1)} all-to-all(bf16[32,16,256]{2,1,0:T(8,128)(2,1)S(1)} %shard_map.69), channel_id=1, replica_groups=mesh['z'=8,'y'=4,'core'=2,'tp'=4] {'z','y'}, dimensions={0} | all-to-all | bytes 524288 | tf_op jit(solution)/shard_map/all_to_all | solution.py:315
  98.6 0.7 shard_map.70
  (68 shorter events, 1.1 us)
Async XLA Ops:
  0.0 0.8 copy-start.2
  0.8 0.8 copy-start.3
  1.7 26.8 %copy-start.5 = (bf16[64,2048]{1,0:T(8,128)(2,1)S(1)}, bf16[64,2048]{1,0:T(8,128)(2,1)}, u32[]{:S(2)}) copy-start(bf16[64,2048]{1,0:T(8,128)(2,1)} %refs_0_.1) | copy-start | bytes 786436
  1.7 11.8 %collective-permute-start.4 = (bf16[128,512]{1,0:T(8,128)(2,1)S(1)}, bf16[128,512]{1,0:T(8,128)(2,1)S(1)}, u32[]{:S(2)}, u32[]{:S(2)}) collective-permute-start(bf16[128,512]{1,0:T(8,128)(2,1)S(1)} %shard_map.64.refs_0_), channel_id=1, source_target_pairs={{0,8},{4,12},{8,16},{12,20},{16,24},{20,28},{24,32},{28,36},{32,40... | collective-permute-start | bytes 393224 | tf_op jit(solution)/shard_map/ppermute | solution.py:188
  3.4 14.0 %collective-permute-start.9 = (bf16[128,512]{1,0:T(8,128)(2,1)S(1)}, bf16[128,512]{1,0:T(8,128)(2,1)S(1)}, u32[]{:S(2)}, u32[]{:S(2)}) collective-permute-start(bf16[128,512]{1,0:T(8,128)(2,1)S(1)} %shard_map.64.refs_0_), channel_id=1, source_target_pairs={{0,16},{4,20},{8,24},{12,28},{16,32},{20,36},{24,40},{28,44},{32,4... | collective-permute-start | bytes 393224 | tf_op jit(solution)/shard_map/ppermute | solution.py:188
  5.7 13.7 %collective-permute-start.10 = (bf16[128,512]{1,0:T(8,128)(2,1)S(1)}, bf16[128,512]{1,0:T(8,128)(2,1)S(1)}, u32[]{:S(2)}, u32[]{:S(2)}) collective-permute-start(bf16[128,512]{1,0:T(8,128)(2,1)S(1)} %shard_map.64.refs_0_), channel_id=1, source_target_pairs={{0,24},{4,28},{8,32},{12,36},{16,40},{20,44},{24,48},{28,52},{32,5... | collective-permute-start | bytes 393224 | tf_op jit(solution)/shard_map/ppermute | solution.py:188
  8.1 11.9 %collective-permute-start.11 = (bf16[128,512]{1,0:T(8,128)(2,1)S(1)}, bf16[128,512]{1,0:T(8,128)(2,1)S(1)}, u32[]{:S(2)}, u32[]{:S(2)}) collective-permute-start(bf16[128,512]{1,0:T(8,128)(2,1)S(1)} %shard_map.64.refs_0_), channel_id=1, source_target_pairs={{0,32},{4,36},{8,40},{12,44},{16,48},{20,52},{24,56},{28,60},{32,6... | collective-permute-start | bytes 393224 | tf_op jit(solution)/shard_map/ppermute | solution.py:188
  10.0 10.1 %collective-permute-start = (bf16[64,2048]{1,0:T(8,128)(2,1)}, bf16[64,2048]{1,0:T(8,128)(2,1)S(1)}, u32[]{:S(2)}, u32[]{:S(2)}) collective-permute-start(bf16[64,2048]{1,0:T(8,128)(2,1)} %refs_0_.1), channel_id=1, source_target_pairs={{0,224},{32,0},{64,32},{96,64},{128,96},{160,128},{192,160},{224,1... | collective-permute-start | bytes 786440 | tf_op jit(solution)/shard_map/ppermute | solution.py:193
  13.5 8.9 %collective-permute-start.5 = (bf16[64,2048]{1,0:T(8,128)(2,1)}, bf16[64,2048]{1,0:T(8,128)(2,1)S(1)}, u32[]{:S(2)}, u32[]{:S(2)}) collective-permute-start(bf16[64,2048]{1,0:T(8,128)(2,1)} %refs_0_.1), channel_id=1, source_target_pairs={{0,32},{32,64},{64,96},{96,128},{128,160},{160,192},{192,224},{224... | collective-permute-start | bytes 786440 | tf_op jit(solution)/shard_map/ppermute | solution.py:193
  17.4 3.1 %collective-permute-start.12 = (bf16[128,512]{1,0:T(8,128)(2,1)S(1)}, bf16[128,512]{1,0:T(8,128)(2,1)S(1)}, u32[]{:S(2)}, u32[]{:S(2)}) collective-permute-start(bf16[128,512]{1,0:T(8,128)(2,1)S(1)} %shard_map.64.refs_0_), channel_id=1, source_target_pairs={{0,4},{4,0},{1,5},{5,1},{2,6},{6,2},{3,7},{7,3},{8,12},{12,8},{9,1... | collective-permute-start | bytes 393224 | tf_op jit(solution)/shard_map/ppermute | solution.py:197
  17.4 1.0 %copy-start = (bf16[128,2048]{1,0:T(8,128)(2,1)S(1)}, bf16[128,2048]{1,0:T(8,128)(2,1)}, u32[]{:S(2)}) copy-start(bf16[128,2048]{1,0:T(8,128)(2,1)} %q_ref) | copy-start | bytes 1572868
  19.4 2.5 %collective-permute-start.13 = (bf16[128,512]{1,0:T(8,128)(2,1)S(1)}, bf16[128,512]{1,0:T(8,128)(2,1)S(1)}, u32[]{:S(2)}, u32[]{:S(2)}) collective-permute-start(bf16[128,512]{1,0:T(8,128)(2,1)S(1)} %collective-permute-done.4.refs_1_), channel_id=1, source_target_pairs={{0,4},{4,0},{1,5},{5,1},{2,6},{6,2},{3,7},{7,3},{8,12},{12,8},{9,1... | collective-permute-start | bytes 393224 | tf_op jit(solution)/shard_map/ppermute | solution.py:197
  20.0 2.0 %collective-permute-start.14 = (bf16[128,512]{1,0:T(8,128)(2,1)S(1)}, bf16[128,512]{1,0:T(8,128)(2,1)S(1)}, u32[]{:S(2)}, u32[]{:S(2)}) collective-permute-start(bf16[128,512]{1,0:T(8,128)(2,1)S(1)} %collective-permute-done.9.refs_2_), channel_id=1, source_target_pairs={{0,4},{4,0},{1,5},{5,1},{2,6},{6,2},{3,7},{7,3},{8,12},{12,8},{9,1... | collective-permute-start | bytes 393224 | tf_op jit(solution)/shard_map/ppermute | solution.py:197
  20.1 3.4 %collective-permute-start.8 = (bf16[64,2048]{1,0:T(8,128)(2,1)S(1)}, bf16[64,2048]{1,0:T(8,128)(2,1)S(1)}, u32[]{:S(2)}, u32[]{:S(2)}) collective-permute-start(bf16[64,2048]{1,0:T(8,128)(2,1)S(1)} %get-tuple-element.32), channel_id=1, source_target_pairs={{0,4},{4,0},{1,5},{5,1},{2,6},{6,2},{3,7},{7,3},{8,12},{12,8},{9,1... | collective-permute-start | bytes 786440 | tf_op jit(solution)/shard_map/ppermute | solution.py:197
  20.5 8.4 %collective-permute-start.1 = (bf16[64,2048]{1,0:T(8,128)(2,1)S(1)}, bf16[64,2048]{1,0:T(8,128)(2,1)S(1)}, u32[]{:S(2)}, u32[]{:S(2)}) collective-permute-start(bf16[64,2048]{1,0:T(8,128)(2,1)S(1)} %collective-permute-done.refs_1_), channel_id=1, source_target_pairs={{0,224},{32,0},{64,32},{96,64},{128,96},{160,128},{192,160},{224,1... | collective-permute-start | bytes 786440 | tf_op jit(solution)/shard_map/ppermute | solution.py:193
  21.9 1.3 %collective-permute-start.15 = (bf16[128,512]{1,0:T(8,128)(2,1)S(1)}, bf16[128,512]{1,0:T(8,128)(2,1)S(1)}, u32[]{:S(2)}, u32[]{:S(2)}) collective-permute-start(bf16[128,512]{1,0:T(8,128)(2,1)S(1)} %collective-permute-done.10.refs_3_), channel_id=1, source_target_pairs={{0,4},{4,0},{1,5},{5,1},{2,6},{6,2},{3,7},{7,3},{8,12},{12,8},{9,1... | collective-permute-start | bytes 393224 | tf_op jit(solution)/shard_map/ppermute | solution.py:197
  21.9 1.5 %collective-permute-start.16 = (bf16[128,512]{1,0:T(8,128)(2,1)S(1)}, bf16[128,512]{1,0:T(8,128)(2,1)S(1)}, u32[]{:S(2)}, u32[]{:S(2)}) collective-permute-start(bf16[128,512]{1,0:T(8,128)(2,1)S(1)} %collective-permute-done.11.refs_4_), channel_id=1, source_target_pairs={{0,4},{4,0},{1,5},{5,1},{2,6},{6,2},{3,7},{7,3},{8,12},{12,8},{9,1... | collective-permute-start | bytes 393224 | tf_op jit(solution)/shard_map/ppermute | solution.py:197
  22.4 30.4 %copy-start.8 = (bf16[64,2048]{1,0:T(8,128)(2,1)}, bf16[64,2048]{1,0:T(8,128)(2,1)S(1)}, u32[]{:S(2)}) copy-start(bf16[64,2048]{1,0:T(8,128)(2,1)S(1)} %collective-permute-done.5.refs_5_) | copy-start | bytes 786436
  22.5 9.9 %collective-permute-start.6 = (bf16[64,2048]{1,0:T(8,128)(2,1)S(1)}, bf16[64,2048]{1,0:T(8,128)(2,1)S(1)}, u32[]{:S(2)}, u32[]{:S(2)}) collective-permute-start(bf16[64,2048]{1,0:T(8,128)(2,1)S(1)} %collective-permute-done.5.refs_5_), channel_id=1, source_target_pairs={{0,32},{32,64},{64,96},{96,128},{128,160},{160,192},{192,224},{224... | collective-permute-start | bytes 786440 | tf_op jit(solution)/shard_map/ppermute | solution.py:193
  28.5 24.4 %copy-start.4 = (bf16[128,2048]{1,0:T(8,128)(2,1)}, bf16[128,2048]{1,0:T(8,128)(2,1)S(1)}, u32[]{:S(2)}) copy-start(bf16[128,2048]{1,0:T(8,128)(2,1)S(1)} %shard_map.66.refs_16_) | copy-start | bytes 1572868
  28.5 5.2 %collective-permute-start.17 = (bf16[64,2048]{1,0:T(8,128)(2,1)S(1)}, bf16[64,2048]{1,0:T(8,128)(2,1)S(1)}, u32[]{:S(2)}, u32[]{:S(2)}) collective-permute-start(bf16[64,2048]{1,0:T(8,128)(2,1)S(1)} %copy-done.5), channel_id=1, source_target_pairs={{0,4},{4,0},{1,5},{5,1},{2,6},{6,2},{3,7},{7,3},{8,12},{12,8},{9,1... | collective-permute-start | bytes 786440 | tf_op jit(solution)/shard_map/ppermute | solution.py:197
  28.9 8.4 %collective-permute-start.2 = (bf16[64,2048]{1,0:T(8,128)(2,1)S(1)}, bf16[64,2048]{1,0:T(8,128)(2,1)S(1)}, u32[]{:S(2)}, u32[]{:S(2)}) collective-permute-start(bf16[64,2048]{1,0:T(8,128)(2,1)S(1)} %collective-permute-done.1.refs_2_), channel_id=1, source_target_pairs={{0,224},{32,0},{64,32},{96,64},{128,96},{160,128},{192,160},{224,1... | collective-permute-start | bytes 786440 | tf_op jit(solution)/shard_map/ppermute | solution.py:193
  31.5 9.3 %collective-permute-start.18 = (bf16[64,2048]{1,0:T(8,128)(2,1)S(1)}, bf16[64,2048]{1,0:T(8,128)(2,1)S(1)}, u32[]{:S(2)}, u32[]{:S(2)}) collective-permute-start(bf16[64,2048]{1,0:T(8,128)(2,1)S(1)} %collective-permute-done.refs_1_), channel_id=1, source_target_pairs={{0,4},{4,0},{1,5},{5,1},{2,6},{6,2},{3,7},{7,3},{8,12},{12,8},{9,1... | collective-permute-start | bytes 786440 | tf_op jit(solution)/shard_map/ppermute | solution.py:197
  31.5 14.6 %collective-permute-start.25 = (bf16[128,2048]{1,0:T(8,128)(2,1)S(1)}, bf16[128,2048]{1,0:T(8,128)(2,1)S(1)}, u32[]{:S(2)}, u32[]{:S(2)}) collective-permute-start(bf16[128,2048]{1,0:T(8,128)(2,1)S(1)} %shard_map.66.refs_16_), channel_id=1, source_target_pairs={{0,24},{8,0},{16,8},{24,16},{1,25},{9,1},{17,9},{25,17},{2,26},{10... | collective-permute-start | bytes 1572872 | tf_op jit(solution)/shard_map/ppermute | solution.py:193
  32.4 20.5 %copy-start.9 = (bf16[64,2048]{1,0:T(8,128)(2,1)}, bf16[64,2048]{1,0:T(8,128)(2,1)S(1)}, u32[]{:S(2)}) copy-start(bf16[64,2048]{1,0:T(8,128)(2,1)S(1)} %collective-permute-done.6.refs_6_) | copy-start | bytes 786436
  32.4 17.1 %collective-permute-start.26 = (bf16[128,2048]{1,0:T(8,128)(2,1)S(1)}, bf16[128,2048]{1,0:T(8,128)(2,1)S(1)}, u32[]{:S(2)}, u32[]{:S(2)}) collective-permute-start(bf16[128,2048]{1,0:T(8,128)(2,1)S(1)} %shard_map.66.refs_16_), channel_id=1, source_target_pairs={{0,8},{8,16},{16,24},{24,0},{1,9},{9,17},{17,25},{25,1},{2,10},{10... | collective-permute-start | bytes 1572872 | tf_op jit(solution)/shard_map/ppermute | solution.py:193
  33.7 0.7 copy-start.10
  33.7 9.6 %collective-permute-start.7 = (bf16[64,2048]{1,0:T(8,128)(2,1)S(1)}, bf16[64,2048]{1,0:T(8,128)(2,1)}, u32[]{:S(2)}, u32[]{:S(2)}) collective-permute-start(bf16[64,2048]{1,0:T(8,128)(2,1)S(1)} %collective-permute-done.6.refs_6_), channel_id=1, source_target_pairs={{0,32},{32,64},{64,96},{96,128},{128,160},{160,192},{192,224},{224... | collective-permute-start | bytes 786440 | tf_op jit(solution)/shard_map/ppermute | solution.py:193
  37.3 8.2 %collective-permute-start.3 = (bf16[64,2048]{1,0:T(8,128)(2,1)S(1)}, bf16[64,2048]{1,0:T(8,128)(2,1)S(1)}, u32[]{:S(2)}, u32[]{:S(2)}) collective-permute-start(bf16[64,2048]{1,0:T(8,128)(2,1)S(1)} %collective-permute-done.2.refs_3_), channel_id=1, source_target_pairs={{0,224},{32,0},{64,32},{96,64},{128,96},{160,128},{192,160},{224,1... | collective-permute-start | bytes 786440 | tf_op jit(solution)/shard_map/ppermute | solution.py:193
  40.8 8.7 %copy-start.11 = (bf16[64,2048]{1,0:T(8,128)(2,1)}, bf16[64,2048]{1,0:T(8,128)(2,1)S(1)}, u32[]{:S(2)}) copy-start(bf16[64,2048]{1,0:T(8,128)(2,1)S(1)} %collective-permute-done.18.refs_9_) | copy-start | bytes 786436
  40.8 4.7 %collective-permute-start.22 = (bf16[64,2048]{1,0:T(8,128)(2,1)S(1)}, bf16[64,2048]{1,0:T(8,128)(2,1)S(1)}, u32[]{:S(2)}, u32[]{:S(2)}) collective-permute-start(bf16[64,2048]{1,0:T(8,128)(2,1)S(1)} %collective-permute-done.5.refs_5_), channel_id=1, source_target_pairs={{0,4},{4,0},{1,5},{5,1},{2,6},{6,2},{3,7},{7,3},{8,12},{12,8},{9,1... | collective-permute-start | bytes 786440 | tf_op jit(solution)/shard_map/ppermute | solution.py:197
  43.3 6.3 %collective-permute-start.19 = (bf16[64,2048]{1,0:T(8,128)(2,1)S(1)}, bf16[64,2048]{1,0:T(8,128)(2,1)}, u32[]{:S(2)}, u32[]{:S(2)}) collective-permute-start(bf16[64,2048]{1,0:T(8,128)(2,1)S(1)} %collective-permute-done.1.refs_2_), channel_id=1, source_target_pairs={{0,4},{4,0},{1,5},{5,1},{2,6},{6,2},{3,7},{7,3},{8,12},{12,8},{9,1... | collective-permute-start | bytes 786440 | tf_op jit(solution)/shard_map/ppermute | solution.py:197
  45.5 4.5 %collective-permute-start.23 = (bf16[64,2048]{1,0:T(8,128)(2,1)S(1)}, bf16[64,2048]{1,0:T(8,128)(2,1)}, u32[]{:S(2)}, u32[]{:S(2)}) collective-permute-start(bf16[64,2048]{1,0:T(8,128)(2,1)S(1)} %collective-permute-done.6.refs_6_), channel_id=1, source_target_pairs={{0,4},{4,0},{1,5},{5,1},{2,6},{6,2},{3,7},{7,3},{8,12},{12,8},{9,1... | collective-permute-start | bytes 786440 | tf_op jit(solution)/shard_map/ppermute | solution.py:197
  45.5 4.0 %copy-start.12 = (bf16[64,2048]{1,0:T(8,128)(2,1)}, bf16[64,2048]{1,0:T(8,128)(2,1)S(1)}, u32[]{:S(2)}) copy-start(bf16[64,2048]{1,0:T(8,128)(2,1)S(1)} %collective-permute-done.22.refs_13_) | copy-start | bytes 786436
  45.5 7.3 %collective-permute-start.20 = (bf16[64,2048]{1,0:T(8,128)(2,1)S(1)}, bf16[64,2048]{1,0:T(8,128)(2,1)}, u32[]{:S(2)}, u32[]{:S(2)}) collective-permute-start(bf16[64,2048]{1,0:T(8,128)(2,1)S(1)} %collective-permute-done.2.refs_3_), channel_id=1, source_target_pairs={{0,4},{4,0},{1,5},{5,1},{2,6},{6,2},{3,7},{7,3},{8,12},{12,8},{9,1... | collective-permute-start | bytes 786440 | tf_op jit(solution)/shard_map/ppermute | solution.py:197
  46.0 6.9 %copy-start.6 = (bf16[128,2048]{1,0:T(8,128)(2,1)}, bf16[128,2048]{1,0:T(8,128)(2,1)S(1)}, u32[]{:S(2)}) copy-start(bf16[128,2048]{1,0:T(8,128)(2,1)S(1)} %collective-permute-done.25.refs_17_) | copy-start | bytes 1572868
  46.0 6.8 %collective-permute-start.24 = (bf16[64,2048]{1,0:T(8,128)(2,1)}, bf16[64,2048]{1,0:T(8,128)(2,1)}, u32[]{:S(2)}, u32[]{:S(2)}) collective-permute-start(bf16[64,2048]{1,0:T(8,128)(2,1)} %collective-permute-done.7.refs_7_), channel_id=1, source_target_pairs={{0,4},{4,0},{1,5},{5,1},{2,6},{6,2},{3,7},{7,3},{8,12},{12,8},{9,1... | collective-permute-start | bytes 786440 | tf_op jit(solution)/shard_map/ppermute | solution.py:197
  49.5 3.4 %copy-start.7 = (bf16[128,2048]{1,0:T(8,128)(2,1)}, bf16[128,2048]{1,0:T(8,128)(2,1)S(1)}, u32[]{:S(2)}) copy-start(bf16[128,2048]{1,0:T(8,128)(2,1)S(1)} %collective-permute-done.26.refs_18_) | copy-start | bytes 1572868
  49.5 3.4 %collective-permute-start.21 = (bf16[64,2048]{1,0:T(8,128)(2,1)S(1)}, bf16[64,2048]{1,0:T(8,128)(2,1)}, u32[]{:S(2)}, u32[]{:S(2)}) collective-permute-start(bf16[64,2048]{1,0:T(8,128)(2,1)S(1)} %collective-permute-done.3.refs_4_), channel_id=1, source_target_pairs={{0,4},{4,0},{1,5},{5,1},{2,6},{6,2},{3,7},{7,3},{8,12},{12,8},{9,1... | collective-permute-start | bytes 786440 | tf_op jit(solution)/shard_map/ppermute | solution.py:197
  49.6 14.0 %collective-permute-start.30 = (bf16[64,2048]{1,0:T(8,128)(2,1)S(1)}, bf16[64,2048]{1,0:T(8,128)(2,1)S(1)}, u32[]{:S(2)}, u32[]{:S(2)}) collective-permute-start(bf16[64,2048]{1,0:T(8,128)(2,1)S(1)} %slice.8), channel_id=1, source_target_pairs={{0,8},{8,16},{16,24},{24,0},{1,9},{9,17},{17,25},{25,1},{2,10},{10... | collective-permute-start | bytes 786440 | tf_op jit(solution)/shard_map/ppermute | solution.py:193
  50.0 13.6 %collective-permute-start.31 = (bf16[64,2048]{1,0:T(8,128)(2,1)S(1)}, bf16[64,2048]{1,0:T(8,128)(2,1)S(1)}, u32[]{:S(2)}, u32[]{:S(2)}) collective-permute-start(bf16[64,2048]{1,0:T(8,128)(2,1)S(1)} %slice.9), channel_id=1, source_target_pairs={{0,24},{8,0},{16,8},{24,16},{1,25},{9,1},{17,9},{25,17},{2,26},{10... | collective-permute-start | bytes 786440 | tf_op jit(solution)/shard_map/ppermute | solution.py:193
  58.5 20.7 %copy-start.1 = (f32[384,256]{1,0:T(8,128)S(1)}, f32[384,256]{1,0:T(8,128)}, u32[]{:S(2)}) copy-start(f32[384,256]{1,0:T(8,128)} %get-tuple-element.42.refs_0_) | copy-start | bytes 1179652
  58.5 20.7 %collective-permute-start.27 = (bf16[384,256]{1,0:T(8,128)(2,1)S(1)}, bf16[384,256]{1,0:T(8,128)(2,1)S(1)}, u32[]{:S(2)}, u32[]{:S(2)}) collective-permute-start(bf16[384,256]{1,0:T(8,128)(2,1)S(1)} %get-tuple-element.43), channel_id=1, source_target_pairs={{0,1},{1,2},{2,3},{3,0},{4,5},{5,6},{6,7},{7,4},{8,9},{9,10},{10,1... | collective-permute-start | bytes 589832 | tf_op jit(solution)/shard_map/ppermute | solution.py:193
  60.0 19.1 %collective-permute-start.28 = (bf16[384,256]{1,0:T(8,128)(2,1)S(1)}, bf16[384,256]{1,0:T(8,128)(2,1)S(1)}, u32[]{:S(2)}, u32[]{:S(2)}) collective-permute-start(bf16[384,256]{1,0:T(8,128)(2,1)S(1)} %get-tuple-element.44), channel_id=1, source_target_pairs={{0,3},{1,0},{2,1},{3,2},{4,7},{5,4},{6,5},{7,6},{8,11},{9,8},{10,9... | collective-permute-start | bytes 589832 | tf_op jit(solution)/shard_map/ppermute | solution.py:193
  61.8 17.4 %collective-permute-start.29 = (bf16[384,256]{1,0:T(8,128)(2,1)S(1)}, bf16[384,256]{1,0:T(8,128)(2,1)S(1)}, u32[]{:S(2)}, u32[]{:S(2)}) collective-permute-start(bf16[384,256]{1,0:T(8,128)(2,1)S(1)} %get-tuple-element.45), channel_id=1, source_target_pairs={{0,2},{1,3},{2,0},{3,1},{4,6},{5,7},{6,4},{7,5},{8,10},{9,11},{10,... | collective-permute-start | bytes 589832 | tf_op jit(solution)/shard_map/ppermute | solution.py:193
  67.7 5.7 %collective-permute-start.32 = (bf16[128,256]{1,0:T(8,128)(2,1)S(1)}, bf16[128,256]{1,0:T(8,128)(2,1)S(1)}, u32[]{:S(2)}, u32[]{:S(2)}) collective-permute-start(bf16[128,256]{1,0:T(8,128)(2,1)S(1)} %get-tuple-element.48), channel_id=1, source_target_pairs={{0,1},{1,2},{2,3},{3,0},{4,5},{5,6},{6,7},{7,4},{8,9},{9,10},{10,1... | collective-permute-start | bytes 196616 | tf_op jit(solution)/shard_map/ppermute | solution.py:193
  68.4 5.9 %collective-permute-start.33 = (bf16[128,256]{1,0:T(8,128)(2,1)S(1)}, bf16[128,256]{1,0:T(8,128)(2,1)S(1)}, u32[]{:S(2)}, u32[]{:S(2)}) collective-permute-start(bf16[128,256]{1,0:T(8,128)(2,1)S(1)} %get-tuple-element.49), channel_id=1, source_target_pairs={{0,3},{1,0},{2,1},{3,2},{4,7},{5,4},{6,5},{7,6},{8,11},{9,8},{10,9... | collective-permute-start | bytes 196616 | tf_op jit(solution)/shard_map/ppermute | solution.py:193
  73.4 5.8 %collective-permute-start.34 = (bf16[128,256]{1,0:T(8,128)(2,1)S(1)}, bf16[128,256]{1,0:T(8,128)(2,1)S(1)}, u32[]{:S(2)}, u32[]{:S(2)}) collective-permute-start(bf16[128,256]{1,0:T(8,128)(2,1)S(1)} %get-tuple-element.50), channel_id=1, source_target_pairs={{0,2},{1,3},{2,0},{3,1},{4,6},{5,7},{6,4},{7,5},{8,10},{9,11},{10,... | collective-permute-start | bytes 196616 | tf_op jit(solution)/shard_map/ppermute | solution.py:193
